TPU v7x, 256 devices: a whole 4x4x8 slice. The times are simulated.
256 devices in a mesh: dp: 8 (over z_lo, core), seq: 32 (over z_hi, x, y).
Axes of the slice: x: 4, y: 4, z: 8 (z_hi: 2, z_lo: 4; z = z_hi * 4 + z_lo), core: 2. Of those that a mesh axis runs over, the one named last changes fastest.
Arguments:
- mapped_askers: bfloat16 [8, 8192, 1024], P('dp', 'seq'), may hold values from -6 to 6
- mapped_lookups: bfloat16 [8, 8192, 1024], P('dp', 'seq'), may hold values from -6 to 6
- mapped_contents: bfloat16 [8, 8192, 1024], P('dp', 'seq'), may hold values from -24 to 24
- result_cotangent: bfloat16 [8, 8192, 1024], P('dp', 'seq'), may hold values from -6 to 6
- result_weight_matrix: bfloat16 [1024, 1024], replicated, may hold values from -0.1875 to 0.1875
- reference_comb_shift: int32 [32, 32], P('seq'), may hold values from 0 to 7
- symbol_frame_label: int32 [8192], replicated, may hold values from 0 to 15, never falling along the last dimension, each value on 1 to 1024 neighbouring positions
Outputs:
- sublayer_out: bfloat16 [8, 8192, 1024], P('dp', 'seq')
- query_grad: bfloat16 [8, 8192, 1024], P('dp', 'seq')
- key_grad: bfloat16 [8, 8192, 1024], P('dp', 'seq')
- value_grad: bfloat16 [8, 8192, 1024], P('dp', 'seq')
- weight_grad: float32 [1024, 1024], P(('dp', 'seq'))
All inputs are finite; a program needn't handle non-finite values.
Results may differ from a plain program's by a relative error of at most 0.012.
Values may be sent and summed in bfloat16 or wider, within the bound.
No kernel may reach another device: no remote copies, remote signals or barrier semaphores. Data moves between devices by JAX's collectives and lax.ppermute only.
A program may use at most 128 MiB of HBM per device.

v0:
```python
import math

import jax
import jax.numpy as jnp
from jax import lax
from jax.sharding import PartitionSpec as P

HEADS = 8
HALF_SPAN = 256
FRAME_SHARDS = 8


def with_halo(value, sides, width):
    for axis, dim in sides:
        peers, length = (lax.axis_size(axis), value.shape[dim])
        up = [(i, (i + 1) % peers) for i in range(peers - 1)]
        down = [(j, i) for i, j in up]
        last = lax.slice_in_dim(value, length - width, length, axis=dim)
        initial = lax.slice_in_dim(value, 0, width, axis=dim)
        before = lax.ppermute(last, axis, up)
        after = lax.ppermute(initial, axis, down)
        value = jnp.concatenate([before, value, after], axis=dim)
    return value


def swapped(value, axis, apart):
    return lax.ppermute(value, axis, [(i, i ^ 1 << apart) for i in range(lax.axis_size(axis))])


def joint_admit_filter(neighbor_frame_label, overall_line_number):
    query_rows = jnp.arange(overall_line_number)[:, None] + HALF_SPAN
    key_cols = jnp.arange(overall_line_number + 2 * HALF_SPAN)[None, :]
    inside_local_distance = jnp.abs(query_rows - key_cols) <= HALF_SPAN
    asker_frame_label = neighbor_frame_label[HALF_SPAN : HALF_SPAN + overall_line_number]
    same_frame_filter = asker_frame_label[:, None] == neighbor_frame_label[None, :]
    return inside_local_distance & same_frame_filter


def attend_shard(query_block, key_win, val_win, key_pil, val_pil, local_admit_filter, grad_att):
    head_dim = query_block.shape[1] // HEADS
    scaling = 1.0 / math.sqrt(head_dim)

    def split_heads(matrix):
        return jnp.transpose(matrix.reshape(matrix.shape[0], HEADS, head_dim), (1, 0, 2))

    def join_heads(matrix):
        return jnp.transpose(matrix, (1, 0, 2)).reshape(matrix.shape[1], HEADS * head_dim)

    def one_head(round_arguments):
        query_head, key_head, val_head, pilot_key, pilot_val, grad_head = round_arguments
        score_win = jnp.dot(query_head, key_head.T, preferred_element_type=jnp.float32) * scaling
        score_win = jnp.where(local_admit_filter, score_win, -jnp.inf)
        score_pil = jnp.dot(query_head, pilot_key.T, preferred_element_type=jnp.float32) * scaling
        row_max = jnp.maximum(jnp.max(score_win, axis=1), jnp.max(score_pil, axis=1))[:, None]
        exp_win = jnp.exp(score_win - row_max)
        exp_pil = jnp.exp(score_pil - row_max)
        softmax_total = jnp.sum(exp_win, axis=1, keepdims=True) + jnp.sum(
            exp_pil, axis=1, keepdims=True
        )
        prob_win = exp_win / softmax_total
        prob_pil = exp_pil / softmax_total
        weight_win = prob_win.astype(jnp.bfloat16)
        weight_pil = prob_pil.astype(jnp.bfloat16)
        attended = (
            jnp.dot(weight_win, val_head, preferred_element_type=jnp.float32)
            + jnp.dot(weight_pil, pilot_val, preferred_element_type=jnp.float32)
        ).astype(jnp.bfloat16)
        dprob_win = jnp.dot(grad_head, val_head.T, preferred_element_type=jnp.float32)
        dprob_pil = jnp.dot(grad_head, pilot_val.T, preferred_element_type=jnp.float32)
        delta = jnp.sum(
            grad_head.astype(jnp.float32) * attended.astype(jnp.float32), axis=1, keepdims=True
        )
        dscore_win = (prob_win * (dprob_win - delta)).astype(jnp.bfloat16)
        dscore_pil = (prob_pil * (dprob_pil - delta)).astype(jnp.bfloat16)
        query_grad = (
            jnp.dot(dscore_win, key_head, preferred_element_type=jnp.float32)
            + jnp.dot(dscore_pil, pilot_key, preferred_element_type=jnp.float32)
        ) * scaling
        keywin_grad = (
            jnp.dot(dscore_win.T, query_head, preferred_element_type=jnp.float32) * scaling
        )
        valwin_grad = jnp.dot(weight_win.T, grad_head, preferred_element_type=jnp.float32)
        keypil_grad = (
            jnp.dot(dscore_pil.T, query_head, preferred_element_type=jnp.float32) * scaling
        )
        valpil_grad = jnp.dot(weight_pil.T, grad_head, preferred_element_type=jnp.float32)
        return (attended, query_grad, keywin_grad, valwin_grad, keypil_grad, valpil_grad)

    stacked = lax.map(
        one_head,
        (
            split_heads(query_block),
            split_heads(key_win),
            split_heads(val_win),
            split_heads(key_pil),
            split_heads(val_pil),
            split_heads(grad_att),
        ),
    )
    return tuple((join_heads(matrix) for matrix in stacked))


def on_device(
    mapped_askers,
    mapped_lookups,
    mapped_contents,
    result_cotangent,
    result_weight_matrix,
    reference_comb_shift,
    symbol_frame_label,
):
    query_block = mapped_askers[0]
    grad_block = result_cotangent[0]
    overall_line_number = query_block.shape[0]
    model_width = query_block.shape[1]
    group_size = lax.axis_size("seq")
    current_shard_index = lax.axis_index("seq")
    pil_count = reference_comb_shift.shape[1]
    frame_pilots = pil_count * FRAME_SHARDS
    group_bits = FRAME_SHARDS.bit_length() - 1
    gather_bits = list(range(group_bits))
    reduce_bits = list(reversed(gather_bits))
    bit_shape = (2,) + (2,) * group_bits + (pil_count, model_width)
    grad_att = jnp.dot(
        grad_block, result_weight_matrix.T, preferred_element_type=jnp.float32
    ).astype(jnp.bfloat16)
    pair_rows = jnp.stack([mapped_lookups[0], mapped_contents[0]])
    window = with_halo(pair_rows, (("seq", 1),), HALF_SPAN)
    pilot_slots = (
        jnp.arange(pil_count, dtype=jnp.int32) * (overall_line_number // pil_count)
        + reference_comb_shift[0]
    )
    own_pilots = jnp.take(pair_rows, pilot_slots, axis=1)
    frame_pil = own_pilots
    for bit_number in gather_bits:
        partner = swapped(frame_pil, "seq", bit_number)
        upper_side = current_shard_index >> bit_number & 1 == 1
        frame_pil = jnp.where(
            upper_side,
            jnp.concatenate([partner, frame_pil], 1),
            jnp.concatenate([frame_pil, partner], 1),
        )
    held_bits = list(reversed(gather_bits))
    gather_perm = (
        [0]
        + [1 + held_bits.index(bit_number) for bit_number in range(group_bits - 1, -1, -1)]
        + [group_bits + 1, group_bits + 2]
    )
    frame_pil = jnp.transpose(frame_pil.reshape(bit_shape), gather_perm).reshape(
        2, frame_pilots, model_width
    )
    extended_frame_label = jnp.pad(symbol_frame_label, (HALF_SPAN, HALF_SPAN), constant_values=-1)
    neighbor_frame_label = lax.dynamic_slice_in_dim(
        extended_frame_label,
        current_shard_index * overall_line_number,
        overall_line_number + 2 * HALF_SPAN,
        0,
    )
    local_admit_filter = joint_admit_filter(neighbor_frame_label, overall_line_number)
    results = attend_shard(
        query_block, window[0], window[1], frame_pil[0], frame_pil[1], local_admit_filter, grad_att
    )
    attended, query_grad, keywin_grad, valwin_grad, keypil_grad, valpil_grad = results
    mixed_rows = jnp.dot(attended, result_weight_matrix, preferred_element_type=jnp.float32).astype(
        jnp.bfloat16
    )
    weight_share = lax.psum_scatter(
        jnp.dot(attended.T, grad_block, preferred_element_type=jnp.float32),
        ("dp", "seq"),
        scatter_dimension=0,
        tiled=True,
    )
    weight_grad = weight_share / math.sqrt(lax.axis_size("dp") * group_size * overall_line_number)
    win_round = lax.optimization_barrier(jnp.stack([keywin_grad, valwin_grad]).astype(jnp.bfloat16))
    win_grads = win_round.astype(jnp.float32)
    rim_grads = jnp.concatenate(
        [win_round[:, :HALF_SPAN], win_round[:, overall_line_number + HALF_SPAN :]], 1
    )
    beside = with_halo(rim_grads, (("seq", 1),), HALF_SPAN).astype(jnp.float32)
    from_left = beside[:, :HALF_SPAN]
    from_right = beside[:, 3 * HALF_SPAN :]
    pair_grad = win_grads[:, HALF_SPAN : HALF_SPAN + overall_line_number] + from_left + from_right
    pilot_round = lax.optimization_barrier(
        jnp.stack([keypil_grad, valpil_grad]).astype(jnp.bfloat16)
    )
    reduce_perm = (
        [0]
        + [1 + (group_bits - 1 - bit_number) for bit_number in reduce_bits]
        + [group_bits + 1, group_bits + 2]
    )
    pilot_back = jnp.transpose(
        pilot_round.astype(jnp.float32).reshape(bit_shape), reduce_perm
    ).reshape(2, frame_pilots, model_width)
    for bit_number in reduce_bits:
        half_rows = pilot_back.shape[1] // 2
        lower_half = pilot_back[:, :half_rows]
        upper_half = pilot_back[:, half_rows:]
        upper_side = current_shard_index >> bit_number & 1 == 1
        outgoing = jnp.where(upper_side, lower_half, upper_half)
        kept_half = jnp.where(upper_side, upper_half, lower_half)
        pilot_back = kept_half + swapped(outgoing.astype(jnp.bfloat16), "seq", bit_number).astype(
            outgoing.dtype
        )
    pair_grad = pair_grad.at[:, pilot_slots].add(pilot_back)
    return (
        mixed_rows[None],
        query_grad.astype(jnp.bfloat16)[None],
        pair_grad[0].astype(jnp.bfloat16)[None],
        pair_grad[1].astype(jnp.bfloat16)[None],
        weight_grad,
    )


def solution(mesh):
    return jax.shard_map(
        on_device,
        mesh=mesh,
        in_specs=(
            P("dp", "seq", None),
            P("dp", "seq", None),
            P("dp", "seq", None),
            P("dp", "seq", None),
            P(),
            P("seq", None),
            P(),
        ),
        out_specs=(
            P("dp", "seq", None),
            P("dp", "seq", None),
            P("dp", "seq", None),
            P("dp", "seq", None),
            P(("dp", "seq"), None),
        ),
        check_vma=False,
    )
```

profile of v0, /device:TPU:32, one launch (start us, length us, event | category | flops | bytes accessed | tf_op | source)
XLA Modules:
  0.0 633.9 jit_solution(7752951473432171265)
XLA Ops:
  8.7 1.9 copy.45
  10.5 1.9 copy.46
  13.4 3.2 pad_maximum_fusion.5
  16.6 2.0 gather_fusion
  20.5 3.8 collective-permute-done.2
  25.8 3.3 collective-permute-start.3
  29.1 3.6 collective-permute-start
  34.0 2.3 collective-permute-done.3
  36.2 3.0 broadcast_select_fusion.1
  39.2 2.3 collective-permute-start.4
  41.6 2.6 convolution_convert_fusion.1
  44.3 2.1 copy.68
  46.4 2.0 copy.44
  48.4 23.1 %collective-permute-done.4 = bf16[2,128,1024]{2,0,1:T(2,128)(2,1)} collective-permute-done((bf16[2,128,1024]{2,0,1:T(2,128)(2,1)}, bf16[2,128,1024]{2,0,1:T(2,128)(2,1)}, u32[]{:S(2)}, u32[]{:S(2)}) %collective-permute-start.4) | collective-permute-done | bytes 524320 | tf_op jit(solution)/shard_map/ppermute | solution.py:27
  71.5 3.5 broadcast_select_fusion
  75.1 2.5 fusion.83
  77.5 3.5 copy.50
  81.0 3.5 copy.48
  84.5 22.8 %pad_maximum_fusion = bf16[2,768,1024]{2,0,1:T(2,128)(2,1)S(1)} fusion(bf16[2,256,1024]{2,0,1:T(2,128)(2,1)} %collective-permute-done.1, bf16[1,256,1024]{2,0,1:T(2,128)(2,1)} %copy-done.7, bf16[1,256,1024]{2,0,1:T(2,128)(2,1)S(1)} %copy.45, bf16[2,256,1024]{2,0,1:T(2,128)(2,1)} %collective-permute-done), kind=kLoop, calls=%fused_computation.87 | loop fusion | flops 12582912 | bytes 6291456 | tf_op jit(solution)/shard_map/concatenate | solution.py:22
  107.3 6.0 fusion.81
  113.2 8.2 %copy.49 = bf16[1,768,1024]{1,2,0:T(8,128)(2,1)} copy(bf16[1,768,1024]{2,0,1:T(2,128)(2,1)} %get-tuple-element.212) | data formatting | bytes 3145728 | tf_op jit(solution)/shard_map/slice | solution.py:161
  121.4 8.2 %copy.47 = bf16[1,768,1024]{1,2,0:T(8,128)(2,1)} copy(bf16[1,768,1024]{2,0,1:T(2,128)(2,1)} %get-tuple-element.213) | data formatting | bytes 3145728 | tf_op jit(solution)/shard_map/slice | solution.py:161
  129.6 160.1 %while.21 = (s32[]{:T(128)}, bf16[8,256,128]{1,2,0:T(8,128)(2,1)}, bf16[8,256,128]{2,1,0:T(8,128)(2,1)}, bf16[8,768,128]{1,2,0:T(8,128)(2,1)}, bf16[8,768,128]{1...) while((s32[]{:T(128)}, bf16[8,256,128]{1,2,0:T(8,128)(2,1)}, ...), condition=%wide.region_6.7_spmd.clone, body=%wide.region_0.6_spmd.clone.sunk | while | flops 408091904 | bytes 14460093 | solution.py:89
  133.7 2.0 bitcast_dynamic-update-slice_fusion.2
  139.9 2.2 fusion.155
  144.3 1.8 fusion.153
  153.8 2.0 bitcast_dynamic-update-slice_fusion.2
  159.9 2.2 fusion.155
  164.3 1.8 fusion.153
  173.7 2.0 bitcast_dynamic-update-slice_fusion.2
  179.9 2.2 fusion.155
  184.3 1.8 fusion.153
  187.9 1.7 fusion.157
  193.8 2.0 bitcast_dynamic-update-slice_fusion.2
  199.9 2.2 fusion.155
  204.3 1.8 fusion.153
  213.8 2.0 bitcast_dynamic-update-slice_fusion.2
  220.0 2.2 fusion.155
  224.3 1.8 fusion.153
  233.8 2.0 bitcast_dynamic-update-slice_fusion.2
  240.0 2.2 fusion.155
  244.3 1.8 fusion.153
  253.8 2.0 bitcast_dynamic-update-slice_fusion.2
  260.0 2.2 fusion.155
  264.3 1.8 fusion.153
  273.8 2.0 bitcast_dynamic-update-slice_fusion.2
  280.0 2.2 fusion.155
  284.3 1.8 fusion.153
  292.8 8.4 %copy.60 = bf16[1,768,1024]{2,0,1:T(2,128)(2,1)} copy(bf16[1,768,1024]{1,2,0:T(8,128)(2,1)} %bitcast.209) | data formatting | bytes 3145728 | tf_op jit(solution)/shard_map/stack;reshape | solution.py:174
  301.3 8.5 %copy.61 = bf16[1,768,1024]{2,0,1:T(2,128)(2,1)} copy(bf16[1,768,1024]{1,2,0:T(8,128)(2,1)} %bitcast.210) | data formatting | bytes 3145728 | tf_op jit(solution)/shard_map/stack;reshape | solution.py:174
  309.7 8.0 %pad_maximum_fusion.1 = bf16[2,768,1024]{2,0,1:T(2,128)(2,1)S(1)} fusion(bf16[1,768,1024]{2,0,1:T(2,128)(2,1)} %copy.61, bf16[1,768,1024]{2,0,1:T(2,128)(2,1)} %copy.60), kind=kLoop, calls=%fused_computation.88 | loop fusion | flops 6291456 | bytes 6291456 | tf_op jit(solution)/shard_map/stack | solution.py:174
  317.8 2.5 fusion.80
  320.2 2.3 collective-permute-start.5
  327.5 3.7 fusion.73
  331.3 24.4 %collective-permute-done.8 = bf16[2,64,1024]{1,2,0:T(8,128)(2,1)} collective-permute-done((bf16[2,64,1024]{1,2,0:T(8,128)(2,1)}, bf16[2,64,1024]{1,2,0:T(8,128)(2,1)}, u32[]{:S(2)}, u32[]{:S(2)}) %collective-permute-start.8) | collective-permute-done | bytes 262176 | tf_op jit(solution)/shard_map/ppermute | solution.py:27
  358.1 7.6 %collective-permute-start.9 = (bf16[2,32,1024]{1,2,0:T(8,128)(2,1)}, bf16[2,32,1024]{1,2,0:T(8,128)(2,1)}, u32[]{:S(2)}, u32[]{:S(2)}) collective-permute-start(bf16[2,32,1024]{1,2,0:T(8,128)(2,1)} %select_convert_fusion), channel_id=1, source_target_pairs={{0,1},{1,0},{2,3},{3,2},{4,5},{5,4},{6,7},{7,6},{8,9},{9,8},{10,11... | collective-permute-start | bytes 393224 | tf_op jit(solution)/shard_map/ppermute | solution.py:27
  365.7 2.6 fusion.72
  369.4 2.1 convert_element_type.78
  371.5 4.2 collective-permute-done.9
  375.7 2.4 add_bitcast_fusion
  379.7 11.8 %fusion.71 = f32[2,256,1024]{2,0,1:T(2,128)} fusion(bf16[2,256,1024]{2,0,1:T(2,128)(2,1)} %collective-permute-done.6, bf16[2,256,1024]{2,0,1:T(2,128)(2,1)} %get-tuple-element.210, bf16[2,256,1024]{2,0,1:T(2,128)(2,1)} %get-tuple-element.211, bf16[2,256,1024]{2,0,1:T(2,128)(2,1)} %collective-permute-done.5, bf16[2,768,1024]{2,0,1:T(2,128)(2,1)} %copy-done.6), kind=kLoop, calls=%fused_computation.90 | loop fusion | flops 5767168 | bytes 7340032 | tf_op jit(solution)/shard_map/add | solution.py:182
  391.5 4.7 scatter_fusion
  396.2 2.3 convert.29
  402.0 223.7 %all-reduce.4.cloned.1.call-done = f32[1024,1024]{1,0:T(8,128)} async-done(((f32[1024,1024]{1,0:T(8,128)}), f32[1024,1024]{1,0:T(8,128)}) %all-reduce.4.cloned.1.call-update) | async-done | bytes 4194320
  (226 shorter events, 134.8 us)
Async XLA Ops:
  7.2 34.4 %copy-start = (bf16[1024,1024]{1,0:T(8,128)(2,1)S(1)}, bf16[1024,1024]{1,0:T(8,128)(2,1)}, u32[]{:S(2)}) copy-start(bf16[1024,1024]{1,0:T(8,128)(2,1)} %param.13) | copy-start | bytes 6291460
  7.2 618.5 %all-reduce.4.cloned.1.call-start = ((), (), s32[]{:S(2)}) async-start(), calls=%async_computation | async-start | bytes 8388608
  12.4 1.0 copy-start.7
  18.8 5.4 collective-permute-start.2
  25.8 10.4 %collective-permute-start.3 = (bf16[2,64,1024]{2,0,1:T(2,128)(2,1)S(1)}, bf16[2,64,1024]{2,0,1:T(2,128)(2,1)}, u32[]{:S(2)}, u32[]{:S(2)}) collective-permute-start(bf16[2,64,1024]{2,0,1:T(2,128)(2,1)S(1)} %broadcast_select_fusion.2), channel_id=1, source_target_pairs={{0,2},{1,3},{2,0},{3,1},{4,6},{5,7},{6,4},{7,5},{8,10},{9,11},{10,... | collective-permute-start | bytes 786440 | tf_op jit(solution)/shard_map/ppermute | solution.py:27
  29.1 55.4 %collective-permute-start = (bf16[2,256,1024]{2,0,1:T(2,128)(2,1)}, bf16[2,256,1024]{2,0,1:T(2,128)(2,1)}, u32[]{:S(2)}, u32[]{:S(2)}) collective-permute-start(bf16[2,256,1024]{2,0,1:T(2,128)(2,1)} %pad_maximum_fusion.5), channel_id=1, source_target_pairs={{0,1},{1,2},{2,3},{3,4},{4,5},{5,6},{6,7},{7,8},{8,9},{9,10},{10,1... | collective-permute-start | bytes 3145736 | tf_op jit(solution)/shard_map/ppermute | solution.py:20
  32.7 51.8 %collective-permute-start.1 = (bf16[2,256,1024]{2,0,1:T(2,128)(2,1)}, bf16[2,256,1024]{2,0,1:T(2,128)(2,1)}, u32[]{:S(2)}, u32[]{:S(2)}) collective-permute-start(bf16[2,256,1024]{2,0,1:T(2,128)(2,1)} %pad_maximum_fusion.5), channel_id=1, source_target_pairs={{1,0},{2,1},{3,2},{4,3},{5,4},{6,5},{7,6},{8,7},{9,8},{10,9},{11,1... | collective-permute-start | bytes 3145736 | tf_op jit(solution)/shard_map/ppermute | solution.py:21
  34.0 10.2 %copy-start.10 = (s32[8192]{0:T(1024)S(1)}, s32[8192]{0:T(1024)}, u32[]{:S(2)}) copy-start(s32[8192]{0:T(1024)} %param.15) | copy-start | bytes 98308
  39.2 32.3 %collective-permute-start.4 = (bf16[2,128,1024]{2,0,1:T(2,128)(2,1)}, bf16[2,128,1024]{2,0,1:T(2,128)(2,1)}, u32[]{:S(2)}, u32[]{:S(2)}) collective-permute-start(bf16[2,128,1024]{2,0,1:T(2,128)(2,1)} %broadcast_select_fusion.1), channel_id=1, source_target_pairs={{0,4},{1,5},{2,6},{3,7},{4,0},{5,1},{6,2},{7,3},{8,12},{9,13},{10,... | collective-permute-start | bytes 1572872 | tf_op jit(solution)/shard_map/ppermute | solution.py:27
  131.0 5.6 copy-start.1
  151.0 5.6 copy-start.1
  171.0 5.6 copy-start.1
  191.1 5.6 copy-start.1
  211.1 5.6 copy-start.1
  231.1 5.6 copy-start.1
  251.1 5.6 copy-start.1
  271.1 5.6 copy-start.1
  291.1 1.3 copy-start.4
  292.5 31.4 %collective-permute-start.7 = (bf16[2,128,1024]{1,2,0:T(8,128)(2,1)S(1)}, bf16[2,128,1024]{1,2,0:T(8,128)(2,1)}, u32[]{:S(2)}, u32[]{:S(2)}) collective-permute-start(bf16[2,128,1024]{1,2,0:T(8,128)(2,1)S(1)} %select_convert_fusion.2), channel_id=1, source_target_pairs={{0,4},{1,5},{2,6},{3,7},{4,0},{5,1},{6,2},{7,3},{8,12},{9,13},{10,... | collective-permute-start | bytes 1572872 | tf_op jit(solution)/shard_map/ppermute | solution.py:27
  317.8 2.5 copy-start.6
  317.8 6.2 copy-start.5
  320.2 59.4 %collective-permute-start.5 = (bf16[2,256,1024]{2,0,1:T(2,128)(2,1)}, bf16[2,256,1024]{2,0,1:T(2,128)(2,1)}, u32[]{:S(2)}, u32[]{:S(2)}) collective-permute-start(bf16[2,256,1024]{2,0,1:T(2,128)(2,1)} %get-tuple-element.210), channel_id=1, source_target_pairs={{0,1},{1,2},{2,3},{3,4},{4,5},{5,6},{6,7},{7,8},{8,9},{9,10},{10,1... | collective-permute-start | bytes 3145736 | tf_op jit(solution)/shard_map/ppermute | solution.py:20
  322.5 5.0 copy-start.8
  322.5 57.2 %collective-permute-start.6 = (bf16[2,256,1024]{2,0,1:T(2,128)(2,1)}, bf16[2,256,1024]{2,0,1:T(2,128)(2,1)}, u32[]{:S(2)}, u32[]{:S(2)}) collective-permute-start(bf16[2,256,1024]{2,0,1:T(2,128)(2,1)} %get-tuple-element.211), channel_id=1, source_target_pairs={{1,0},{2,1},{3,2},{4,3},{5,4},{6,5},{7,6},{8,7},{9,8},{10,9},{11,1... | collective-permute-start | bytes 3145736 | tf_op jit(solution)/shard_map/ppermute | solution.py:21
  326.2 29.5 %collective-permute-start.8 = (bf16[2,64,1024]{1,2,0:T(8,128)(2,1)}, bf16[2,64,1024]{1,2,0:T(8,128)(2,1)}, u32[]{:S(2)}, u32[]{:S(2)}) collective-permute-start(bf16[2,64,1024]{1,2,0:T(8,128)(2,1)} %select_convert_fusion.1), channel_id=1, source_target_pairs={{0,2},{1,3},{2,0},{3,1},{4,6},{5,7},{6,4},{7,5},{8,10},{9,11},{10,... | collective-permute-start | bytes 786440 | tf_op jit(solution)/shard_map/ppermute | solution.py:27
  357.1 11.2 %copy-start.2 = (f32[2,64,1024]{1,2,0:T(8,128)}, f32[2,64,1024]{1,2,0:T(8,128)S(1)}, u32[]{:S(2)}) copy-start(f32[2,64,1024]{1,2,0:T(8,128)S(1)} %convert_add_fusion.1) | copy-start | bytes 1572868
  357.1 11.2 %copy-start.9 = (bf16[8,256,128]{2,1,0:T(8,128)(2,1)S(1)}, bf16[8,256,128]{2,1,0:T(8,128)(2,1)}, u32[]{:S(2)}) copy-start(bf16[8,256,128]{2,1,0:T(8,128)(2,1)} %get-tuple-element.83) | copy-start | bytes 1572868
  358.1 17.6 %collective-permute-start.9 = (bf16[2,32,1024]{1,2,0:T(8,128)(2,1)}, bf16[2,32,1024]{1,2,0:T(8,128)(2,1)}, u32[]{:S(2)}, u32[]{:S(2)}) collective-permute-start(bf16[2,32,1024]{1,2,0:T(8,128)(2,1)} %select_convert_fusion), channel_id=1, source_target_pairs={{0,1},{1,0},{2,3},{3,2},{4,5},{5,4},{6,7},{7,6},{8,9},{9,8},{10,11... | collective-permute-start | bytes 393224 | tf_op jit(solution)/shard_map/ppermute | solution.py:27
  368.3 7.4 %copy-start.3 = (f32[2,64,1024]{1,2,0:T(8,128)S(1)}, f32[2,64,1024]{1,2,0:T(8,128)}, u32[]{:S(2)}) copy-start(f32[2,64,1024]{1,2,0:T(8,128)} %copy-done.2) | copy-start | bytes 1572868
Sparse Core Ops, SparseCore 0:
  331.4 294.1 all-reduce.3
where the time goes:
time: 643 us; the launch traced here: 634 us
  waiting for transfers between devices  281 us (44%)
  matrix products  145 us (23%)
  local copies, waits for them, and re-layouts  84.2 us (13%)
  other arithmetic  82.8 us (13%)
  starting transfers between devices  25.2 us (4%)
  between operations  14.3 us (2%)
    unnamed x2, waiting for transfers between devices  224 us
    ppermute x6, waiting for transfers between devices, swapped(): lax.ppermute(value, axis, [(i, i ^ 1 << apart) for i in range(lax.axis_si...  57.8 us
    concatenate x1, other arithmetic, with_halo(): value = jnp.concatenate([before, value, after], axis=dim)  22.8 us
    dot_general x8, matrix products, one_head(): jnp.dot(weight_win.T, grad_head, preferred_element_type=jnp.float32)  17.8 us
    another operation x2, local copies, waits for them, and re-layouts, on_device(): jnp.stack([keywin_grad, valwin_grad]).astype(jnp.bfloat16)  16.9 us
    ppermute x6, starting transfers between devices, swapped(): lax.ppermute(value, axis, [(i, i ^ 1 << apart) for i in range(lax.axis_si...  16.6 us
    dot_general x8, matrix products, one_head(): jnp.dot(weight_win, val_head, preferred_element_type=jnp.float32)  15.8 us
    dot_general x8, matrix products, one_head(): jnp.dot(dscore_win, key_head, preferred_element_type=jnp.float32)  14.6 us
  transfers between devices with their start and end apart: 11, of which 6 were waited for; matrix products, arithmetic and copies ran while one was open for 14% of the time, Pallas kernels for 0%

commit v1 on v0

v1 whole, which is shorter than its diff:
```python
import functools
import math

import jax
import jax.numpy as jnp
from jax import lax
from jax.experimental import pallas as pl
from jax.experimental.pallas import tpu as pltpu
from jax.sharding import Mesh, PartitionSpec as P

HEADS = 8
HALF_SPAN = 256
SHARDS = 8
ROWS = 256
HD = 128
PILS = 32
SLOT = ROWS // PILS
FRAME_ROWS = SHARDS * ROWS
BLOCKS = SHARDS + 2
KV_ROWS = 2 * ROWS + PILS
BF = jnp.bfloat16
F32 = jnp.float32

FRAME = ("xl", "y")
FRAMES = ("zh", "xh")
SCALE = 1.0 / math.sqrt(HD)
LOG2E = math.log2(math.e)


def mm(a, b, ca, cb):
    return lax.dot_general(a, b, (((ca,), (cb,)), ((), ())), preferred_element_type=F32)


def pack_kv_kernel(k_ref, v_ref, s_ref, o_ref):
    o_ref[0, :ROWS] = k_ref[...]
    o_ref[0, ROWS : 2 * ROWS] = v_ref[...]
    o_ref[0, 2 * ROWS :] = s_ref[...]


def pack_kv(k, v, shift_cols):
    return pl.pallas_call(
        pack_kv_kernel,
        grid=(HEADS,),
        in_specs=[
            pl.BlockSpec((ROWS, HD), lambda h: (0, h)),
            pl.BlockSpec((ROWS, HD), lambda h: (0, h)),
            pl.BlockSpec((PILS, HD), lambda h: (0, 0)),
        ],
        out_specs=pl.BlockSpec((1, KV_ROWS, HD), lambda h: (h, 0, 0)),
        out_shape=jax.ShapeDtypeStruct((HEADS, KV_ROWS, HD), BF),
        name="pack_kv",
    )(k, v, shift_cols)


def pack_qg_kernel(q_ref, g_ref, w_ref, o_ref):
    o_ref[0, :ROWS] = q_ref[...]
    o_ref[0, ROWS:] = mm(g_ref[...], w_ref[...], 1, 1).astype(BF)


def pack_qg(q, g, w):
    width = g.shape[1]
    return pl.pallas_call(
        pack_qg_kernel,
        grid=(HEADS,),
        in_specs=[
            pl.BlockSpec((ROWS, HD), lambda h: (0, h)),
            pl.BlockSpec((ROWS, width), lambda h: (0, 0)),
            pl.BlockSpec((HD, width), lambda h: (h, 0)),
        ],
        out_specs=pl.BlockSpec((1, 2 * ROWS, HD), lambda h: (h, 0, 0)),
        out_shape=jax.ShapeDtypeStruct((HEADS, 2 * ROWS, HD), BF),
        name="pack_qg",
    )(q, g, w)


def pilot_pick(shift):
    where_to = lax.broadcasted_iota(jnp.int32, (PILS, HD), 0) * SLOT + shift.astype(F32).astype(jnp.int32)
    lane = lax.broadcasted_iota(jnp.int32, (PILS, HD), 1)
    picks = [jnp.where(lane + part * HD == where_to, 1.0, 0.0) for part in range(ROWS // HD)]
    return jnp.concatenate(picks, axis=1).astype(BF)


def attend_kernel(
    kv_ref, qg_ref, left_ref, right_ref, labk_ref, labq_ref,
    att_ref, dq_ref, dkv_ref, dleft_ref, dright_ref,
    k_all, v_all, kt_all, vt_all, k_pil, v_pil, kt_pil, vt_pil, dk_all, dv_all, dk_pil, dv_pil,
):
    i = pl.program_id(0)

    @pl.when(i == 0)
    def _():
        for b in range(BLOCKS):
            if b == 0:
                kb, vb = left_ref[:ROWS], left_ref[ROWS:]
            elif b == BLOCKS - 1:
                kb, vb = right_ref[:ROWS], right_ref[ROWS:]
            else:
                kb, vb = kv_ref[b - 1, :ROWS], kv_ref[b - 1, ROWS : 2 * ROWS]
            k_all[b] = kb
            v_all[b] = vb
            kt_all[b] = kb.T
            vt_all[b] = vb.T
            if 0 < b < BLOCKS - 1:
                pick = pilot_pick(kv_ref[b - 1, 2 * ROWS :])
                at = slice((b - 1) * PILS, b * PILS)
                k_pil[at] = mm(pick, kb, 1, 0).astype(BF)
                v_pil[at] = mm(pick, vb, 1, 0).astype(BF)
        kt_pil[...] = k_pil[...].T
        vt_pil[...] = v_pil[...].T
        dk_all[...] = jnp.zeros_like(dk_all)
        dv_all[...] = jnp.zeros_like(dv_all)
        dk_pil[...] = jnp.zeros_like(dk_pil)
        dv_pil[...] = jnp.zeros_like(dv_pil)

    q = qg_ref[i, :ROWS]
    ga = qg_ref[i, ROWS:]
    label_q = labq_ref[i]
    key_at = lax.broadcasted_iota(jnp.int32, (ROWS, ROWS), 0)
    query_at = lax.broadcasted_iota(jnp.int32, (ROWS, ROWS), 1)
    scores = []
    for part in range(3):
        label_k = labk_ref[i + part][:, :1]
        admit = label_k == label_q
        if part == 0:
            admit = admit & (key_at >= query_at)
        elif part == 2:
            admit = admit & (key_at <= query_at)
        scores.append(jnp.where(admit, mm(k_all[i + part], q, 1, 1), -jnp.inf))
    scores.append(mm(k_pil[...], q, 1, 1))
    top = functools.reduce(jnp.maximum, [jnp.max(s, axis=0, keepdims=True) for s in scores])
    factor = SCALE * LOG2E
    top = top * factor
    exps = [jnp.exp2(s * factor - top) for s in scores]
    inverse = 1.0 / functools.reduce(jnp.add, [jnp.sum(e, axis=0, keepdims=True) for e in exps])
    probs = [e * inverse for e in exps]
    weights = [p.astype(BF) for p in probs]
    vts = [vt_all[i + part] for part in range(3)] + [vt_pil[...]]
    att_t = functools.reduce(jnp.add, [mm(vt, w, 1, 0) for vt, w in zip(vts, weights)])
    att = att_t.T.astype(BF)
    att_ref[i] = att
    product = ga.astype(F32) * att.astype(F32)
    delta = jnp.sum(product.T, axis=0, keepdims=True)
    vals = [v_all[i + part] for part in range(3)] + [v_pil[...]]
    kts = [kt_all[i + part] for part in range(3)] + [kt_pil[...]]
    dq_t = jnp.zeros((HD, ROWS), F32)
    for part in range(4):
        dprob = mm(vals[part], ga, 1, 1)
        dscore = (probs[part] * (dprob - delta)).astype(BF)
        dq_t = dq_t + mm(kts[part], dscore, 1, 0)
        dk = mm(dscore, q, 1, 0)
        dv = mm(weights[part], ga, 1, 0)
        if part < 3:
            dk_all[i + part] += dk
            dv_all[i + part] += dv
        else:
            dk_pil[...] += dk
            dv_pil[...] += dv
    dq_ref[i] = (dq_t * SCALE).T.astype(BF)

    @pl.when(i == SHARDS - 1)
    def _():
        for sh in range(SHARDS):
            pick = pilot_pick(kv_ref[sh, 2 * ROWS :])
            at = slice(sh * PILS, (sh + 1) * PILS)
            for which, (own, pil, by) in enumerate(((dk_all, dk_pil, SCALE), (dv_all, dv_pil, 1.0))):
                fine = pil[at]
                high = fine.astype(BF)
                low = (fine - high.astype(F32)).astype(BF)
                total = own[sh + 1] + (mm(pick, high, 0, 0) + mm(pick, low, 0, 0))
                dkv_ref[sh, which * ROWS : (which + 1) * ROWS] = (total * by).astype(BF)
        for ref, b in ((dleft_ref, 0), (dright_ref, BLOCKS - 1)):
            ref[:ROWS] = (dk_all[b] * SCALE).astype(BF)
            ref[ROWS:] = dv_all[b].astype(BF)


def whole(shape):
    return pl.BlockSpec(shape, lambda i: (0,) * len(shape))


def attend(kv, qg, left, right, labk, labq):
    ins = (kv, qg, left, right, labk, labq)
    outs = [
        (SHARDS, ROWS, HD), (SHARDS, ROWS, HD), (SHARDS, 2 * ROWS, HD), (2 * ROWS, HD), (2 * ROWS, HD),
    ]
    matmul = 2 * FRAME_ROWS * 4 * ROWS * HD
    return pl.pallas_call(
        attend_kernel,
        grid=(SHARDS,),
        in_specs=[whole(a.shape) for a in ins],
        out_specs=[whole(s) for s in outs],
        out_shape=[jax.ShapeDtypeStruct(s, BF) for s in outs],
        scratch_shapes=[
            pltpu.VMEM((BLOCKS, ROWS, HD), BF),
            pltpu.VMEM((BLOCKS, ROWS, HD), BF),
            pltpu.VMEM((BLOCKS, HD, ROWS), BF),
            pltpu.VMEM((BLOCKS, HD, ROWS), BF),
            pltpu.VMEM((SHARDS * PILS, HD), BF),
            pltpu.VMEM((SHARDS * PILS, HD), BF),
            pltpu.VMEM((HD, SHARDS * PILS), BF),
            pltpu.VMEM((HD, SHARDS * PILS), BF),
            pltpu.VMEM((BLOCKS, ROWS, HD), F32),
            pltpu.VMEM((BLOCKS, ROWS, HD), F32),
            pltpu.VMEM((SHARDS * PILS, HD), F32),
            pltpu.VMEM((SHARDS * PILS, HD), F32),
        ],
        compiler_params=pltpu.CompilerParams(vmem_limit_bytes=48 * 1024 * 1024),
        cost_estimate=pl.CostEstimate(
            flops=6 * matmul, bytes_accessed=8 << 20, transcendentals=FRAME_ROWS * 4 * ROWS
        ),
        name="attend",
    )(*ins)


def finish_kernel(att_ref, g_ref, w_ref, mixed_ref, share_ref, acc):
    h = pl.program_id(0)
    att = att_ref[0]
    part = mm(att, w_ref[...], 1, 0)

    @pl.when(h == 0)
    def _():
        acc[...] = part

    @pl.when(h > 0)
    def _():
        acc[...] += part

    share_ref[0] = mm(att, g_ref[...], 0, 0)

    @pl.when(h == HEADS - 1)
    def _():
        mixed_ref[...] = acc[...].astype(BF)


def finish(att, g, w):
    width = g.shape[1]
    return pl.pallas_call(
        finish_kernel,
        grid=(HEADS,),
        in_specs=[
            pl.BlockSpec((1, ROWS, HD), lambda h: (h, 0, 0)),
            pl.BlockSpec((ROWS, width), lambda h: (0, 0)),
            pl.BlockSpec((HD, width), lambda h: (h, 0)),
        ],
        out_specs=[
            pl.BlockSpec((ROWS, width), lambda h: (0, 0)),
            pl.BlockSpec((1, HD, width), lambda h: (h, 0, 0)),
        ],
        out_shape=[
            jax.ShapeDtypeStruct((ROWS, width), BF),
            jax.ShapeDtypeStruct((HEADS, HD, width), F32),
        ],
        scratch_shapes=[pltpu.VMEM((ROWS, width), F32)],
        name="finish",
    )(att, g, w)


def halved(value, dim, axis, bit):
    count = lax.axis_size(axis)
    size = value.shape[dim] // 2
    upper = (lax.axis_index(axis) >> bit) & 1 == 1
    low = lax.slice_in_dim(value, 0, size, axis=dim)
    high = lax.slice_in_dim(value, size, 2 * size, axis=dim)
    out = jnp.where(upper, low, high).astype(BF)
    got = lax.ppermute(out, axis, [(j, j ^ (1 << bit)) for j in range(count)])
    return jnp.where(upper, high, low) + got.astype(F32)


def to_heads(x):
    return lax.all_to_all(x, FRAME, 0, 0, tiled=True)


def joined(x):
    return jnp.transpose(x, (1, 0, 2)).reshape(ROWS, HEADS * HD)


def on_device(askers, lookups, contents, cotangent, w, comb_shift, label):
    q, k, v, g = askers[0], lookups[0], contents[0], cotangent[0]
    frame = lax.axis_index(FRAMES)
    ups = [(j, j + 1) for j in range(lax.axis_size(FRAMES) - 1)]
    downs = [(j, i) for i, j in ups]

    shift_cols = jnp.broadcast_to(comb_shift[0].astype(BF)[:, None], (PILS, HD))
    kv = to_heads(pack_kv(k, v, shift_cols))
    left = lax.ppermute(kv[SHARDS - 1, : 2 * ROWS], FRAMES, ups)
    right = lax.ppermute(kv[0, : 2 * ROWS], FRAMES, downs)
    qg = to_heads(pack_qg(q, g, w))

    label = jnp.pad(label, (HALF_SPAN, HALF_SPAN), constant_values=-1)
    label = lax.dynamic_slice_in_dim(label, frame * FRAME_ROWS, BLOCKS * ROWS, 0)
    labk = jnp.broadcast_to(label.reshape(BLOCKS, ROWS, 1), (BLOCKS, ROWS, HD))
    labq = label[HALF_SPAN : HALF_SPAN + FRAME_ROWS].reshape(SHARDS, 1, ROWS)

    att, dq, dkv, dleft, dright = attend(kv, qg, left, right, labk, labq)

    from_right = lax.ppermute(dleft, FRAMES, downs)
    from_left = lax.ppermute(dright, FRAMES, ups)
    att = to_heads(att)
    mixed, share = finish(att, g, w)

    width = share.shape[-1]
    share = share.reshape(4, 2, HD, width)
    share = halved(share, 1, "c", 0).reshape(4, HD, width)
    share = halved(share, 0, "zl", 1)
    share = halved(share, 0, "zl", 0)[0]
    share = halved(share, 0, "zh", 0)
    share = halved(share, 0, "xh", 0)
    share = halved(share, 0, "xl", 0)
    share = halved(share, 0, "y", 1)
    share = halved(share, 0, "y", 0)
    weight_grad = share * (1.0 / math.sqrt(8 * 32 * ROWS))

    dq = to_heads(dq)
    first = dkv[:1].astype(F32) + from_left.astype(F32)[None]
    last = dkv[SHARDS - 1 :].astype(F32) + from_right.astype(F32)[None]
    dkv = jnp.concatenate([first.astype(BF), dkv[1 : SHARDS - 1], last.astype(BF)], axis=0)
    dkv = to_heads(dkv)
    return (
        mixed[None],
        joined(dq)[None],
        joined(dkv[:, :ROWS])[None],
        joined(dkv[:, ROWS:])[None],
        weight_grad,
    )


def solution(mesh):
    fine = Mesh(mesh.devices.reshape(4, 2, 2, 2, 2, 4), ("zl", "c", "zh", "xh", "xl", "y"))
    dp, seq = ("zl", "c"), ("zh", "xh", "xl", "y")
    rows = P(dp, seq, None)
    return jax.shard_map(
        on_device,
        mesh=fine,
        in_specs=(rows, rows, rows, rows, P(), P(seq, None), P()),
        out_specs=(rows, rows, rows, rows, P(dp + seq, None)),
        check_vma=False,
    )
```

time: 643 us -> 195 us (0.30)
  the two profiles are of different devices: /device:TPU:32 before, /device:TPU:6 now
where the time goes in v1:
time: 195 us; the launch traced here: 194 us
  waiting for transfers between devices  79.4 us (41%)
  starting transfers between devices  54.4 us (28%)
  Pallas kernels  37.8 us (19%)
  other arithmetic  11.7 us (6%)
  local copies, waits for them, and re-layouts  9.67 us (5%)
    ppermute x8, waiting for transfers between devices, halved(): got = lax.ppermute(out, axis, [(j, j ^ 1 << bit) for j in range(count)])  42.4 us
    all_to_all x5, starting transfers between devices, to_heads(): return lax.all_to_all(x, FRAME, 0, 0, tiled=True)  26.6 us
    all_to_all x5, waiting for transfers between devices, to_heads(): return lax.all_to_all(x, FRAME, 0, 0, tiled=True)  17.7 us
    pallas_call x1, Pallas kernels, attend(): pl.pallas_call(attend_kernel, grid=(SHARDS,), in_specs=[whole(a.shape) fo...  16.9 us
    ppermute x1, starting transfers between devices, on_device(): left = lax.ppermute(kv[SHARDS - 1, :2 * ROWS], FRAMES, ups)  9.94 us
    pallas_call x1, Pallas kernels, finish(): pl.pallas_call(finish_kernel, grid=(HEADS,), in_specs=[pl.BlockSpec((1, R...  8.9 us
    ppermute x8, starting transfers between devices, halved(): got = lax.ppermute(out, axis, [(j, j ^ 1 << bit) for j in range(count)])  8.64 us
    unnamed x19, local copies, waits for them, and re-layouts  7.63 us
  transfers between devices with their start and end apart: 17, of which 12 were waited for; matrix products, arithmetic and copies ran while one was open for 3% of the time, Pallas kernels for 4%

profile of v1, /device:TPU:6, one launch (start us, length us, event | category | flops | bytes accessed | tf_op | source)
XLA Modules:
  0.0 193.8 jit_solution(259153051979177650)
XLA Ops:
  0.6 0.7 convert_bitcast_fusion
  1.3 0.7 broadcast_in_dim.28.s_ref
  2.0 5.1 %pack_kv.1 = bf16[8,544,128]{2,1,0:T(8,128)(2,1)} custom-call(bf16[256,1024]{1,0:T(8,128)(2,1)} %bitcast.56, bf16[256,1024]{1,0:T(8,128)(2,1)} %bitcast.57, bf16[32,128]{1,0:T(8,128)(2,1)} %broadcast_in_dim.28.s_ref), custom_call_target="tpu_custom_call" | custom-call | tf_op jit(solution)/shard_map/pack_kv/pallas_call | solution.py:41
  7.0 5.9 %all-to-all-start = ((bf16[8,544,128]{2,1,0:T(8,128)(2,1)}), bf16[8,544,128]{2,1,0:T(8,128)(2,1)S(1)}, u32[]{:S(2)}, u32[]{:S(2)}) async-start(bf16[8,544,128]{2,1,0:T(8,128)(2,1)} %pack_kv.1), calls=%async_computation | async-start | bytes 2228224 | tf_op jit(solution)/shard_map/all_to_all | solution.py:269
  13.0 6.9 %pack_qg.1 = bf16[8,512,128]{2,1,0:T(8,128)(2,1)} custom-call(bf16[256,1024]{1,0:T(8,128)(2,1)} %bitcast.58, bf16[256,1024]{1,0:T(8,128)(2,1)} %bitcast.54, bf16[1024,1024]{1,0:T(8,128)(2,1)} %w_ref.3), custom_call_target="tpu_custom_call" | custom-call | tf_op jit(solution)/shard_map/pack_qg/pallas_call | solution.py:62
  19.8 8.1 %all-to-all-done.kv_ref = bf16[8,544,128]{2,1,0:T(8,128)(2,1)S(1)} async-done(((bf16[8,544,128]{2,1,0:T(8,128)(2,1)}), bf16[8,544,128]{2,1,0:T(8,128)(2,1)S(1)}, u32[]{:S(2)}, u32[]{:S(2)}) %all-to-all-start) | async-done | bytes 1114144 | tf_op jit(solution)/shard_map/all_to_all | solution.py:269
  27.9 4.2 %all-to-all-start.1 = ((bf16[8,512,128]{2,1,0:T(8,128)(2,1)}), bf16[8,512,128]{2,1,0:T(8,128)(2,1)S(1)}, u32[]{:S(2)}, u32[]{:S(2)}) async-start(bf16[8,512,128]{2,1,0:T(8,128)(2,1)} %pack_qg.1), calls=%async_computation.1 | async-start | bytes 2097152 | tf_op jit(solution)/shard_map/all_to_all | solution.py:269
  32.1 9.9 %collective-permute-start = (bf16[512,128]{1,0:T(8,128)(2,1)S(1)}, bf16[512,128]{1,0:T(8,128)(2,1)S(1)}, u32[]{:S(2)}, u32[]{:S(2)}) collective-permute-start(bf16[512,128]{1,0:T(8,128)(2,1)S(1)} %get-tuple-element.25), channel_id=1, source_target_pairs={{0,8},{8,16},{16,24},{1,9},{9,17},{17,25},{2,10},{10,18},{18,26},{... | collective-permute-start | bytes 393224 | tf_op jit(solution)/shard_map/ppermute | solution.py:284
  42.1 1.9 collective-permute-start.1
  44.0 0.1 pad_dynamic-slice_fusion.1
  44.1 0.1 pad_dynamic-slice_fusion
  44.2 2.3 %all-to-all-done.1.qg_ref = bf16[8,512,128]{2,1,0:T(8,128)(2,1)S(1)} async-done(((bf16[8,512,128]{2,1,0:T(8,128)(2,1)}), bf16[8,512,128]{2,1,0:T(8,128)(2,1)S(1)}, u32[]{:S(2)}, u32[]{:S(2)}) %all-to-all-start.1) | async-done | bytes 1048608 | tf_op jit(solution)/shard_map/all_to_all | solution.py:269
  46.5 1.6 collective-permute-done.left_ref
  48.1 7.1 %collective-permute-done.1.right_ref = bf16[512,128]{1,0:T(8,128)(2,1)S(1)} collective-permute-done((bf16[512,128]{1,0:T(8,128)(2,1)S(1)}, bf16[512,128]{1,0:T(8,128)(2,1)S(1)}, u32[]{:S(2)}, u32[]{:S(2)}) %collective-permute-start.1) | collective-permute-done | bytes 131104 | tf_op jit(solution)/shard_map/ppermute | solution.py:285
  55.2 0.4 broadcast_in_dim.30.labk_ref
  55.6 0.2 copy-done.3
  55.9 0.9 copy-done.2
  56.8 0.9 copy-done.4
  57.7 16.9 %attend.1 = (bf16[8,256,128]{2,1,0:T(8,128)(2,1)S(1)}, bf16[8,256,128]{2,1,0:T(8,128)(2,1)}, bf16[8,512,128]{2,1,0:T(8,128)(2,1)S(1)}, bf16[512,128]{1,0:T(8,128)(2,1)S(1)}, bf16[512,128]{1,0:T(8,128)(2,1)S(1)}) custom-call(bf16[8,544,128]{2,1,0:T(8,128)(2,1)S(1)} %all-to-all-done.kv_ref, bf16[8,512,128]{2,1,0:T(8,128)(2,1)S(1)} %all-to-all-done.1.qg_ref, ...), custom_call_target="tpu_custom_call" | custom-call | flops 3221225472 | bytes 8388608 | tf_op jit(solution)/shard_map/attend/pallas_call | solution.py:186
  74.7 0.8 copy-done
  75.4 5.7 %all-to-all-start.2 = ((bf16[8,256,128]{2,1,0:T(8,128)(2,1)}), bf16[8,256,128]{2,1,0:T(8,128)(2,1)S(1)}, u32[]{:S(2)}, u32[]{:S(2)}) async-start(bf16[8,256,128]{2,1,0:T(8,128)(2,1)} %copy-done), calls=%async_computation.2 | async-start | bytes 1048576 | tf_op jit(solution)/shard_map/all_to_all | solution.py:269
  81.1 7.2 %all-to-all-done.2.att_ref = bf16[8,256,128]{2,1,0:T(8,128)(2,1)S(1)} async-done(((bf16[8,256,128]{2,1,0:T(8,128)(2,1)}), bf16[8,256,128]{2,1,0:T(8,128)(2,1)S(1)}, u32[]{:S(2)}, u32[]{:S(2)}) %all-to-all-start.2) | async-done | bytes 524320 | tf_op jit(solution)/shard_map/all_to_all | solution.py:269
  88.4 0.8 copy-done.6
  89.2 8.9 %finish.1 = (bf16[256,1024]{1,0:T(8,128)(2,1)}, f32[8,128,1024]{2,1,0:T(8,128)}) custom-call(bf16[8,256,128]{2,1,0:T(8,128)(2,1)} %copy-done.6, bf16[256,1024]{1,0:T(8,128)(2,1)} %bitcast.55, bf16[1024,1024]{1,0:T(8,128)(2,1)} %w_ref.3), custom_call_target="tpu_custom_call" | custom-call | tf_op jit(solution)/shard_map/finish/pallas_call | solution.py:236
  98.1 2.4 %select_convert_fusion = bf16[4,1,128,1024]{3,2,0,1:T(8,128)(2,1)S(1)} fusion(f32[4,2,128,1024]{3,2,1,0:T(8,128)} %bitcast.48, pred[]{:T(512)S(6)} %eq.31), kind=kLoop, calls=%fused_computation.3 | loop fusion | flops 524288 | bytes 3145729 | tf_op jit(solution)/shard_map/convert_element_type | solution.py:263
  100.5 0.1 collective-permute-start.4
  100.6 2.8 %collective-permute-done.4 = bf16[4,1,128,1024]{3,2,0,1:T(8,128)(2,1)} collective-permute-done((bf16[4,1,128,1024]{3,2,0,1:T(8,128)(2,1)S(1)}, bf16[4,1,128,1024]{3,2,0,1:T(8,128)(2,1)}, u32[]{:S(2)}, u32[]{:S(2)}) %collective-permute-start.4) | collective-permute-done | bytes 1048608 | tf_op jit(solution)/shard_map/ppermute | solution.py:264
  103.4 3.1 %convert_add_fusion = f32[4,1,128,1024]{3,2,0,1:T(8,128)S(1)} fusion(bf16[4,1,128,1024]{3,2,0,1:T(8,128)(2,1)} %collective-permute-done.4, f32[4,2,128,1024]{3,2,1,0:T(8,128)} %bitcast.49, pred[]{:T(512)S(6)} %eq.31), kind=kLoop, calls=%fused_computation.2 | loop fusion | flops 1572864 | bytes 7340033 | tf_op jit(solution)/shard_map/add | solution.py:265
  106.5 0.9 fusion
  107.4 4.5 %collective-permute-start.5 = (bf16[2,128,1024]{2,1,0:T(8,128)(2,1)}, bf16[2,128,1024]{2,1,0:T(8,128)(2,1)}, u32[]{:S(2)}, u32[]{:S(2)}) collective-permute-start(bf16[2,128,1024]{2,1,0:T(8,128)(2,1)} %fusion), channel_id=1, source_target_pairs={{0,128},{64,192},{128,0},{192,64},{1,129},{65,193},{129,1},{193,65... | collective-permute-start | bytes 1572872 | tf_op jit(solution)/shard_map/ppermute | solution.py:264
  111.9 23.8 %collective-permute-done.5 = bf16[2,128,1024]{2,1,0:T(8,128)(2,1)} collective-permute-done((bf16[2,128,1024]{2,1,0:T(8,128)(2,1)}, bf16[2,128,1024]{2,1,0:T(8,128)(2,1)}, u32[]{:S(2)}, u32[]{:S(2)}) %collective-permute-start.5) | collective-permute-done | bytes 524320 | tf_op jit(solution)/shard_map/ppermute | solution.py:264
  135.7 1.3 bitcast_add_fusion
  137.0 1.0 copy-done.5
  138.0 0.1 collective-permute-start.6
  138.1 7.8 %collective-permute-done.6 = bf16[1,128,1024]{2,1,0:T(8,128)(2,1)S(1)} collective-permute-done((bf16[1,128,1024]{2,1,0:T(8,128)(2,1)S(1)}, bf16[1,128,1024]{2,1,0:T(8,128)(2,1)S(1)}, u32[]{:S(2)}, u32[]{:S(2)}) %collective-permute-start.6) | collective-permute-done | bytes 262176 | tf_op jit(solution)/shard_map/ppermute | solution.py:264
  145.9 1.3 convert_add_fusion.1
  147.3 0.1 collective-permute-start.7
  147.4 4.5 %all-to-all-start.3 = ((bf16[8,256,128]{2,1,0:T(8,128)(2,1)}), bf16[8,256,128]{2,1,0:T(8,128)(2,1)S(1)}, u32[]{:S(2)}, u32[]{:S(2)}) async-start(bf16[8,256,128]{2,1,0:T(8,128)(2,1)} %get-tuple-element.14), calls=%async_computation.3 | async-start | bytes 1048576 | tf_op jit(solution)/shard_map/all_to_all | solution.py:269
  151.8 4.9 %collective-permute-start.2 = (bf16[512,128]{1,0:T(8,128)(2,1)S(1)}, bf16[512,128]{1,0:T(8,128)(2,1)S(1)}, u32[]{:S(2)}, u32[]{:S(2)}) collective-permute-start(bf16[512,128]{1,0:T(8,128)(2,1)S(1)} %get-tuple-element.16), channel_id=1, source_target_pairs={{0,8},{8,16},{16,24},{1,9},{9,17},{17,25},{2,10},{10,18},{18,26},{... | collective-permute-start | bytes 393224 | tf_op jit(solution)/shard_map/ppermute | solution.py:296
  156.8 2.4 %collective-permute-start.3 = (bf16[512,128]{1,0:T(8,128)(2,1)S(1)}, bf16[512,128]{1,0:T(8,128)(2,1)S(1)}, u32[]{:S(2)}, u32[]{:S(2)}) collective-permute-start(bf16[512,128]{1,0:T(8,128)(2,1)S(1)} %get-tuple-element.17), channel_id=1, source_target_pairs={{8,0},{16,8},{24,16},{9,1},{17,9},{25,17},{10,2},{18,10},{26,18},{... | collective-permute-start | bytes 393224 | tf_op jit(solution)/shard_map/ppermute | solution.py:295
  159.2 0.1 slice.91
  159.3 0.0 collective-permute-done.7
  159.3 0.1 collective-permute-start.8
  159.4 4.2 %collective-permute-done.2 = bf16[512,128]{1,0:T(8,128)(2,1)S(1)} collective-permute-done((bf16[512,128]{1,0:T(8,128)(2,1)S(1)}, bf16[512,128]{1,0:T(8,128)(2,1)S(1)}, u32[]{:S(2)}, u32[]{:S(2)}) %collective-permute-start.2) | collective-permute-done | bytes 131104 | tf_op jit(solution)/shard_map/ppermute | solution.py:296
  163.7 6.4 %collective-permute-done.3 = bf16[512,128]{1,0:T(8,128)(2,1)S(1)} collective-permute-done((bf16[512,128]{1,0:T(8,128)(2,1)S(1)}, bf16[512,128]{1,0:T(8,128)(2,1)S(1)}, u32[]{:S(2)}, u32[]{:S(2)}) %collective-permute-start.3) | collective-permute-done | bytes 131104 | tf_op jit(solution)/shard_map/ppermute | solution.py:295
  170.1 0.1 fusion.2
  170.2 0.0 collective-permute-done.8
  170.2 0.1 collective-permute-start.9
  170.3 1.1 pad_maximum_fusion
  171.5 6.2 %all-to-all-start.4 = ((bf16[8,512,128]{2,1,0:T(8,128)(2,1)}), bf16[8,512,128]{2,1,0:T(8,128)(2,1)S(1)}, u32[]{:S(2)}, u32[]{:S(2)}) async-start(bf16[8,512,128]{2,1,0:T(8,128)(2,1)} %pad_maximum_fusion), calls=%async_computation.4 | async-start | bytes 2097152 | tf_op jit(solution)/shard_map/all_to_all | solution.py:269
  177.7 0.0 collective-permute-done.9
  177.7 3.1 %collective-permute-start.10 = (bf16[8,1024]{1,0:T(8,128)(2,1)S(1)}, bf16[8,1024]{1,0:T(8,128)(2,1)S(1)}, u32[]{:S(2)}, u32[]{:S(2)}) collective-permute-start(bf16[8,1024]{1,0:T(8,128)(2,1)S(1)} %select_convert_fusion.6), channel_id=1, source_target_pairs={{0,2},{1,3},{2,0},{3,1},{4,6},{5,7},{6,4},{7,5},{8,10},{9,11},{10,... | collective-permute-start | bytes 49160 | tf_op jit(solution)/shard_map/ppermute | solution.py:264
  180.8 0.2 copy.14
  181.0 1.0 copy.19
  182.0 7.4 %collective-permute-done.10 = bf16[8,1024]{1,0:T(8,128)(2,1)S(1)} collective-permute-done((bf16[8,1024]{1,0:T(8,128)(2,1)S(1)}, bf16[8,1024]{1,0:T(8,128)(2,1)S(1)}, u32[]{:S(2)}, u32[]{:S(2)}) %collective-permute-start.10) | collective-permute-done | bytes 16416 | tf_op jit(solution)/shard_map/ppermute | solution.py:264
  189.5 0.6 collective-permute-start.11
  190.1 0.0 all-to-all-done.4
  190.1 0.1 slice_bitcast_fusion.2
  190.2 0.2 copy.15
  190.4 1.0 copy.20
  191.4 0.2 copy.16
  191.6 1.0 copy.21
  192.6 0.6 collective-permute-done.11
  193.2 0.6 add_multiply_fusion
  (23 shorter events, 0.3 us)
Async XLA Ops:
  7.0 20.9 %all-to-all-start = ((bf16[8,544,128]{2,1,0:T(8,128)(2,1)}), bf16[8,544,128]{2,1,0:T(8,128)(2,1)S(1)}, u32[]{:S(2)}, u32[]{:S(2)}) async-start(bf16[8,544,128]{2,1,0:T(8,128)(2,1)} %pack_kv.1), calls=%async_computation | async-start | bytes 2228224 | tf_op jit(solution)/shard_map/all_to_all | solution.py:269
  19.8 24.2 %copy-start.7 = (s32[8192]{0:T(1024)S(1)}, s32[8192]{0:T(1024)}, u32[]{:S(2)}) copy-start(s32[8192]{0:T(1024)} %param.13) | copy-start | bytes 98308
  27.9 18.6 %all-to-all-start.1 = ((bf16[8,512,128]{2,1,0:T(8,128)(2,1)}), bf16[8,512,128]{2,1,0:T(8,128)(2,1)S(1)}, u32[]{:S(2)}, u32[]{:S(2)}) async-start(bf16[8,512,128]{2,1,0:T(8,128)(2,1)} %pack_qg.1), calls=%async_computation.1 | async-start | bytes 2097152 | tf_op jit(solution)/shard_map/all_to_all | solution.py:269
  32.1 16.0 %collective-permute-start = (bf16[512,128]{1,0:T(8,128)(2,1)S(1)}, bf16[512,128]{1,0:T(8,128)(2,1)S(1)}, u32[]{:S(2)}, u32[]{:S(2)}) collective-permute-start(bf16[512,128]{1,0:T(8,128)(2,1)S(1)} %get-tuple-element.25), channel_id=1, source_target_pairs={{0,8},{8,16},{16,24},{1,9},{9,17},{17,25},{2,10},{10,18},{18,26},{... | collective-permute-start | bytes 393224 | tf_op jit(solution)/shard_map/ppermute | solution.py:284
  42.1 13.2 %collective-permute-start.1 = (bf16[512,128]{1,0:T(8,128)(2,1)S(1)}, bf16[512,128]{1,0:T(8,128)(2,1)S(1)}, u32[]{:S(2)}, u32[]{:S(2)}) collective-permute-start(bf16[512,128]{1,0:T(8,128)(2,1)S(1)} %get-tuple-element.24), channel_id=1, source_target_pairs={{8,0},{16,8},{24,16},{9,1},{17,9},{25,17},{10,2},{18,10},{26,18},{... | collective-permute-start | bytes 393224 | tf_op jit(solution)/shard_map/ppermute | solution.py:285
  48.1 7.5 %copy-start.1 = (bf16[512,128]{1,0:T(8,128)(2,1)}, bf16[512,128]{1,0:T(8,128)(2,1)S(1)}, u32[]{:S(2)}) copy-start(bf16[512,128]{1,0:T(8,128)(2,1)S(1)} %collective-permute-done.left_ref) | copy-start | bytes 393220
  55.2 0.7 copy-start.3
  55.9 0.9 copy-start.2
  56.8 0.9 copy-start.4
  74.7 0.8 copy-start
  75.4 12.9 %all-to-all-start.2 = ((bf16[8,256,128]{2,1,0:T(8,128)(2,1)}), bf16[8,256,128]{2,1,0:T(8,128)(2,1)S(1)}, u32[]{:S(2)}, u32[]{:S(2)}) async-start(bf16[8,256,128]{2,1,0:T(8,128)(2,1)} %copy-done), calls=%async_computation.2 | async-start | bytes 1048576 | tf_op jit(solution)/shard_map/all_to_all | solution.py:269
  88.4 0.8 copy-start.6
  100.5 2.9 %collective-permute-start.4 = (bf16[4,1,128,1024]{3,2,0,1:T(8,128)(2,1)S(1)}, bf16[4,1,128,1024]{3,2,0,1:T(8,128)(2,1)}, u32[]{:S(2)}, u32[]{:S(2)}) collective-permute-start(bf16[4,1,128,1024]{3,2,0,1:T(8,128)(2,1)S(1)} %select_convert_fusion), channel_id=1, source_target_pairs={{0,32},{32,0},{1,33},{33,1},{2,34},{34,2},{3,35},{35,3},{4,36},{36... | collective-permute-start | bytes 3145736 | tf_op jit(solution)/shard_map/ppermute | solution.py:264
  107.4 28.3 %collective-permute-start.5 = (bf16[2,128,1024]{2,1,0:T(8,128)(2,1)}, bf16[2,128,1024]{2,1,0:T(8,128)(2,1)}, u32[]{:S(2)}, u32[]{:S(2)}) collective-permute-start(bf16[2,128,1024]{2,1,0:T(8,128)(2,1)} %fusion), channel_id=1, source_target_pairs={{0,128},{64,192},{128,0},{192,64},{1,129},{65,193},{129,1},{193,65... | collective-permute-start | bytes 1572872 | tf_op jit(solution)/shard_map/ppermute | solution.py:264
  137.0 1.0 copy-start.5
  138.0 7.9 %collective-permute-start.6 = (bf16[1,128,1024]{2,1,0:T(8,128)(2,1)S(1)}, bf16[1,128,1024]{2,1,0:T(8,128)(2,1)S(1)}, u32[]{:S(2)}, u32[]{:S(2)}) collective-permute-start(bf16[1,128,1024]{2,1,0:T(8,128)(2,1)S(1)} %select_convert_fusion.2), channel_id=1, source_target_pairs={{0,64},{64,0},{128,192},{192,128},{1,65},{65,1},{129,193},{193,129... | collective-permute-start | bytes 786440 | tf_op jit(solution)/shard_map/ppermute | solution.py:264
  147.3 12.0 %collective-permute-start.7 = (bf16[64,1024]{1,0:T(8,128)(2,1)S(1)}, bf16[64,1024]{1,0:T(8,128)(2,1)S(1)}, u32[]{:S(2)}, u32[]{:S(2)}) collective-permute-start(bf16[64,1024]{1,0:T(8,128)(2,1)S(1)} %fusion.3), channel_id=1, source_target_pairs={{0,16},{16,0},{1,17},{17,1},{2,18},{18,2},{3,19},{19,3},{4,20},{20... | collective-permute-start | bytes 393224 | tf_op jit(solution)/shard_map/ppermute | solution.py:264
  147.4 24.1 %all-to-all-start.3 = ((bf16[8,256,128]{2,1,0:T(8,128)(2,1)}), bf16[8,256,128]{2,1,0:T(8,128)(2,1)S(1)}, u32[]{:S(2)}, u32[]{:S(2)}) async-start(bf16[8,256,128]{2,1,0:T(8,128)(2,1)} %get-tuple-element.14), calls=%async_computation.3 | async-start | bytes 1048576 | tf_op jit(solution)/shard_map/all_to_all | solution.py:269
  151.8 11.8 %collective-permute-start.2 = (bf16[512,128]{1,0:T(8,128)(2,1)S(1)}, bf16[512,128]{1,0:T(8,128)(2,1)S(1)}, u32[]{:S(2)}, u32[]{:S(2)}) collective-permute-start(bf16[512,128]{1,0:T(8,128)(2,1)S(1)} %get-tuple-element.16), channel_id=1, source_target_pairs={{0,8},{8,16},{16,24},{1,9},{9,17},{17,25},{2,10},{10,18},{18,26},{... | collective-permute-start | bytes 393224 | tf_op jit(solution)/shard_map/ppermute | solution.py:296
  156.8 13.4 %collective-permute-start.3 = (bf16[512,128]{1,0:T(8,128)(2,1)S(1)}, bf16[512,128]{1,0:T(8,128)(2,1)S(1)}, u32[]{:S(2)}, u32[]{:S(2)}) collective-permute-start(bf16[512,128]{1,0:T(8,128)(2,1)S(1)} %get-tuple-element.17), channel_id=1, source_target_pairs={{8,0},{16,8},{24,16},{9,1},{17,9},{25,17},{10,2},{18,10},{26,18},{... | collective-permute-start | bytes 393224 | tf_op jit(solution)/shard_map/ppermute | solution.py:295
  159.3 10.8 %collective-permute-start.8 = (bf16[32,1024]{1,0:T(8,128)(2,1)S(1)}, bf16[32,1024]{1,0:T(8,128)(2,1)S(1)}, u32[]{:S(2)}, u32[]{:S(2)}) collective-permute-start(bf16[32,1024]{1,0:T(8,128)(2,1)S(1)} %select_convert_fusion.4), channel_id=1, source_target_pairs={{0,8},{8,0},{1,9},{9,1},{2,10},{10,2},{3,11},{11,3},{4,12},{12,4},... | collective-permute-start | bytes 196616 | tf_op jit(solution)/shard_map/ppermute | solution.py:264
  170.2 7.5 %collective-permute-start.9 = (bf16[16,1024]{1,0:T(8,128)(2,1)S(1)}, bf16[16,1024]{1,0:T(8,128)(2,1)S(1)}, u32[]{:S(2)}, u32[]{:S(2)}) collective-permute-start(bf16[16,1024]{1,0:T(8,128)(2,1)S(1)} %select_convert_fusion.5), channel_id=1, source_target_pairs={{0,4},{4,0},{1,5},{5,1},{2,6},{6,2},{3,7},{7,3},{8,12},{12,8},{9,1... | collective-permute-start | bytes 98312 | tf_op jit(solution)/shard_map/ppermute | solution.py:264
  171.5 18.6 %all-to-all-start.4 = ((bf16[8,512,128]{2,1,0:T(8,128)(2,1)}), bf16[8,512,128]{2,1,0:T(8,128)(2,1)S(1)}, u32[]{:S(2)}, u32[]{:S(2)}) async-start(bf16[8,512,128]{2,1,0:T(8,128)(2,1)} %pad_maximum_fusion), calls=%async_computation.4 | async-start | bytes 2097152 | tf_op jit(solution)/shard_map/all_to_all | solution.py:269
  177.7 11.7 %collective-permute-start.10 = (bf16[8,1024]{1,0:T(8,128)(2,1)S(1)}, bf16[8,1024]{1,0:T(8,128)(2,1)S(1)}, u32[]{:S(2)}, u32[]{:S(2)}) collective-permute-start(bf16[8,1024]{1,0:T(8,128)(2,1)S(1)} %select_convert_fusion.6), channel_id=1, source_target_pairs={{0,2},{1,3},{2,0},{3,1},{4,6},{5,7},{6,4},{7,5},{8,10},{9,11},{10,... | collective-permute-start | bytes 49160 | tf_op jit(solution)/shard_map/ppermute | solution.py:264
  189.5 3.7 %collective-permute-start.11 = (bf16[4,1024]{1,0:T(4,128)(2,1)S(1)}, bf16[4,1024]{1,0:T(4,128)(2,1)S(1)}, u32[]{:S(2)}, u32[]{:S(2)}) collective-permute-start(bf16[4,1024]{1,0:T(4,128)(2,1)S(1)} %select_convert_fusion.7), channel_id=1, source_target_pairs={{0,1},{1,0},{2,3},{3,2},{4,5},{5,4},{6,7},{7,6},{8,9},{9,8},{10,11... | collective-permute-start | bytes 24584 | tf_op jit(solution)/shard_map/ppermute | solution.py:264

commit v2 on v1

v2 whole, which is shorter than its diff:
```python
import functools
import math

import jax
import jax.numpy as jnp
from jax import lax
from jax.experimental import pallas as pl
from jax.experimental.pallas import tpu as pltpu
from jax.sharding import Mesh, PartitionSpec as P

HEADS = 8
HALF_SPAN = 256
SHARDS = 8
ROWS = 256
HD = 128
PILS = 32
SLOT = ROWS // PILS
FRAME_ROWS = SHARDS * ROWS
BLOCKS = SHARDS + 2
KV_ROWS = 2 * ROWS + PILS
BF = jnp.bfloat16
F32 = jnp.float32

FRAME = ("xl", "y")
FRAMES = ("zh", "xh")
SCALE = 1.0 / math.sqrt(HD)
LOG2E = math.log2(math.e)


def mm(a, b, ca, cb):
    return lax.dot_general(a, b, (((ca,), (cb,)), ((), ())), preferred_element_type=F32)


def pack_kv_kernel(k_ref, v_ref, s_ref, o_ref):
    for n in range(o_ref.shape[0]):
        columns = slice(n * HD, (n + 1) * HD)
        o_ref[n, :ROWS] = k_ref[:, columns]
        o_ref[n, ROWS : 2 * ROWS] = v_ref[:, columns]
        o_ref[n, 2 * ROWS :] = s_ref[...]


def pack_kv(k, v, shift_cols):
    some = 4
    return pl.pallas_call(
        pack_kv_kernel,
        grid=(HEADS // some,),
        in_specs=[
            pl.BlockSpec((ROWS, some * HD), lambda h: (0, h)),
            pl.BlockSpec((ROWS, some * HD), lambda h: (0, h)),
            pl.BlockSpec((PILS, HD), lambda h: (0, 0)),
        ],
        out_specs=pl.BlockSpec((some, KV_ROWS, HD), lambda h: (h, 0, 0)),
        out_shape=jax.ShapeDtypeStruct((HEADS, KV_ROWS, HD), BF),
        name="pack_kv",
    )(k, v, shift_cols)


def pack_qg_kernel(q_ref, g_ref, w_ref, o_ref):
    grad = mm(g_ref[...], w_ref[...], 1, 1).astype(BF)
    for n in range(o_ref.shape[0]):
        columns = slice(n * HD, (n + 1) * HD)
        o_ref[n, :ROWS] = q_ref[:, columns]
        o_ref[n, ROWS:] = grad[:, columns]


def pack_qg(q, g, w):
    width = g.shape[1]
    some = 2
    return pl.pallas_call(
        pack_qg_kernel,
        grid=(HEADS // some,),
        in_specs=[
            pl.BlockSpec((ROWS, some * HD), lambda h: (0, h)),
            pl.BlockSpec((ROWS, width), lambda h: (0, 0)),
            pl.BlockSpec((some * HD, width), lambda h: (h, 0)),
        ],
        out_specs=pl.BlockSpec((some, 2 * ROWS, HD), lambda h: (h, 0, 0)),
        out_shape=jax.ShapeDtypeStruct((HEADS, 2 * ROWS, HD), BF),
        cost_estimate=pl.CostEstimate(
            flops=2 * ROWS * width * width, bytes_accessed=5 << 20, transcendentals=0
        ),
        name="pack_qg",
    )(q, g, w)


def pilot_pick(shift):
    where_to = lax.broadcasted_iota(jnp.int32, (PILS, HD), 0) * SLOT + shift.astype(F32).astype(jnp.int32)
    lane = lax.broadcasted_iota(jnp.int32, (PILS, HD), 1)
    picks = [jnp.where(lane + part * HD == where_to, 1.0, 0.0) for part in range(ROWS // HD)]
    return jnp.concatenate(picks, axis=1).astype(BF)


def window_scores(i, q, k_all, k_pil, labk_ref, labq_ref):
    label_q = labq_ref[i]
    key_at = lax.broadcasted_iota(jnp.int32, (ROWS, ROWS), 0)
    query_at = lax.broadcasted_iota(jnp.int32, (ROWS, ROWS), 1)
    scores = []
    for part in range(3):
        admit = labk_ref[i + part][:, :1] == label_q
        if part == 0:
            admit = admit & (key_at >= query_at)
        elif part == 2:
            admit = admit & (key_at <= query_at)
        scores.append(jnp.where(admit, mm(k_all[i + part], q, 1, 1), -jnp.inf))
    return scores + [mm(k_pil[...], q, 1, 1)]


def block_of(b, kv_ref, left_ref, right_ref):
    if b == 0:
        return left_ref[:ROWS], left_ref[ROWS:]
    if b == BLOCKS - 1:
        return right_ref[:ROWS], right_ref[ROWS:]
    return kv_ref[b - 1, :ROWS], kv_ref[b - 1, ROWS : 2 * ROWS]


def forward_kernel(
    kv_ref, qg_ref, left_ref, right_ref, labk_ref, labq_ref,
    att_ref, stat_ref, k_pil, v_pil,
    k_all, vt_all, vt_pil,
):
    i = pl.program_id(0)

    @pl.when(i == 0)
    def _():
        for b in range(BLOCKS):
            kb, vb = block_of(b, kv_ref, left_ref, right_ref)
            k_all[b] = kb
            vt_all[b] = vb.T
            if 0 < b < BLOCKS - 1:
                pick = pilot_pick(kv_ref[b - 1, 2 * ROWS :])
                at = slice((b - 1) * PILS, b * PILS)
                k_pil[at] = mm(pick, kb, 1, 0).astype(BF)
                v_pil[at] = mm(pick, vb, 1, 0).astype(BF)
        vt_pil[...] = v_pil[...].T

    scores = window_scores(i, qg_ref[i, :ROWS], k_all, k_pil, labk_ref, labq_ref)
    factor = SCALE * LOG2E
    top = functools.reduce(jnp.maximum, [jnp.max(s, axis=0, keepdims=True) for s in scores])
    top = top * factor
    exps = [jnp.exp2(s * factor - top) for s in scores]
    inverse = 1.0 / functools.reduce(jnp.add, [jnp.sum(e, axis=0, keepdims=True) for e in exps])
    stat_ref[i] = jnp.concatenate([top, inverse], axis=0)
    vts = [vt_all[i + part] for part in range(3)] + [vt_pil[...]]
    att_t = functools.reduce(
        jnp.add, [mm(vt, (e * inverse).astype(BF), 1, 0) for vt, e in zip(vts, exps)]
    )
    att_ref[i] = att_t.T.astype(BF)


def backward_kernel(
    kv_ref, qg_ref, left_ref, right_ref, labk_ref, labq_ref, att_ref, stat_ref, k_pil, v_pil,
    dq_ref, dkv_ref, dleft_ref, dright_ref,
    k_all, v_all, kt_all, kt_pil, dk_all, dv_all, dk_pil, dv_pil,
):
    i = pl.program_id(0)

    @pl.when(i == 0)
    def _():
        for b in range(BLOCKS):
            kb, vb = block_of(b, kv_ref, left_ref, right_ref)
            k_all[b] = kb
            v_all[b] = vb
            kt_all[b] = kb.T
        kt_pil[...] = k_pil[...].T
        dk_all[...] = jnp.zeros_like(dk_all)
        dv_all[...] = jnp.zeros_like(dv_all)
        dk_pil[...] = jnp.zeros_like(dk_pil)
        dv_pil[...] = jnp.zeros_like(dv_pil)

    q = qg_ref[i, :ROWS]
    ga = qg_ref[i, ROWS:]
    scores = window_scores(i, q, k_all, k_pil, labk_ref, labq_ref)
    top, inverse = stat_ref[i][:1], stat_ref[i][1:]
    product = ga.astype(F32) * att_ref[i].astype(F32)
    delta = jnp.sum(product.T, axis=0, keepdims=True)
    vals = [v_all[i + part] for part in range(3)] + [v_pil[...]]
    kts = [kt_all[i + part] for part in range(3)] + [kt_pil[...]]
    dq_t = jnp.zeros((HD, ROWS), F32)
    for part in range(4):
        prob = jnp.exp2(scores[part] * (SCALE * LOG2E) - top) * inverse
        dprob = mm(vals[part], ga, 1, 1)
        dscore = (prob * (dprob - delta)).astype(BF)
        dq_t = dq_t + mm(kts[part], dscore, 1, 0)
        dk = mm(dscore, q, 1, 0)
        dv = mm(prob.astype(BF), ga, 1, 0)
        if part < 3:
            dk_all[i + part] += dk
            dv_all[i + part] += dv
        else:
            dk_pil[...] += dk
            dv_pil[...] += dv
    dq_ref[i] = (dq_t * SCALE).T.astype(BF)

    @pl.when(i == SHARDS - 1)
    def _():
        for sh in range(SHARDS):
            pick = pilot_pick(kv_ref[sh, 2 * ROWS :])
            at = slice(sh * PILS, (sh + 1) * PILS)
            for which, (own, pil, by) in enumerate(((dk_all, dk_pil, SCALE), (dv_all, dv_pil, 1.0))):
                fine = pil[at]
                high = fine.astype(BF)
                low = (fine - high.astype(F32)).astype(BF)
                total = own[sh + 1] + (mm(pick, high, 0, 0) + mm(pick, low, 0, 0))
                dkv_ref[sh, which * ROWS : (which + 1) * ROWS] = (total * by).astype(BF)
        for ref, b in ((dleft_ref, 0), (dright_ref, BLOCKS - 1)):
            ref[:ROWS] = (dk_all[b] * SCALE).astype(BF)
            ref[ROWS:] = dv_all[b].astype(BF)


def whole(shape):
    return pl.BlockSpec(shape, lambda i: (0,) * len(shape))


def over_blocks(kernel, name, ins, outs, scratch, matmuls):
    return pl.pallas_call(
        kernel,
        grid=(SHARDS,),
        in_specs=[whole(a.shape) for a in ins],
        out_specs=[whole(o.shape) for o in outs],
        out_shape=outs,
        scratch_shapes=scratch,
        compiler_params=pltpu.CompilerParams(vmem_limit_bytes=48 * 1024 * 1024),
        cost_estimate=pl.CostEstimate(
            flops=matmuls * 2 * FRAME_ROWS * 4 * ROWS * HD,
            bytes_accessed=8 << 20,
            transcendentals=FRAME_ROWS * 4 * ROWS,
        ),
        name=name,
    )(*ins)


def like(*shape, dtype=BF):
    return jax.ShapeDtypeStruct(shape, dtype)


def forward(ins):
    outs = [like(SHARDS, ROWS, HD), like(SHARDS, 2, ROWS, dtype=F32)]
    outs += [like(SHARDS * PILS, HD)] * 2
    scratch = [
        pltpu.VMEM((BLOCKS, ROWS, HD), BF),
        pltpu.VMEM((BLOCKS, HD, ROWS), BF),
        pltpu.VMEM((HD, SHARDS * PILS), BF),
    ]
    return over_blocks(forward_kernel, "forward", ins, outs, scratch, 2)


def backward(ins):
    outs = [like(SHARDS, ROWS, HD), like(SHARDS, 2 * ROWS, HD)] + [like(2 * ROWS, HD)] * 2
    scratch = [
        pltpu.VMEM((BLOCKS, ROWS, HD), BF),
        pltpu.VMEM((BLOCKS, ROWS, HD), BF),
        pltpu.VMEM((BLOCKS, HD, ROWS), BF),
        pltpu.VMEM((HD, SHARDS * PILS), BF),
        pltpu.VMEM((BLOCKS, ROWS, HD), F32),
        pltpu.VMEM((BLOCKS, ROWS, HD), F32),
        pltpu.VMEM((SHARDS * PILS, HD), F32),
        pltpu.VMEM((SHARDS * PILS, HD), F32),
    ]
    return over_blocks(backward_kernel, "backward", ins, outs, scratch, 5)


def mix_kernel(att_ref, w_ref, mixed_ref):
    att = jnp.concatenate([att_ref[h] for h in range(HEADS)], axis=1)
    mixed_ref[...] = mm(att, w_ref[...], 1, 0).astype(BF)


def mix(att, w):
    width = w.shape[1]
    return pl.pallas_call(
        mix_kernel,
        grid=(4,),
        in_specs=[whole(att.shape), pl.BlockSpec((width, width // 4), lambda n: (0, n))],
        out_specs=pl.BlockSpec((ROWS, width // 4), lambda n: (0, n)),
        out_shape=like(ROWS, width),
        cost_estimate=pl.CostEstimate(
            flops=2 * ROWS * width * width, bytes_accessed=3 << 20, transcendentals=0
        ),
        name="mix",
    )(att, w)


def share_kernel(heads_ref, att_ref, g_ref, *refs):
    total = mm(att_ref[0], g_ref[...], 0, 0)
    if len(refs) == 2:
        total = total + refs[0][0].astype(F32)
    refs[-1][0] = total.astype(refs[-1].dtype)


def share_of(att, g, heads, got, dtype):
    width, count = g.shape[1], heads.shape[0]
    block = (1, HD, width)
    in_specs = [
        pl.BlockSpec((1, ROWS, HD), lambda n, heads: (heads[n], 0, 0)),
        pl.BlockSpec((ROWS, width), lambda n, heads: (0, 0)),
    ]
    ins = [heads, att, g]
    if got is not None:
        in_specs.append(pl.BlockSpec(block, lambda n, heads: (heads[n] // 2, 0, 0)))
        ins.append(got)
    return pl.pallas_call(
        share_kernel,
        grid_spec=pltpu.PrefetchScalarGridSpec(
            num_scalar_prefetch=1,
            grid=(count,),
            in_specs=in_specs,
            out_specs=pl.BlockSpec(block, lambda n, heads: (n, 0, 0)),
        ),
        out_shape=like(count, HD, width, dtype=dtype),
        cost_estimate=pl.CostEstimate(
            flops=2 * count * ROWS * HD * width, bytes_accessed=2 << 20, transcendentals=0
        ),
        name="share",
    )(*ins)


def halved(value, dim, axis, bit):
    count = lax.axis_size(axis)
    size = value.shape[dim] // 2
    upper = (lax.axis_index(axis) >> bit) & 1 == 1
    low = lax.slice_in_dim(value, 0, size, axis=dim)
    high = lax.slice_in_dim(value, size, 2 * size, axis=dim)
    out = jnp.where(upper, low, high).astype(BF)
    got = lax.ppermute(out, axis, [(j, j ^ (1 << bit)) for j in range(count)])
    return jnp.where(upper, high, low) + got.astype(F32)


def to_heads(x):
    return lax.all_to_all(x, FRAME, 0, 0, tiled=True)


def joined(x):
    return jnp.transpose(x, (1, 0, 2)).reshape(ROWS, HEADS * HD)


def on_device(askers, lookups, contents, cotangent, w, comb_shift, label):
    q, k, v, g = askers[0], lookups[0], contents[0], cotangent[0]
    frame = lax.axis_index(FRAMES)
    ups = [(j, j + 1) for j in range(lax.axis_size(FRAMES) - 1)]
    downs = [(j, i) for i, j in ups]

    shift_cols = jnp.broadcast_to(comb_shift[0].astype(BF)[:, None], (PILS, HD))
    kv = to_heads(pack_kv(k, v, shift_cols))
    left = lax.ppermute(kv[SHARDS - 1, : 2 * ROWS], FRAMES, ups)
    right = lax.ppermute(kv[0, : 2 * ROWS], FRAMES, downs)
    qg = to_heads(pack_qg(q, g, w))

    label = jnp.pad(label, (HALF_SPAN, HALF_SPAN), constant_values=-1)
    label = lax.dynamic_slice_in_dim(label, frame * FRAME_ROWS, BLOCKS * ROWS, 0)
    labk = jnp.broadcast_to(label.reshape(BLOCKS, ROWS, 1), (BLOCKS, ROWS, HD))
    labq = label[HALF_SPAN : HALF_SPAN + FRAME_ROWS].reshape(SHARDS, 1, ROWS)

    frame_ins = (kv, qg, left, right, labk, labq)
    att, stats, k_pil, v_pil = forward(frame_ins)
    att_rows = to_heads(att)
    dq, dkv, dleft, dright = backward(frame_ins + (att, stats, k_pil, v_pil))
    from_right = lax.ppermute(dleft, FRAMES, downs)
    from_left = lax.ppermute(dright, FRAMES, ups)

    core, z_bit = lax.axis_index("c"), lax.axis_index("zl") & 1
    head = jnp.arange(4, dtype=jnp.int32) * 2
    share = share_of(att_rows, g, head + (1 - core), None, BF)
    got = lax.ppermute(share, "c", [(0, 1), (1, 0)])
    mixed = mix(att_rows, w)
    mine = jnp.arange(2, dtype=jnp.int32) * 4 + core
    send = share_of(att_rows, g, mine + 2 * (1 - z_bit), got, BF)
    keep = share_of(att_rows, g, mine + 2 * z_bit, got, F32)
    got = lax.ppermute(send, "zl", [(j, j ^ 1) for j in range(4)])
    share = keep + got.astype(F32)

    dq = to_heads(dq)
    first = dkv[:1].astype(F32) + from_left.astype(F32)[None]
    last = dkv[SHARDS - 1 :].astype(F32) + from_right.astype(F32)[None]
    dkv = jnp.concatenate([first.astype(BF), dkv[1 : SHARDS - 1], last.astype(BF)], axis=0)
    share = halved(share, 0, "zl", 1)[0]
    share, dq = lax.optimization_barrier((share, dq))
    dkv = to_heads(dkv)

    width = share.shape[-1]
    share = halved(share.reshape(4, 2, 16, width), 1, "xl", 0)
    share = halved(share.reshape(2, 2, 16, width), 1, "xh", 0)
    share = halved(share.reshape(2, 16, width), 0, "zh", 0)
    share = share.reshape(16, width)
    share = halved(share, 0, "y", 1)
    share = halved(share, 0, "y", 0)
    weight_grad = share * (1.0 / math.sqrt(8 * 32 * ROWS))
    return (
        mixed[None],
        joined(dq)[None],
        joined(dkv[:, :ROWS])[None],
        joined(dkv[:, ROWS:])[None],
        weight_grad,
    )


def solution(mesh):
    fine = Mesh(mesh.devices.reshape(4, 2, 2, 2, 2, 4), ("zl", "c", "zh", "xh", "xl", "y"))
    dp, seq = ("zl", "c"), ("zh", "xh", "xl", "y")
    rows = P(dp, seq, None)
    return jax.shard_map(
        on_device,
        mesh=fine,
        in_specs=(rows, rows, rows, rows, P(), P(seq, None), P()),
        out_specs=(rows, rows, rows, rows, P(dp + seq, None)),
        check_vma=False,
    )
```

time: 195 us -> 179 us (0.918)
  the two profiles are of different devices: /device:TPU:6 before, /device:TPU:32 now
where the time goes in v2:
time: 179 us; the launch traced here: 177 us
  waiting for transfers between devices  58.6 us (33%)
  starting transfers between devices  57.9 us (32%)
  Pallas kernels  42.4 us (24%)
  other arithmetic  8.6 us (5%)
  local copies, waits for them, and re-layouts  8.6 us (5%)
    all_to_all x5, waiting for transfers between devices, to_heads(): return lax.all_to_all(x, FRAME, 0, 0, tiled=True)  36.4 us
    all_to_all x5, starting transfers between devices, to_heads(): return lax.all_to_all(x, FRAME, 0, 0, tiled=True)  21.1 us
    pallas_call x2, Pallas kernels, over_blocks(): pl.pallas_call(kernel, grid=(SHARDS,), in_specs=[whole(a.shape) for a in...  20.6 us
    ppermute x6, starting transfers between devices, halved(): got = lax.ppermute(out, axis, [(j, j ^ 1 << bit) for j in range(count)])  19.1 us
    pallas_call x3, Pallas kernels, share_of(): pl.pallas_call(share_kernel, grid_spec=pltpu.PrefetchScalarGridSpec(num_s...  10.9 us
    ppermute x1, waiting for transfers between devices, on_device(): got = lax.ppermute(send, 'zl', [(j, j ^ 1) for j in range(4)])  10.5 us
    ppermute x1, starting transfers between devices, on_device(): from_left = lax.ppermute(dright, FRAMES, ups)  10.5 us
    unnamed x31, local copies, waits for them, and re-layouts  6.56 us
  transfers between devices with their start and end apart: 17, of which 10 were waited for; matrix products, arithmetic and copies ran while one was open for 5% of the time, Pallas kernels for 14%

profile of v2, /device:TPU:32, one launch (start us, length us, event | category | flops | bytes accessed | tf_op | source)
XLA Modules:
  0.0 177.0 jit_solution(1649656693006845458)
XLA Ops:
  0.6 0.7 convert_bitcast_fusion
  1.3 0.7 broadcast_in_dim.28.s_ref
  2.0 2.1 %pack_kv.1 = bf16[8,544,128]{2,1,0:T(8,128)(2,1)} custom-call(bf16[256,1024]{1,0:T(8,128)(2,1)} %bitcast.52, bf16[256,1024]{1,0:T(8,128)(2,1)} %bitcast.53, bf16[32,128]{1,0:T(8,128)(2,1)} %broadcast_in_dim.28.s_ref), custom_call_target="tpu_custom_call" | custom-call | tf_op jit(solution)/shard_map/pack_kv/pallas_call | solution.py:44
  4.1 5.4 %all-to-all-start = ((bf16[8,544,128]{2,1,0:T(8,128)(2,1)}), bf16[8,544,128]{2,1,0:T(8,128)(2,1)S(1)}, u32[]{:S(2)}, u32[]{:S(2)}) async-start(bf16[8,544,128]{2,1,0:T(8,128)(2,1)} %pack_kv.1), calls=%async_computation | async-start | bytes 2228224 | tf_op jit(solution)/shard_map/all_to_all | solution.py:328
  9.5 4.6 %pack_qg.1 = bf16[8,512,128]{2,1,0:T(8,128)(2,1)} custom-call(bf16[256,1024]{1,0:T(8,128)(2,1)} %bitcast.55, bf16[256,1024]{1,0:T(8,128)(2,1)} %bitcast.40, bf16[1024,1024]{1,0:T(8,128)(2,1)} %w_ref.3), custom_call_target="tpu_custom_call" | custom-call | flops 536870912 | bytes 5242880 | tf_op jit(solution)/shard_map/pack_qg/pallas_call | solution.py:69
  14.1 10.9 %all-to-all-done.kv_ref = bf16[8,544,128]{2,1,0:T(8,128)(2,1)S(1)} async-done(((bf16[8,544,128]{2,1,0:T(8,128)(2,1)}), bf16[8,544,128]{2,1,0:T(8,128)(2,1)S(1)}, u32[]{:S(2)}, u32[]{:S(2)}) %all-to-all-start) | async-done | bytes 1114144 | tf_op jit(solution)/shard_map/all_to_all | solution.py:328
  25.0 3.6 %all-to-all-start.1 = ((bf16[8,512,128]{2,1,0:T(8,128)(2,1)}), bf16[8,512,128]{2,1,0:T(8,128)(2,1)S(1)}, u32[]{:S(2)}, u32[]{:S(2)}) async-start(bf16[8,512,128]{2,1,0:T(8,128)(2,1)} %pack_qg.1), calls=%async_computation.1 | async-start | bytes 2097152 | tf_op jit(solution)/shard_map/all_to_all | solution.py:328
  28.7 4.6 %collective-permute-start = (bf16[512,128]{1,0:T(8,128)(2,1)S(1)}, bf16[512,128]{1,0:T(8,128)(2,1)S(1)}, u32[]{:S(2)}, u32[]{:S(2)}) collective-permute-start(bf16[512,128]{1,0:T(8,128)(2,1)S(1)} %get-tuple-element.31), channel_id=1, source_target_pairs={{0,8},{8,16},{16,24},{1,9},{9,17},{17,25},{2,10},{10,18},{18,26},{... | collective-permute-start | bytes 393224 | tf_op jit(solution)/shard_map/ppermute | solution.py:343
  33.3 1.3 collective-permute-start.1
  34.6 0.1 pad_dynamic-slice_fusion.1
  34.7 0.1 pad_dynamic-slice_fusion
  34.8 8.9 %all-to-all-done.1.qg_ref = bf16[8,512,128]{2,1,0:T(8,128)(2,1)S(1)} async-done(((bf16[8,512,128]{2,1,0:T(8,128)(2,1)}), bf16[8,512,128]{2,1,0:T(8,128)(2,1)S(1)}, u32[]{:S(2)}, u32[]{:S(2)}) %all-to-all-start.1) | async-done | bytes 1048608 | tf_op jit(solution)/shard_map/all_to_all | solution.py:328
  43.7 0.0 collective-permute-done.left_ref
  43.7 2.5 %collective-permute-done.1.right_ref = bf16[512,128]{1,0:T(8,128)(2,1)S(1)} collective-permute-done((bf16[512,128]{1,0:T(8,128)(2,1)S(1)}, bf16[512,128]{1,0:T(8,128)(2,1)S(1)}, u32[]{:S(2)}, u32[]{:S(2)}) %collective-permute-start.1) | collective-permute-done | bytes 131104 | tf_op jit(solution)/shard_map/ppermute | solution.py:344
  46.3 0.4 broadcast_in_dim.30.labk_ref
  46.7 8.4 %forward.1 = (bf16[8,256,128]{2,1,0:T(8,128)(2,1)}, f32[8,2,256]{2,1,0:T(2,128)S(1)}, bf16[256,128]{1,0:T(8,128)(2,1)S(1)}, bf16[256,128]{1,0:T(8,128)(2,1)S(1)}) custom-call(bf16[8,544,128]{2,1,0:T(8,128)(2,1)S(1)} %all-to-all-done.kv_ref, bf16[8,512,128]{2,1,0:T(8,128)(2,1)S(1)} %all-to-all-done.1.qg_ref, ...), custom_call_target="tpu_custom_call" | custom-call | flops 1073741824 | bytes 8388608 | tf_op jit(solution)/shard_map/forward/pallas_call | solution.py:215
  55.0 0.6 copy-done.6
  55.7 4.9 %all-to-all-start.2 = ((bf16[8,256,128]{2,1,0:T(8,128)(2,1)}), bf16[8,256,128]{2,1,0:T(8,128)(2,1)S(1)}, u32[]{:S(2)}, u32[]{:S(2)}) async-start(bf16[8,256,128]{2,1,0:T(8,128)(2,1)} %get-tuple-element.15.att_ref), calls=%async_computation.2 | async-start | bytes 1048576 | tf_op jit(solution)/shard_map/all_to_all | solution.py:328
  60.5 0.5 multiply_add_fusion.heads_ref
  61.1 8.7 %all-to-all-done.2.att_ref = bf16[8,256,128]{2,1,0:T(8,128)(2,1)S(1)} async-done(((bf16[8,256,128]{2,1,0:T(8,128)(2,1)}), bf16[8,256,128]{2,1,0:T(8,128)(2,1)S(1)}, u32[]{:S(2)}, u32[]{:S(2)}) %all-to-all-start.2) | async-done | bytes 524320 | tf_op jit(solution)/shard_map/all_to_all | solution.py:328
  69.7 0.8 copy-done.10
  70.5 4.5 %share.3 = bf16[4,128,1024]{2,1,0:T(8,128)(2,1)} custom-call(s32[4]{0:T(128)} %multiply_add_fusion.heads_ref, bf16[8,256,128]{2,1,0:T(8,128)(2,1)} %copy-done.10, bf16[256,1024]{1,0:T(8,128)(2,1)} %bitcast.41), custom_call_target="tpu_custom_call" | custom-call | flops 268435456 | bytes 2097152 | tf_op jit(solution)/shard_map/share/pallas_call | solution.py:300
  75.0 0.5 fusion.4.heads_ref
  75.6 2.5 %collective-permute-done.2.refs_0_ = bf16[4,128,1024]{2,1,0:T(8,128)(2,1)} collective-permute-done((bf16[4,128,1024]{2,1,0:T(8,128)(2,1)}, bf16[4,128,1024]{2,1,0:T(8,128)(2,1)}, u32[]{:S(2)}, u32[]{:S(2)}) %collective-permute-start.2) | collective-permute-done | bytes 1048608 | tf_op jit(solution)/shard_map/ppermute | solution.py:362
  78.0 3.1 %share.5 = bf16[2,128,1024]{2,1,0:T(8,128)(2,1)} custom-call(s32[2]{0:T(128)} %fusion.4.heads_ref, bf16[8,256,128]{2,1,0:T(8,128)(2,1)} %copy-done.10, bf16[256,1024]{1,0:T(8,128)(2,1)} %bitcast.42, bf16[4,128,1024]{2,1,0:T(8,128)(2,1)} %collective-permute-done.2.refs_0_), custom_call_target="tpu_custom_call" | custom-call | flops 134217728 | bytes 2097152 | tf_op jit(solution)/shard_map/share/pallas_call | solution.py:300
  81.2 0.6 fusion.5.heads_ref
  81.7 3.2 %share.4 = f32[2,128,1024]{2,1,0:T(8,128)} custom-call(s32[2]{0:T(128)} %fusion.5.heads_ref, bf16[8,256,128]{2,1,0:T(8,128)(2,1)} %copy-done.10, bf16[256,1024]{1,0:T(8,128)(2,1)} %bitcast.43, bf16[4,128,1024]{2,1,0:T(8,128)(2,1)} %collective-permute-done.2.refs_0_), custom_call_target="tpu_custom_call" | custom-call | flops 134217728 | bytes 2097152 | tf_op jit(solution)/shard_map/share/pallas_call | solution.py:300
  85.0 10.5 %collective-permute-done.3 = bf16[2,128,1024]{2,1,0:T(8,128)(2,1)} collective-permute-done((bf16[2,128,1024]{2,1,0:T(8,128)(2,1)}, bf16[2,128,1024]{2,1,0:T(8,128)(2,1)}, u32[]{:S(2)}, u32[]{:S(2)}) %collective-permute-start.3) | collective-permute-done | bytes 524320 | tf_op jit(solution)/shard_map/ppermute | solution.py:367
  95.4 1.5 convert_add_fusion
  96.9 0.9 select_convert_fusion
  97.8 2.8 %collective-permute-start.4 = (bf16[1,128,1024]{2,1,0:T(8,128)(2,1)}, bf16[1,128,1024]{2,1,0:T(8,128)(2,1)}, u32[]{:S(2)}, u32[]{:S(2)}) collective-permute-start(bf16[1,128,1024]{2,1,0:T(8,128)(2,1)} %select_convert_fusion), channel_id=1, source_target_pairs={{0,128},{64,192},{128,0},{192,64},{1,129},{65,193},{129,1},{193,65... | collective-permute-start | bytes 786440 | tf_op jit(solution)/shard_map/ppermute | solution.py:323
  100.6 12.2 %backward.1 = (bf16[8,256,128]{2,1,0:T(8,128)(2,1)S(1)}, bf16[8,512,128]{2,1,0:T(8,128)(2,1)S(1)}, bf16[512,128]{1,0:T(8,128)(2,1)S(1)}, bf16[512,128]{1,0:T(8,128)(2,1)S(1)}) custom-call(bf16[8,544,128]{2,1,0:T(8,128)(2,1)S(1)} %all-to-all-done.kv_ref, bf16[8,512,128]{2,1,0:T(8,128)(2,1)S(1)} %all-to-all-done.1.qg_ref, ...), custom_call_target="tpu_custom_call" | custom-call | flops 2684354560 | bytes 8388608 | tf_op jit(solution)/shard_map/backward/pallas_call | solution.py:215
  112.9 0.0 copy-start.1
  112.9 0.8 copy-done.1
  113.7 0.7 copy-done.2
  114.3 0.7 copy-done.4
  115.0 3.6 %all-to-all-start.3 = ((bf16[8,256,128]{2,1,0:T(8,128)(2,1)}), bf16[8,256,128]{2,1,0:T(8,128)(2,1)S(1)}, u32[]{:S(2)}, u32[]{:S(2)}) async-start(bf16[8,256,128]{2,1,0:T(8,128)(2,1)} %copy-done.1), calls=%async_computation.3 | async-start | bytes 1048576 | tf_op jit(solution)/shard_map/all_to_all | solution.py:328
  118.6 0.0 copy-start.5
  118.7 1.1 add_bitcast_fusion
  119.8 7.9 %all-to-all-done.3 = bf16[8,256,128]{2,1,0:T(8,128)(2,1)S(1)} async-done(((bf16[8,256,128]{2,1,0:T(8,128)(2,1)}), bf16[8,256,128]{2,1,0:T(8,128)(2,1)S(1)}, u32[]{:S(2)}, u32[]{:S(2)}) %all-to-all-start.3) | async-done | bytes 524320 | tf_op jit(solution)/shard_map/all_to_all | solution.py:328
  127.7 1.1 collective-permute-start.7
  128.8 10.5 %collective-permute-start.5 = (bf16[512,128]{1,0:T(8,128)(2,1)S(1)}, bf16[512,128]{1,0:T(8,128)(2,1)S(1)}, u32[]{:S(2)}, u32[]{:S(2)}) collective-permute-start(bf16[512,128]{1,0:T(8,128)(2,1)S(1)} %copy-done.5), channel_id=1, source_target_pairs={{0,8},{8,16},{16,24},{1,9},{9,17},{17,25},{2,10},{10,18},{18,26},{... | collective-permute-start | bytes 393224 | tf_op jit(solution)/shard_map/ppermute | solution.py:357
  139.3 1.3 collective-permute-start.6
  140.6 0.1 slice.81
  140.6 0.9 convert_add_fusion.3
  141.6 4.2 %collective-permute-start.8 = (bf16[2,1,16,1024]{3,2,1,0:T(8,128)(2,1)S(1)}, bf16[2,1,16,1024]{3,2,1,0:T(8,128)(2,1)S(1)}, u32[]{:S(2)}, u32[]{:S(2)}) collective-permute-start(bf16[2,1,16,1024]{3,2,1,0:T(8,128)(2,1)S(1)} %select_convert_fusion.2), channel_id=1, source_target_pairs={{0,8},{8,0},{1,9},{9,1},{2,10},{10,2},{3,11},{11,3},{4,12},{12,4},... | collective-permute-start | bytes 196616 | tf_op jit(solution)/shard_map/ppermute | solution.py:323
  145.8 1.8 %collective-permute-done.6 = bf16[512,128]{1,0:T(8,128)(2,1)S(1)} collective-permute-done((bf16[512,128]{1,0:T(8,128)(2,1)S(1)}, bf16[512,128]{1,0:T(8,128)(2,1)S(1)}, u32[]{:S(2)}, u32[]{:S(2)}) %collective-permute-start.6) | collective-permute-done | bytes 131104 | tf_op jit(solution)/shard_map/ppermute | solution.py:356
  147.6 0.1 fusion.1
  147.7 0.6 collective-permute-done.8
  148.4 6.9 %collective-permute-start.9 = (bf16[1,16,1024]{2,1,0:T(8,128)(2,1)S(1)}, bf16[1,16,1024]{2,1,0:T(8,128)(2,1)S(1)}, u32[]{:S(2)}, u32[]{:S(2)}) collective-permute-start(bf16[1,16,1024]{2,1,0:T(8,128)(2,1)S(1)} %fusion.2), channel_id=1, source_target_pairs={{0,16},{16,0},{1,17},{17,1},{2,18},{18,2},{3,19},{19,3},{4,20},{20... | collective-permute-start | bytes 98312 | tf_op jit(solution)/shard_map/ppermute | solution.py:323
  155.3 1.1 pad_maximum_fusion
  156.4 3.6 %all-to-all-start.4 = ((bf16[8,512,128]{2,1,0:T(8,128)(2,1)}), bf16[8,512,128]{2,1,0:T(8,128)(2,1)S(1)}, u32[]{:S(2)}, u32[]{:S(2)}) async-start(bf16[8,512,128]{2,1,0:T(8,128)(2,1)} %pad_maximum_fusion), calls=%async_computation.4 | async-start | bytes 2097152 | tf_op jit(solution)/shard_map/all_to_all | solution.py:328
  160.0 3.5 %collective-permute-start.10 = (bf16[8,1024]{1,0:T(8,128)(2,1)S(1)}, bf16[8,1024]{1,0:T(8,128)(2,1)S(1)}, u32[]{:S(2)}, u32[]{:S(2)}) collective-permute-start(bf16[8,1024]{1,0:T(8,128)(2,1)S(1)} %fusion.3), channel_id=1, source_target_pairs={{0,2},{1,3},{2,0},{3,1},{4,6},{5,7},{6,4},{7,5},{8,10},{9,11},{10,... | collective-permute-start | bytes 49160 | tf_op jit(solution)/shard_map/ppermute | solution.py:323
  163.5 4.2 %mix.1 = bf16[256,1024]{1,0:T(8,128)(2,1)} custom-call(bf16[8,256,128]{2,1,0:T(8,128)(2,1)} %copy-done.10, bf16[1024,1024]{1,0:T(8,128)(2,1)} %w_ref.3), custom_call_target="tpu_custom_call" | custom-call | flops 536870912 | bytes 3145728 | tf_op jit(solution)/shard_map/mix/pallas_call | solution.py:269
  167.7 4.2 %collective-permute-done.10 = bf16[8,1024]{1,0:T(8,128)(2,1)S(1)} collective-permute-done((bf16[8,1024]{1,0:T(8,128)(2,1)S(1)}, bf16[8,1024]{1,0:T(8,128)(2,1)S(1)}, u32[]{:S(2)}, u32[]{:S(2)}) %collective-permute-start.10) | collective-permute-done | bytes 16416 | tf_op jit(solution)/shard_map/ppermute | solution.py:323
  172.0 0.6 collective-permute-start.11
  172.6 0.1 slice_bitcast_fusion
  172.7 0.2 copy.13
  172.9 1.0 copy.16
  173.9 0.2 copy.14
  174.1 1.0 copy.17
  175.1 0.2 copy.12
  175.3 1.0 copy.15
  176.3 0.6 add_multiply_fusion
  (39 shorter events, 0.2 us)
Async XLA Ops:
  4.1 20.9 %all-to-all-start = ((bf16[8,544,128]{2,1,0:T(8,128)(2,1)}), bf16[8,544,128]{2,1,0:T(8,128)(2,1)S(1)}, u32[]{:S(2)}, u32[]{:S(2)}) async-start(bf16[8,544,128]{2,1,0:T(8,128)(2,1)} %pack_kv.1), calls=%async_computation | async-start | bytes 2228224 | tf_op jit(solution)/shard_map/all_to_all | solution.py:328
  14.1 20.6 %copy-start.13 = (s32[8192]{0:T(1024)S(1)}, s32[8192]{0:T(1024)}, u32[]{:S(2)}) copy-start(s32[8192]{0:T(1024)} %param.13) | copy-start | bytes 98308
  25.0 18.7 %all-to-all-start.1 = ((bf16[8,512,128]{2,1,0:T(8,128)(2,1)}), bf16[8,512,128]{2,1,0:T(8,128)(2,1)S(1)}, u32[]{:S(2)}, u32[]{:S(2)}) async-start(bf16[8,512,128]{2,1,0:T(8,128)(2,1)} %pack_qg.1), calls=%async_computation.1 | async-start | bytes 2097152 | tf_op jit(solution)/shard_map/all_to_all | solution.py:328
  28.7 15.1 %collective-permute-start = (bf16[512,128]{1,0:T(8,128)(2,1)S(1)}, bf16[512,128]{1,0:T(8,128)(2,1)S(1)}, u32[]{:S(2)}, u32[]{:S(2)}) collective-permute-start(bf16[512,128]{1,0:T(8,128)(2,1)S(1)} %get-tuple-element.31), channel_id=1, source_target_pairs={{0,8},{8,16},{16,24},{1,9},{9,17},{17,25},{2,10},{10,18},{18,26},{... | collective-permute-start | bytes 393224 | tf_op jit(solution)/shard_map/ppermute | solution.py:343
  33.3 12.9 %collective-permute-start.1 = (bf16[512,128]{1,0:T(8,128)(2,1)S(1)}, bf16[512,128]{1,0:T(8,128)(2,1)S(1)}, u32[]{:S(2)}, u32[]{:S(2)}) collective-permute-start(bf16[512,128]{1,0:T(8,128)(2,1)S(1)} %get-tuple-element.30), channel_id=1, source_target_pairs={{8,0},{16,8},{24,16},{9,1},{17,9},{25,17},{10,2},{18,10},{26,18},{... | collective-permute-start | bytes 393224 | tf_op jit(solution)/shard_map/ppermute | solution.py:344
  46.7 8.4 %copy-start = (s32[10,256,128]{2,1,0:T(8,128)}, s32[10,256,128]{2,1,0:T(8,128)S(1)}, u32[]{:S(2)}) copy-start(s32[10,256,128]{2,1,0:T(8,128)S(1)} %broadcast_in_dim.30.labk_ref) | copy-start | bytes 3932164
  55.0 0.6 copy-start.6
  55.7 19.3 %copy-start.8 = (f32[8,2,256]{2,1,0:T(2,128)}, f32[8,2,256]{2,1,0:T(2,128)S(1)}, u32[]{:S(2)}) copy-start(f32[8,2,256]{2,1,0:T(2,128)S(1)} %get-tuple-element.16.stat_ref) | copy-start | bytes 49156
  55.7 14.0 %all-to-all-start.2 = ((bf16[8,256,128]{2,1,0:T(8,128)(2,1)}), bf16[8,256,128]{2,1,0:T(8,128)(2,1)S(1)}, u32[]{:S(2)}, u32[]{:S(2)}) async-start(bf16[8,256,128]{2,1,0:T(8,128)(2,1)} %get-tuple-element.15.att_ref), calls=%async_computation.2 | async-start | bytes 1048576 | tf_op jit(solution)/shard_map/all_to_all | solution.py:328
  69.7 0.8 copy-start.10
  75.0 3.0 %collective-permute-start.2 = (bf16[4,128,1024]{2,1,0:T(8,128)(2,1)}, bf16[4,128,1024]{2,1,0:T(8,128)(2,1)}, u32[]{:S(2)}, u32[]{:S(2)}) collective-permute-start(bf16[4,128,1024]{2,1,0:T(8,128)(2,1)} %share.3), channel_id=1, source_target_pairs={{0,32},{32,0},{1,33},{33,1},{2,34},{34,2},{3,35},{35,3},{4,36},{36... | collective-permute-start | bytes 3145736 | tf_op jit(solution)/shard_map/ppermute | solution.py:362
  81.2 14.3 %collective-permute-start.3 = (bf16[2,128,1024]{2,1,0:T(8,128)(2,1)}, bf16[2,128,1024]{2,1,0:T(8,128)(2,1)}, u32[]{:S(2)}, u32[]{:S(2)}) collective-permute-start(bf16[2,128,1024]{2,1,0:T(8,128)(2,1)} %share.5), channel_id=1, source_target_pairs={{0,64},{64,0},{128,192},{192,128},{1,65},{65,1},{129,193},{193,129... | collective-permute-start | bytes 1572872 | tf_op jit(solution)/shard_map/ppermute | solution.py:367
  85.0 15.7 %copy-start.7 = (bf16[256,128]{1,0:T(8,128)(2,1)S(1)}, bf16[256,128]{1,0:T(8,128)(2,1)}, u32[]{:S(2)}) copy-start(bf16[256,128]{1,0:T(8,128)(2,1)} %copy-done.6) | copy-start | bytes 196612
  85.0 15.7 %copy-start.9 = (f32[8,2,256]{2,1,0:T(2,128)S(1)}, f32[8,2,256]{2,1,0:T(2,128)}, u32[]{:S(2)}) copy-start(f32[8,2,256]{2,1,0:T(2,128)} %copy-done.8) | copy-start | bytes 49156
  96.9 3.7 %copy-start.11 = (f32[2,128,1024]{2,1,0:T(8,128)}, f32[2,128,1024]{2,1,0:T(8,128)S(1)}, u32[]{:S(2)}) copy-start(f32[2,128,1024]{2,1,0:T(8,128)S(1)} %convert_add_fusion) | copy-start | bytes 3145732
  97.8 20.8 %collective-permute-start.4 = (bf16[1,128,1024]{2,1,0:T(8,128)(2,1)}, bf16[1,128,1024]{2,1,0:T(8,128)(2,1)}, u32[]{:S(2)}, u32[]{:S(2)}) collective-permute-start(bf16[1,128,1024]{2,1,0:T(8,128)(2,1)} %select_convert_fusion), channel_id=1, source_target_pairs={{0,128},{64,192},{128,0},{192,64},{1,129},{65,193},{129,1},{193,65... | collective-permute-start | bytes 786440 | tf_op jit(solution)/shard_map/ppermute | solution.py:323
  112.9 0.8 copy-start.1
  113.7 0.7 copy-start.2
  114.3 0.7 copy-start.4
  115.0 3.7 %copy-start.12 = (f32[2,128,1024]{2,1,0:T(8,128)S(1)}, f32[2,128,1024]{2,1,0:T(8,128)}, u32[]{:S(2)}) copy-start(f32[2,128,1024]{2,1,0:T(8,128)} %copy-done.11) | copy-start | bytes 3145732
  115.0 12.7 %all-to-all-start.3 = ((bf16[8,256,128]{2,1,0:T(8,128)(2,1)}), bf16[8,256,128]{2,1,0:T(8,128)(2,1)S(1)}, u32[]{:S(2)}, u32[]{:S(2)}) async-start(bf16[8,256,128]{2,1,0:T(8,128)(2,1)} %copy-done.1), calls=%async_computation.3 | async-start | bytes 1048576 | tf_op jit(solution)/shard_map/all_to_all | solution.py:328
  118.6 10.2 %copy-start.5 = (bf16[512,128]{1,0:T(8,128)(2,1)S(1)}, bf16[512,128]{1,0:T(8,128)(2,1)}, u32[]{:S(2)}) copy-start(bf16[512,128]{1,0:T(8,128)(2,1)} %copy-done.4) | copy-start | bytes 393220
  118.6 20.6 %copy-start.3 = (bf16[512,128]{1,0:T(8,128)(2,1)S(1)}, bf16[512,128]{1,0:T(8,128)(2,1)}, u32[]{:S(2)}) copy-start(bf16[512,128]{1,0:T(8,128)(2,1)} %copy-done.2) | copy-start | bytes 393220
  127.7 12.9 %collective-permute-start.7 = (bf16[4,1,16,1024]{3,2,1,0:T(8,128)(2,1)S(1)}, bf16[4,1,16,1024]{3,2,1,0:T(8,128)(2,1)}, u32[]{:S(2)}, u32[]{:S(2)}) collective-permute-start(bf16[4,1,16,1024]{3,2,1,0:T(8,128)(2,1)S(1)} %select_convert_fusion.1), channel_id=1, source_target_pairs={{0,4},{4,0},{1,5},{5,1},{2,6},{6,2},{3,7},{7,3},{8,12},{12,8},{9,1... | collective-permute-start | bytes 393224 | tf_op jit(solution)/shard_map/ppermute | solution.py:323
  128.8 17.1 %collective-permute-start.5 = (bf16[512,128]{1,0:T(8,128)(2,1)S(1)}, bf16[512,128]{1,0:T(8,128)(2,1)S(1)}, u32[]{:S(2)}, u32[]{:S(2)}) collective-permute-start(bf16[512,128]{1,0:T(8,128)(2,1)S(1)} %copy-done.5), channel_id=1, source_target_pairs={{0,8},{8,16},{16,24},{1,9},{9,17},{17,25},{2,10},{10,18},{18,26},{... | collective-permute-start | bytes 393224 | tf_op jit(solution)/shard_map/ppermute | solution.py:357
  139.3 8.4 %collective-permute-start.6 = (bf16[512,128]{1,0:T(8,128)(2,1)S(1)}, bf16[512,128]{1,0:T(8,128)(2,1)S(1)}, u32[]{:S(2)}, u32[]{:S(2)}) collective-permute-start(bf16[512,128]{1,0:T(8,128)(2,1)S(1)} %copy-done.3), channel_id=1, source_target_pairs={{8,0},{16,8},{24,16},{9,1},{17,9},{25,17},{10,2},{18,10},{26,18},{... | collective-permute-start | bytes 393224 | tf_op jit(solution)/shard_map/ppermute | solution.py:356
  141.6 6.7 %collective-permute-start.8 = (bf16[2,1,16,1024]{3,2,1,0:T(8,128)(2,1)S(1)}, bf16[2,1,16,1024]{3,2,1,0:T(8,128)(2,1)S(1)}, u32[]{:S(2)}, u32[]{:S(2)}) collective-permute-start(bf16[2,1,16,1024]{3,2,1,0:T(8,128)(2,1)S(1)} %select_convert_fusion.2), channel_id=1, source_target_pairs={{0,8},{8,0},{1,9},{9,1},{2,10},{10,2},{3,11},{11,3},{4,12},{12,4},... | collective-permute-start | bytes 196616 | tf_op jit(solution)/shard_map/ppermute | solution.py:323
  148.4 11.6 %collective-permute-start.9 = (bf16[1,16,1024]{2,1,0:T(8,128)(2,1)S(1)}, bf16[1,16,1024]{2,1,0:T(8,128)(2,1)S(1)}, u32[]{:S(2)}, u32[]{:S(2)}) collective-permute-start(bf16[1,16,1024]{2,1,0:T(8,128)(2,1)S(1)} %fusion.2), channel_id=1, source_target_pairs={{0,16},{16,0},{1,17},{17,1},{2,18},{18,2},{3,19},{19,3},{4,20},{20... | collective-permute-start | bytes 98312 | tf_op jit(solution)/shard_map/ppermute | solution.py:323
  156.4 16.2 %all-to-all-start.4 = ((bf16[8,512,128]{2,1,0:T(8,128)(2,1)}), bf16[8,512,128]{2,1,0:T(8,128)(2,1)S(1)}, u32[]{:S(2)}, u32[]{:S(2)}) async-start(bf16[8,512,128]{2,1,0:T(8,128)(2,1)} %pad_maximum_fusion), calls=%async_computation.4 | async-start | bytes 2097152 | tf_op jit(solution)/shard_map/all_to_all | solution.py:328
  160.0 12.0 %collective-permute-start.10 = (bf16[8,1024]{1,0:T(8,128)(2,1)S(1)}, bf16[8,1024]{1,0:T(8,128)(2,1)S(1)}, u32[]{:S(2)}, u32[]{:S(2)}) collective-permute-start(bf16[8,1024]{1,0:T(8,128)(2,1)S(1)} %fusion.3), channel_id=1, source_target_pairs={{0,2},{1,3},{2,0},{3,1},{4,6},{5,7},{6,4},{7,5},{8,10},{9,11},{10,... | collective-permute-start | bytes 49160 | tf_op jit(solution)/shard_map/ppermute | solution.py:323
  172.0 4.4 %collective-permute-start.11 = (bf16[4,1024]{1,0:T(4,128)(2,1)S(1)}, bf16[4,1024]{1,0:T(4,128)(2,1)S(1)}, u32[]{:S(2)}, u32[]{:S(2)}) collective-permute-start(bf16[4,1024]{1,0:T(4,128)(2,1)S(1)} %select_convert_fusion.5), channel_id=1, source_target_pairs={{0,1},{1,0},{2,3},{3,2},{4,5},{5,4},{6,7},{7,6},{8,9},{9,8},{10,11... | collective-permute-start | bytes 24584 | tf_op jit(solution)/shard_map/ppermute | solution.py:323

commit v3 on v2

--- a/solution.py
+++ b/solution.py
@@ -32,14 +32,18 @@
 
 
 def pack_kv_kernel(k_ref, v_ref, s_ref, o_ref):
+    down = lax.broadcasted_iota(jnp.int32, (PILS, PILS), 0)
+    along = lax.broadcasted_iota(jnp.int32, (PILS, PILS), 1)
+    shift = jnp.where(down == along, s_ref[...].astype(F32), 0.0)
+    shift = jnp.broadcast_to(jnp.sum(shift, axis=1, keepdims=True), (PILS, HD)).astype(BF)
     for n in range(o_ref.shape[0]):
         columns = slice(n * HD, (n + 1) * HD)
         o_ref[n, :ROWS] = k_ref[:, columns]
         o_ref[n, ROWS : 2 * ROWS] = v_ref[:, columns]
-        o_ref[n, 2 * ROWS :] = s_ref[...]
-
-
-def pack_kv(k, v, shift_cols):
+        o_ref[n, 2 * ROWS :] = shift
+
+
+def pack_kv(k, v, comb_shift):
     some = 4
     return pl.pallas_call(
         pack_kv_kernel,
@@ -47,20 +51,20 @@
         in_specs=[
             pl.BlockSpec((ROWS, some * HD), lambda h: (0, h)),
             pl.BlockSpec((ROWS, some * HD), lambda h: (0, h)),
-            pl.BlockSpec((PILS, HD), lambda h: (0, 0)),
+            pl.BlockSpec((1, PILS), lambda h: (0, 0)),
         ],
         out_specs=pl.BlockSpec((some, KV_ROWS, HD), lambda h: (h, 0, 0)),
         out_shape=jax.ShapeDtypeStruct((HEADS, KV_ROWS, HD), BF),
         name="pack_kv",
-    )(k, v, shift_cols)
-
-
-def pack_qg_kernel(q_ref, g_ref, w_ref, o_ref):
+    )(k, v, comb_shift)
+
+
+def pack_qg_kernel(q_ref, g_ref, w_ref, qo_ref, go_ref):
     grad = mm(g_ref[...], w_ref[...], 1, 1).astype(BF)
-    for n in range(o_ref.shape[0]):
+    for n in range(qo_ref.shape[0]):
         columns = slice(n * HD, (n + 1) * HD)
-        o_ref[n, :ROWS] = q_ref[:, columns]
-        o_ref[n, ROWS:] = grad[:, columns]
+        qo_ref[n] = q_ref[:, columns]
+        go_ref[n] = grad[:, columns]
 
 
 def pack_qg(q, g, w):
@@ -74,8 +78,8 @@
             pl.BlockSpec((ROWS, width), lambda h: (0, 0)),
             pl.BlockSpec((some * HD, width), lambda h: (h, 0)),
         ],
-        out_specs=pl.BlockSpec((some, 2 * ROWS, HD), lambda h: (h, 0, 0)),
-        out_shape=jax.ShapeDtypeStruct((HEADS, 2 * ROWS, HD), BF),
+        out_specs=[pl.BlockSpec((some, ROWS, HD), lambda h: (h, 0, 0))] * 2,
+        out_shape=[jax.ShapeDtypeStruct((HEADS, ROWS, HD), BF)] * 2,
         cost_estimate=pl.CostEstimate(
             flops=2 * ROWS * width * width, bytes_accessed=5 << 20, transcendentals=0
         ),
@@ -114,7 +118,7 @@
 
 
 def forward_kernel(
-    kv_ref, qg_ref, left_ref, right_ref, labk_ref, labq_ref,
+    kv_ref, q_ref, left_ref, right_ref, labk_ref, labq_ref,
     att_ref, stat_ref, k_pil, v_pil,
     k_all, vt_all, vt_pil,
 ):
@@ -133,7 +137,7 @@
                 v_pil[at] = mm(pick, vb, 1, 0).astype(BF)
         vt_pil[...] = v_pil[...].T
 
-    scores = window_scores(i, qg_ref[i, :ROWS], k_all, k_pil, labk_ref, labq_ref)
+    scores = window_scores(i, q_ref[i], k_all, k_pil, labk_ref, labq_ref)
     factor = SCALE * LOG2E
     top = functools.reduce(jnp.maximum, [jnp.max(s, axis=0, keepdims=True) for s in scores])
     top = top * factor
@@ -148,7 +152,7 @@
 
 
 def backward_kernel(
-    kv_ref, qg_ref, left_ref, right_ref, labk_ref, labq_ref, att_ref, stat_ref, k_pil, v_pil,
+    kv_ref, q_ref, left_ref, right_ref, labk_ref, labq_ref, ga_ref, att_ref, stat_ref, k_pil, v_pil,
     dq_ref, dkv_ref, dleft_ref, dright_ref,
     k_all, v_all, kt_all, kt_pil, dk_all, dv_all, dk_pil, dv_pil,
 ):
@@ -167,8 +171,8 @@
         dk_pil[...] = jnp.zeros_like(dk_pil)
         dv_pil[...] = jnp.zeros_like(dv_pil)
 
-    q = qg_ref[i, :ROWS]
-    ga = qg_ref[i, ROWS:]
+    q = q_ref[i]
+    ga = ga_ref[i]
     scores = window_scores(i, q, k_all, k_pil, labk_ref, labq_ref)
     top, inverse = stat_ref[i][:1], stat_ref[i][1:]
     product = ga.astype(F32) * att_ref[i].astype(F32)
@@ -324,6 +328,20 @@
     return jnp.where(upper, high, low) + got.astype(F32)
 
 
+def scattered(value, dim, axes):
+    count = lax.axis_size(axes)
+    me = lax.axis_index(axes)
+
+    def part(at):
+        return lax.dynamic_index_in_dim(value, at, dim, keepdims=False)
+
+    total = part(me)
+    for apart in range(1, count):
+        out = part(me ^ apart).astype(BF)
+        total = total + lax.ppermute(out, axes, [(j, j ^ apart) for j in range(count)]).astype(F32)
+    return total
+
+
 def to_heads(x):
     return lax.all_to_all(x, FRAME, 0, 0, tiled=True)
 
@@ -338,21 +356,25 @@
     ups = [(j, j + 1) for j in range(lax.axis_size(FRAMES) - 1)]
     downs = [(j, i) for i, j in ups]
 
-    shift_cols = jnp.broadcast_to(comb_shift[0].astype(BF)[:, None], (PILS, HD))
-    kv = to_heads(pack_kv(k, v, shift_cols))
+    kv = to_heads(pack_kv(k, v, comb_shift))
     left = lax.ppermute(kv[SHARDS - 1, : 2 * ROWS], FRAMES, ups)
     right = lax.ppermute(kv[0, : 2 * ROWS], FRAMES, downs)
-    qg = to_heads(pack_qg(q, g, w))
+    q, ga = pack_qg(q, g, w)
+    q, kv = lax.optimization_barrier((q, kv))
+    q = to_heads(q)
+    q, ga = lax.optimization_barrier((q, ga))
 
     label = jnp.pad(label, (HALF_SPAN, HALF_SPAN), constant_values=-1)
     label = lax.dynamic_slice_in_dim(label, frame * FRAME_ROWS, BLOCKS * ROWS, 0)
     labk = jnp.broadcast_to(label.reshape(BLOCKS, ROWS, 1), (BLOCKS, ROWS, HD))
     labq = label[HALF_SPAN : HALF_SPAN + FRAME_ROWS].reshape(SHARDS, 1, ROWS)
 
-    frame_ins = (kv, qg, left, right, labk, labq)
+    frame_ins = (kv, q, left, right, labk, labq)
     att, stats, k_pil, v_pil = forward(frame_ins)
+    ga = to_heads(ga)
     att_rows = to_heads(att)
-    dq, dkv, dleft, dright = backward(frame_ins + (att, stats, k_pil, v_pil))
+    dq, dkv, dleft, dright = backward(frame_ins + (ga, att, stats, k_pil, v_pil))
+    att_rows, dq, dkv, dleft, dright = lax.optimization_barrier((att_rows, dq, dkv, dleft, dright))
     from_right = lax.ppermute(dleft, FRAMES, downs)
     from_left = lax.ppermute(dright, FRAMES, ups)
 
@@ -360,9 +382,9 @@
     head = jnp.arange(4, dtype=jnp.int32) * 2
     share = share_of(att_rows, g, head + (1 - core), None, BF)
     got = lax.ppermute(share, "c", [(0, 1), (1, 0)])
-    mixed = mix(att_rows, w)
     mine = jnp.arange(2, dtype=jnp.int32) * 4 + core
     send = share_of(att_rows, g, mine + 2 * (1 - z_bit), got, BF)
+    send, from_left, from_right = lax.optimization_barrier((send, from_left, from_right))
     keep = share_of(att_rows, g, mine + 2 * z_bit, got, F32)
     got = lax.ppermute(send, "zl", [(j, j ^ 1) for j in range(4)])
     share = keep + got.astype(F32)
@@ -371,17 +393,16 @@
     first = dkv[:1].astype(F32) + from_left.astype(F32)[None]
     last = dkv[SHARDS - 1 :].astype(F32) + from_right.astype(F32)[None]
     dkv = jnp.concatenate([first.astype(BF), dkv[1 : SHARDS - 1], last.astype(BF)], axis=0)
+    share, dq, dkv = lax.optimization_barrier((share, dq, dkv))
+    dkv = to_heads(dkv)
+    mixed = mix(att_rows, w)
     share = halved(share, 0, "zl", 1)[0]
-    share, dq = lax.optimization_barrier((share, dq))
-    dkv = to_heads(dkv)
+    share, dkv, mixed = lax.optimization_barrier((share, dkv, mixed))
 
     width = share.shape[-1]
-    share = halved(share.reshape(4, 2, 16, width), 1, "xl", 0)
-    share = halved(share.reshape(2, 2, 16, width), 1, "xh", 0)
-    share = halved(share.reshape(2, 16, width), 0, "zh", 0)
-    share = share.reshape(16, width)
-    share = halved(share, 0, "y", 1)
-    share = halved(share, 0, "y", 0)
+    share = scattered(share.reshape(2, 4, 16, width), 1, ("xh", "xl"))
+    share = halved(share, 0, "zh", 0)
+    share = scattered(share.reshape(4, 4, width), 0, ("y",))
     weight_grad = share * (1.0 / math.sqrt(8 * 32 * ROWS))
     return (
         mixed[None],

time: 179 us -> 186 us (1.039)
  local copies, waits for them, and re-layouts: 8.6 us -> 15.2 us
  starting transfers between devices: 57.9 us -> 63.1 us
  other arithmetic: 8.6 us -> 3.76 us
    ppermute x6 -> x2, starting transfers between devices: 19.1 us -> 1.35 us  [halved(): got = lax.ppermute(out, axis, [(j, j ^ 1 << bit) for j in range(count)])]
    ppermute x0 -> x6, starting transfers between devices: none -> 13.4 us  [scattered(): lax.ppermute(out, axes, [(j, j ^ apart) for j in range(count)]).astype(F32)]
    all_to_all x5 -> x6, waiting for transfers between devices: 36.4 us -> 24.1 us  [to_heads(): return lax.all_to_all(x, FRAME, 0, 0, tiled=True)]
    ppermute x6 -> x2, waiting for transfers between devices: 4.88 us -> 12.3 us  [halved(): got = lax.ppermute(out, axis, [(j, j ^ 1 << bit) for j in range(count)])]
    unnamed x31 -> x39, local copies, waits for them, and re-layouts: 6.56 us -> 13.8 us
    all_to_all x5 -> x6, starting transfers between devices: 21.1 us -> 27.9 us  [to_heads(): return lax.all_to_all(x, FRAME, 0, 0, tiled=True)]
    ppermute x0 -> x6, waiting for transfers between devices: none -> 6.36 us  [scattered(): lax.ppermute(out, axes, [(j, j ^ apart) for j in range(count)]).astype(F32)]
    ppermute x1, waiting for transfers between devices: 10.5 us -> 4.13 us  [on_device(): got = lax.ppermute(send, 'zl', [(j, j ^ 1) for j in range(4)])]
  transfers between devices with their start and end apart: 17 -> 20, of which waited for: 10 -> 13; matrix products, arithmetic and copies ran while one was open for 5% -> 4% of each run, Pallas kernels for 14% -> 19%
where the time goes in v3:
time: 186 us; the launch traced here: 184 us
  starting transfers between devices  63.1 us (34%)
  waiting for transfers between devices  59.2 us (32%)
  Pallas kernels  42.3 us (23%)
  local copies, waits for them, and re-layouts  15.2 us (8%)
  other arithmetic  3.76 us (2%)
    all_to_all x6, starting transfers between devices, to_heads(): return lax.all_to_all(x, FRAME, 0, 0, tiled=True)  27.9 us
    all_to_all x6, waiting for transfers between devices, to_heads(): return lax.all_to_all(x, FRAME, 0, 0, tiled=True)  24.1 us
    pallas_call x2, Pallas kernels, over_blocks(): pl.pallas_call(kernel, grid=(SHARDS,), in_specs=[whole(a.shape) for a in...  20.5 us
    unnamed x39, local copies, waits for them, and re-layouts  13.8 us
    ppermute x6, starting transfers between devices, scattered(): lax.ppermute(out, axes, [(j, j ^ apart) for j in range(count)]).astype(F32)  13.4 us
    ppermute x1, starting transfers between devices, on_device(): from_left = lax.ppermute(dright, FRAMES, ups)  13.2 us
    ppermute x2, waiting for transfers between devices, halved(): got = lax.ppermute(out, axis, [(j, j ^ 1 << bit) for j in range(count)])  12.3 us
    pallas_call x3, Pallas kernels, share_of(): pl.pallas_call(share_kernel, grid_spec=pltpu.PrefetchScalarGridSpec(num_s...  11 us
  transfers between devices with their start and end apart: 20, of which 13 were waited for; matrix products, arithmetic and copies ran while one was open for 4% of the time, Pallas kernels for 19%

profile of v3, /device:TPU:32, one launch (start us, length us, event | category | flops | bytes accessed | tf_op | source)
XLA Modules:
  0.0 184.5 jit_solution(5634942045177284272)
XLA Ops:
  0.6 2.2 %pack_kv.1 = bf16[8,544,128]{2,1,0:T(8,128)(2,1)} custom-call(bf16[256,1024]{1,0:T(8,128)(2,1)} %bitcast.73, bf16[256,1024]{1,0:T(8,128)(2,1)} %bitcast.74, s32[1,32]{1,0:T(1,128)} %s_ref.1), custom_call_target="tpu_custom_call" | custom-call | tf_op jit(solution)/shard_map/pack_kv/pallas_call | solution.py:48
  2.8 5.4 %all-to-all-start = ((bf16[8,544,128]{2,1,0:T(8,128)(2,1)}), bf16[8,544,128]{2,1,0:T(8,128)(2,1)S(1)}, u32[]{:S(2)}, u32[]{:S(2)}) async-start(bf16[8,544,128]{2,1,0:T(8,128)(2,1)} %pack_kv.1), calls=%async_computation | async-start | bytes 2228224 | tf_op jit(solution)/shard_map/all_to_all | solution.py:346
  8.2 4.4 %pack_qg.1 = (bf16[8,256,128]{2,1,0:T(8,128)(2,1)}, bf16[8,256,128]{2,1,0:T(8,128)(2,1)}) custom-call(bf16[256,1024]{1,0:T(8,128)(2,1)} %bitcast.75, bf16[256,1024]{1,0:T(8,128)(2,1)} %bitcast.63, bf16[1024,1024]{1,0:T(8,128)(2,1)} %w_ref.3), custom_call_target="tpu_custom_call" | custom-call | flops 536870912 | bytes 5242880 | tf_op jit(solution)/shard_map/pack_qg/pallas_call | solution.py:73
  12.7 11.1 %all-to-all-done.kv_ref = bf16[8,544,128]{2,1,0:T(8,128)(2,1)S(1)} async-done(((bf16[8,544,128]{2,1,0:T(8,128)(2,1)}), bf16[8,544,128]{2,1,0:T(8,128)(2,1)S(1)}, u32[]{:S(2)}, u32[]{:S(2)}) %all-to-all-start) | async-done | bytes 1114144 | tf_op jit(solution)/shard_map/all_to_all | solution.py:346
  23.7 3.8 %all-to-all-start.1 = ((bf16[8,256,128]{2,1,0:T(8,128)(2,1)}), bf16[8,256,128]{2,1,0:T(8,128)(2,1)S(1)}, u32[]{:S(2)}, u32[]{:S(2)}) async-start(bf16[8,256,128]{2,1,0:T(8,128)(2,1)} %get-tuple-element.35), calls=%async_computation.1 | async-start | bytes 1048576 | tf_op jit(solution)/shard_map/all_to_all | solution.py:346
  27.5 9.6 %all-to-all-done.1.q_ref = bf16[8,256,128]{2,1,0:T(8,128)(2,1)S(1)} async-done(((bf16[8,256,128]{2,1,0:T(8,128)(2,1)}), bf16[8,256,128]{2,1,0:T(8,128)(2,1)S(1)}, u32[]{:S(2)}, u32[]{:S(2)}) %all-to-all-start.1) | async-done | bytes 524320 | tf_op jit(solution)/shard_map/all_to_all | solution.py:346
  37.1 3.5 %all-to-all-start.3 = ((bf16[8,256,128]{2,1,0:T(8,128)(2,1)}), bf16[8,256,128]{2,1,0:T(8,128)(2,1)S(1)}, u32[]{:S(2)}, u32[]{:S(2)}) async-start(bf16[8,256,128]{2,1,0:T(8,128)(2,1)} %get-tuple-element.39), calls=%async_computation.3 | async-start | bytes 1048576 | tf_op jit(solution)/shard_map/all_to_all | solution.py:346
  40.6 4.6 %collective-permute-start = (bf16[512,128]{1,0:T(8,128)(2,1)S(1)}, bf16[512,128]{1,0:T(8,128)(2,1)S(1)}, u32[]{:S(2)}, u32[]{:S(2)}) collective-permute-start(bf16[512,128]{1,0:T(8,128)(2,1)S(1)} %get-tuple-element.67), channel_id=1, source_target_pairs={{0,8},{8,16},{16,24},{1,9},{9,17},{17,25},{2,10},{10,18},{18,26},{... | collective-permute-start | bytes 393224 | tf_op jit(solution)/shard_map/ppermute | solution.py:360
  45.3 1.3 collective-permute-start.1
  46.7 2.5 %collective-permute-done.left_ref = bf16[512,128]{1,0:T(8,128)(2,1)S(1)} collective-permute-done((bf16[512,128]{1,0:T(8,128)(2,1)S(1)}, bf16[512,128]{1,0:T(8,128)(2,1)S(1)}, u32[]{:S(2)}, u32[]{:S(2)}) %collective-permute-start) | collective-permute-done | bytes 131104 | tf_op jit(solution)/shard_map/ppermute | solution.py:360
  49.2 0.7 copy-done.3
  49.9 6.8 %collective-permute-done.1.right_ref = bf16[512,128]{1,0:T(8,128)(2,1)S(1)} collective-permute-done((bf16[512,128]{1,0:T(8,128)(2,1)S(1)}, bf16[512,128]{1,0:T(8,128)(2,1)S(1)}, u32[]{:S(2)}, u32[]{:S(2)}) %collective-permute-start.1) | collective-permute-done | bytes 131104 | tf_op jit(solution)/shard_map/ppermute | solution.py:361
  56.7 0.7 copy-done.6
  57.3 0.4 broadcast_in_dim.23.labk_ref
  57.8 0.5 copy-done.4
  58.3 0.9 copy-done.7
  59.2 7.6 %forward.1 = (bf16[8,256,128]{2,1,0:T(8,128)(2,1)S(1)}, f32[8,2,256]{2,1,0:T(2,128)S(1)}, bf16[256,128]{1,0:T(8,128)(2,1)S(1)}, bf16[256,128]{1,0:T(8,128)(2,1)S(1)}) custom-call(bf16[8,544,128]{2,1,0:T(8,128)(2,1)S(1)} %all-to-all-done.kv_ref, bf16[8,256,128]{2,1,0:T(8,128)(2,1)S(1)} %all-to-all-done.1.q_ref, bf16[512,128]{1,0:T(8,128)(2,1)S(1)} %copy-done.4, ...), custom_call_target="tpu_custom_call" | custom-call | flops 1073741824 | bytes 8388608 | tf_op jit(solution)/shard_map/forward/pallas_call | solution.py:219
  66.8 0.8 copy-done.1
  67.5 0.6 copy-done.11
  68.1 0.6 copy-done.13
  68.8 5.6 %all-to-all-start.2 = ((bf16[8,256,128]{2,1,0:T(8,128)(2,1)}), bf16[8,256,128]{2,1,0:T(8,128)(2,1)}, u32[]{:S(2)}, u32[]{:S(2)}) async-start(bf16[8,256,128]{2,1,0:T(8,128)(2,1)} %copy-done.1), calls=%async_computation.2 | async-start | bytes 1048576 | tf_op jit(solution)/shard_map/all_to_all | solution.py:346
  74.3 0.6 multiply_add_fusion.heads_ref
  74.9 1.0 copy-done.2
  76.0 0.9 copy-done.5
  76.9 0.9 copy-done.8
  77.8 0.8 copy-done.12
  78.6 0.7 copy-done.14
  79.3 12.9 %backward.1 = (bf16[8,256,128]{2,1,0:T(8,128)(2,1)}, bf16[8,512,128]{2,1,0:T(8,128)(2,1)S(1)}, bf16[512,128]{1,0:T(8,128)(2,1)S(1)}, bf16[512,128]{1,0:T(8,128)(2,1)S(1)}) custom-call(bf16[8,544,128]{2,1,0:T(8,128)(2,1)S(1)} %all-to-all-done.kv_ref, bf16[8,256,128]{2,1,0:T(8,128)(2,1)S(1)} %all-to-all-done.1.q_ref, bf16[512,128]{1,0:T(8,128)(2,1)S(1)} %copy-done.5, ...), custom_call_target="tpu_custom_call" | custom-call | flops 2684354560 | bytes 8388608 | tf_op jit(solution)/shard_map/backward/pallas_call | solution.py:219
  92.2 0.7 copy-done.9
  92.9 4.6 %share.3 = bf16[4,128,1024]{2,1,0:T(8,128)(2,1)} custom-call(s32[4]{0:T(128)} %multiply_add_fusion.heads_ref, bf16[8,256,128]{2,1,0:T(8,128)(2,1)} %all-to-all-done.2.att_ref, bf16[256,1024]{1,0:T(8,128)(2,1)} %bitcast.64), custom_call_target="tpu_custom_call" | custom-call | flops 268435456 | bytes 2097152 | tf_op jit(solution)/shard_map/share/pallas_call | solution.py:304
  97.5 13.2 %collective-permute-start.3 = (bf16[512,128]{1,0:T(8,128)(2,1)S(1)}, bf16[512,128]{1,0:T(8,128)(2,1)S(1)}, u32[]{:S(2)}, u32[]{:S(2)}) collective-permute-start(bf16[512,128]{1,0:T(8,128)(2,1)S(1)} %copy-done.10), channel_id=1, source_target_pairs={{0,8},{8,16},{16,24},{1,9},{9,17},{17,25},{2,10},{10,18},{18,26},{... | collective-permute-start | bytes 393224 | tf_op jit(solution)/shard_map/ppermute | solution.py:379
  110.8 1.3 collective-permute-start.4
  112.1 0.5 fusion.13.heads_ref
  112.6 1.0 copy-done.15
  113.6 3.1 %share.5 = bf16[2,128,1024]{2,1,0:T(8,128)(2,1)} custom-call(s32[2]{0:T(128)} %fusion.13.heads_ref, bf16[8,256,128]{2,1,0:T(8,128)(2,1)} %all-to-all-done.2.att_ref, bf16[256,1024]{1,0:T(8,128)(2,1)} %bitcast.65, bf16[4,128,1024]{2,1,0:T(8,128)(2,1)} %copy-done.15), custom_call_target="tpu_custom_call" | custom-call | flops 134217728 | bytes 2097152 | tf_op jit(solution)/shard_map/share/pallas_call | solution.py:304
  116.7 3.1 %collective-permute-done.4 = bf16[512,128]{1,0:T(8,128)(2,1)S(1)} collective-permute-done((bf16[512,128]{1,0:T(8,128)(2,1)S(1)}, bf16[512,128]{1,0:T(8,128)(2,1)S(1)}, u32[]{:S(2)}, u32[]{:S(2)}) %collective-permute-start.4) | collective-permute-done | bytes 131104 | tf_op jit(solution)/shard_map/ppermute | solution.py:378
  119.8 0.5 fusion.14.heads_ref
  120.4 5.1 %all-to-all-start.4 = ((bf16[8,256,128]{2,1,0:T(8,128)(2,1)}), bf16[8,256,128]{2,1,0:T(8,128)(2,1)S(1)}, u32[]{:S(2)}, u32[]{:S(2)}) async-start(bf16[8,256,128]{2,1,0:T(8,128)(2,1)} %get-tuple-element.51), calls=%async_computation.4 | async-start | bytes 1048576 | tf_op jit(solution)/shard_map/all_to_all | solution.py:346
  125.5 3.2 %share.4 = f32[2,128,1024]{2,1,0:T(8,128)} custom-call(s32[2]{0:T(128)} %fusion.14.heads_ref, bf16[8,256,128]{2,1,0:T(8,128)(2,1)} %all-to-all-done.2.att_ref, bf16[256,1024]{1,0:T(8,128)(2,1)} %bitcast.66, bf16[4,128,1024]{2,1,0:T(8,128)(2,1)} %copy-done.15), custom_call_target="tpu_custom_call" | custom-call | flops 134217728 | bytes 2097152 | tf_op jit(solution)/shard_map/share/pallas_call | solution.py:304
  128.8 1.1 pad_maximum_fusion
  129.9 4.1 %collective-permute-done.5 = bf16[2,128,1024]{2,1,0:T(8,128)(2,1)S(1)} collective-permute-done((bf16[2,128,1024]{2,1,0:T(8,128)(2,1)}, bf16[2,128,1024]{2,1,0:T(8,128)(2,1)S(1)}, u32[]{:S(2)}, u32[]{:S(2)}) %collective-permute-start.5) | collective-permute-done | bytes 524320 | tf_op jit(solution)/shard_map/ppermute | solution.py:389
  134.0 0.1 convert_add_fusion
  134.2 0.5 all-to-all-done.4
  134.7 4.6 %all-to-all-start.5 = ((bf16[8,512,128]{2,1,0:T(8,128)(2,1)}), bf16[8,512,128]{2,1,0:T(8,128)(2,1)S(1)}, u32[]{:S(2)}, u32[]{:S(2)}) async-start(bf16[8,512,128]{2,1,0:T(8,128)(2,1)} %pad_maximum_fusion), calls=%async_computation.5 | async-start | bytes 2097152 | tf_op jit(solution)/shard_map/all_to_all | solution.py:346
  139.4 1.3 collective-permute-start.6
  140.6 4.2 %mix.1 = bf16[256,1024]{1,0:T(8,128)(2,1)} custom-call(bf16[8,256,128]{2,1,0:T(8,128)(2,1)} %all-to-all-done.2.att_ref, bf16[1024,1024]{1,0:T(8,128)(2,1)} %w_ref.3), custom_call_target="tpu_custom_call" | custom-call | flops 536870912 | bytes 3145728 | tf_op jit(solution)/shard_map/mix/pallas_call | solution.py:273
  144.8 5.7 %collective-permute-done.6 = bf16[1,128,1024]{2,1,0:T(8,128)(2,1)S(1)} collective-permute-done((bf16[1,128,1024]{2,1,0:T(8,128)(2,1)S(1)}, bf16[1,128,1024]{2,1,0:T(8,128)(2,1)S(1)}, u32[]{:S(2)}, u32[]{:S(2)}) %collective-permute-start.6) | collective-permute-done | bytes 262176 | tf_op jit(solution)/shard_map/ppermute | solution.py:327
  150.6 2.9 %all-to-all-done.5 = bf16[8,512,128]{2,1,0:T(8,128)(2,1)S(1)} async-done(((bf16[8,512,128]{2,1,0:T(8,128)(2,1)}), bf16[8,512,128]{2,1,0:T(8,128)(2,1)S(1)}, u32[]{:S(2)}, u32[]{:S(2)}) %all-to-all-start.5) | async-done | bytes 1048608 | tf_op jit(solution)/shard_map/all_to_all | solution.py:346
  153.6 1.6 collective-permute-start.7
  155.1 7.0 %collective-permute-start.8 = (bf16[2,16,1024]{2,1,0:T(8,128)(2,1)S(1)}, bf16[2,16,1024]{2,1,0:T(8,128)(2,1)S(1)}, u32[]{:S(2)}, u32[]{:S(2)}) collective-permute-start(bf16[2,16,1024]{2,1,0:T(8,128)(2,1)S(1)} %get-tuple-element.74), channel_id=1, source_target_pairs={{0,8},{4,12},{8,0},{12,4},{1,9},{5,13},{9,1},{13,5},{2,10},{6,14},... | collective-permute-start | bytes 196616 | tf_op jit(solution)/shard_map/ppermute | solution.py:341
  162.1 3.0 %collective-permute-done.8 = bf16[2,16,1024]{2,1,0:T(8,128)(2,1)S(1)} collective-permute-done((bf16[2,16,1024]{2,1,0:T(8,128)(2,1)S(1)}, bf16[2,16,1024]{2,1,0:T(8,128)(2,1)S(1)}, u32[]{:S(2)}, u32[]{:S(2)}) %collective-permute-start.8) | collective-permute-done | bytes 65568 | tf_op jit(solution)/shard_map/ppermute | solution.py:341
  165.2 2.4 %collective-permute-done.9 = bf16[2,16,1024]{2,1,0:T(8,128)(2,1)S(1)} collective-permute-done((bf16[2,16,1024]{2,1,0:T(8,128)(2,1)S(1)}, bf16[2,16,1024]{2,1,0:T(8,128)(2,1)S(1)}, u32[]{:S(2)}, u32[]{:S(2)}) %collective-permute-start.9) | collective-permute-done | bytes 65568 | tf_op jit(solution)/shard_map/ppermute | solution.py:341
  167.8 0.2 copy.14
  168.0 1.0 copy.19
  169.0 6.6 %collective-permute-done.10 = bf16[1,16,1024]{2,1,0:T(8,128)(2,1)S(1)} collective-permute-done((bf16[1,16,1024]{2,1,0:T(8,128)(2,1)S(1)}, bf16[1,16,1024]{2,1,0:T(8,128)(2,1)S(1)}, u32[]{:S(2)}, u32[]{:S(2)}) %collective-permute-start.10) | collective-permute-done | bytes 32800 | tf_op jit(solution)/shard_map/ppermute | solution.py:327
  175.6 1.1 collective-permute-start.11
  176.7 2.3 %collective-permute-start.12 = (bf16[4,1024]{1,0:T(4,128)(2,1)S(1)}, bf16[4,1024]{1,0:T(4,128)(2,1)S(1)}, u32[]{:S(2)}, u32[]{:S(2)}) collective-permute-start(bf16[4,1024]{1,0:T(4,128)(2,1)S(1)} %get-tuple-element.77), channel_id=1, source_target_pairs={{0,2},{1,3},{2,0},{3,1},{4,6},{5,7},{6,4},{7,5},{8,10},{9,11},{10,... | collective-permute-start | bytes 24584 | tf_op jit(solution)/shard_map/ppermute | solution.py:341
  179.0 1.4 collective-permute-start.13
  180.5 0.2 copy.15
  180.7 1.0 copy.20
  181.7 0.2 copy.16
  182.0 1.0 copy.21
  183.0 0.9 collective-permute-done.13
  183.9 0.6 fusion.9
  (48 shorter events, 0.8 us)
Async XLA Ops:
  2.8 20.9 %all-to-all-start = ((bf16[8,544,128]{2,1,0:T(8,128)(2,1)}), bf16[8,544,128]{2,1,0:T(8,128)(2,1)S(1)}, u32[]{:S(2)}, u32[]{:S(2)}) async-start(bf16[8,544,128]{2,1,0:T(8,128)(2,1)} %pack_kv.1), calls=%async_computation | async-start | bytes 2228224 | tf_op jit(solution)/shard_map/all_to_all | solution.py:346
  23.7 22.9 %copy-start.17 = (s32[8192]{0:T(1024)S(1)}, s32[8192]{0:T(1024)}, u32[]{:S(2)}) copy-start(s32[8192]{0:T(1024)} %param.13) | copy-start | bytes 98308
  23.7 13.4 %all-to-all-start.1 = ((bf16[8,256,128]{2,1,0:T(8,128)(2,1)}), bf16[8,256,128]{2,1,0:T(8,128)(2,1)S(1)}, u32[]{:S(2)}, u32[]{:S(2)}) async-start(bf16[8,256,128]{2,1,0:T(8,128)(2,1)} %get-tuple-element.35), calls=%async_computation.1 | async-start | bytes 1048576 | tf_op jit(solution)/shard_map/all_to_all | solution.py:346
  37.1 31.7 %all-to-all-start.3 = ((bf16[8,256,128]{2,1,0:T(8,128)(2,1)}), bf16[8,256,128]{2,1,0:T(8,128)(2,1)S(1)}, u32[]{:S(2)}, u32[]{:S(2)}) async-start(bf16[8,256,128]{2,1,0:T(8,128)(2,1)} %get-tuple-element.39), calls=%async_computation.3 | async-start | bytes 1048576 | tf_op jit(solution)/shard_map/all_to_all | solution.py:346
  40.6 8.6 %collective-permute-start = (bf16[512,128]{1,0:T(8,128)(2,1)S(1)}, bf16[512,128]{1,0:T(8,128)(2,1)S(1)}, u32[]{:S(2)}, u32[]{:S(2)}) collective-permute-start(bf16[512,128]{1,0:T(8,128)(2,1)S(1)} %get-tuple-element.67), channel_id=1, source_target_pairs={{0,8},{8,16},{16,24},{1,9},{9,17},{17,25},{2,10},{10,18},{18,26},{... | collective-permute-start | bytes 393224 | tf_op jit(solution)/shard_map/ppermute | solution.py:360
  45.3 11.4 %collective-permute-start.1 = (bf16[512,128]{1,0:T(8,128)(2,1)S(1)}, bf16[512,128]{1,0:T(8,128)(2,1)S(1)}, u32[]{:S(2)}, u32[]{:S(2)}) collective-permute-start(bf16[512,128]{1,0:T(8,128)(2,1)S(1)} %get-tuple-element.66), channel_id=1, source_target_pairs={{8,0},{16,8},{24,16},{9,1},{17,9},{25,17},{10,2},{18,10},{26,18},{... | collective-permute-start | bytes 393224 | tf_op jit(solution)/shard_map/ppermute | solution.py:361
  49.2 0.7 copy-start.3
  56.7 0.7 copy-start.6
  57.3 0.9 copy-start.4
  57.7 9.0 %copy-start = (s32[10,256,128]{2,1,0:T(8,128)}, s32[10,256,128]{2,1,0:T(8,128)S(1)}, u32[]{:S(2)}) copy-start(s32[10,256,128]{2,1,0:T(8,128)S(1)} %broadcast_in_dim.23.labk_ref) | copy-start | bytes 3932164
  58.2 0.9 copy-start.7
  66.7 0.8 copy-start.1
  67.5 0.6 copy-start.11
  68.1 0.6 copy-start.13
  68.8 24.1 %all-to-all-start.2 = ((bf16[8,256,128]{2,1,0:T(8,128)(2,1)}), bf16[8,256,128]{2,1,0:T(8,128)(2,1)}, u32[]{:S(2)}, u32[]{:S(2)}) async-start(bf16[8,256,128]{2,1,0:T(8,128)(2,1)} %copy-done.1), calls=%async_computation.2 | async-start | bytes 1048576 | tf_op jit(solution)/shard_map/all_to_all | solution.py:346
  74.9 1.0 copy-start.2
  76.0 0.9 copy-start.5
  76.9 0.9 copy-start.8
  77.8 0.8 copy-start.12
  78.6 0.7 copy-start.14
  92.2 0.7 copy-start.9
  92.9 4.7 %copy-start.10 = (bf16[512,128]{1,0:T(8,128)(2,1)S(1)}, bf16[512,128]{1,0:T(8,128)(2,1)}, u32[]{:S(2)}) copy-start(bf16[512,128]{1,0:T(8,128)(2,1)} %copy-done.9) | copy-start | bytes 393220
  97.5 15.1 %collective-permute-start.2 = (bf16[4,128,1024]{2,1,0:T(8,128)(2,1)}, bf16[4,128,1024]{2,1,0:T(8,128)(2,1)S(1)}, u32[]{:S(2)}, u32[]{:S(2)}) collective-permute-start(bf16[4,128,1024]{2,1,0:T(8,128)(2,1)} %share.3), channel_id=1, source_target_pairs={{0,32},{32,0},{1,33},{33,1},{2,34},{34,2},{3,35},{35,3},{4,36},{36... | collective-permute-start | bytes 3145736 | tf_op jit(solution)/shard_map/ppermute | solution.py:384
  97.5 19.2 %collective-permute-start.3 = (bf16[512,128]{1,0:T(8,128)(2,1)S(1)}, bf16[512,128]{1,0:T(8,128)(2,1)S(1)}, u32[]{:S(2)}, u32[]{:S(2)}) collective-permute-start(bf16[512,128]{1,0:T(8,128)(2,1)S(1)} %copy-done.10), channel_id=1, source_target_pairs={{0,8},{8,16},{16,24},{1,9},{9,17},{17,25},{2,10},{10,18},{18,26},{... | collective-permute-start | bytes 393224 | tf_op jit(solution)/shard_map/ppermute | solution.py:379
  110.8 9.0 %collective-permute-start.4 = (bf16[512,128]{1,0:T(8,128)(2,1)S(1)}, bf16[512,128]{1,0:T(8,128)(2,1)S(1)}, u32[]{:S(2)}, u32[]{:S(2)}) collective-permute-start(bf16[512,128]{1,0:T(8,128)(2,1)S(1)} %get-tuple-element.49), channel_id=1, source_target_pairs={{8,0},{16,8},{24,16},{9,1},{17,9},{25,17},{10,2},{18,10},{26,18},{... | collective-permute-start | bytes 393224 | tf_op jit(solution)/shard_map/ppermute | solution.py:378
  112.6 1.0 copy-start.15
  119.8 14.2 %collective-permute-start.5 = (bf16[2,128,1024]{2,1,0:T(8,128)(2,1)}, bf16[2,128,1024]{2,1,0:T(8,128)(2,1)S(1)}, u32[]{:S(2)}, u32[]{:S(2)}) collective-permute-start(bf16[2,128,1024]{2,1,0:T(8,128)(2,1)} %share.5), channel_id=1, source_target_pairs={{0,64},{64,0},{128,192},{192,128},{1,65},{65,1},{129,193},{193,129... | collective-permute-start | bytes 1572872 | tf_op jit(solution)/shard_map/ppermute | solution.py:389
  120.4 14.3 %all-to-all-start.4 = ((bf16[8,256,128]{2,1,0:T(8,128)(2,1)}), bf16[8,256,128]{2,1,0:T(8,128)(2,1)S(1)}, u32[]{:S(2)}, u32[]{:S(2)}) async-start(bf16[8,256,128]{2,1,0:T(8,128)(2,1)} %get-tuple-element.51), calls=%async_computation.4 | async-start | bytes 1048576 | tf_op jit(solution)/shard_map/all_to_all | solution.py:346
  128.8 5.2 %copy-start.16 = (f32[2,128,1024]{2,1,0:T(8,128)S(1)}, f32[2,128,1024]{2,1,0:T(8,128)}, u32[]{:S(2)}) copy-start(f32[2,128,1024]{2,1,0:T(8,128)} %share.4) | copy-start | bytes 3145732
  134.7 18.8 %all-to-all-start.5 = ((bf16[8,512,128]{2,1,0:T(8,128)(2,1)}), bf16[8,512,128]{2,1,0:T(8,128)(2,1)S(1)}, u32[]{:S(2)}, u32[]{:S(2)}) async-start(bf16[8,512,128]{2,1,0:T(8,128)(2,1)} %pad_maximum_fusion), calls=%async_computation.5 | async-start | bytes 2097152 | tf_op jit(solution)/shard_map/all_to_all | solution.py:346
  139.4 11.2 %collective-permute-start.6 = (bf16[1,128,1024]{2,1,0:T(8,128)(2,1)S(1)}, bf16[1,128,1024]{2,1,0:T(8,128)(2,1)S(1)}, u32[]{:S(2)}, u32[]{:S(2)}) collective-permute-start(bf16[1,128,1024]{2,1,0:T(8,128)(2,1)S(1)} %select_convert_fusion), channel_id=1, source_target_pairs={{0,128},{64,192},{128,0},{192,64},{1,129},{65,193},{129,1},{193,65... | collective-permute-start | bytes 786440 | tf_op jit(solution)/shard_map/ppermute | solution.py:327
  153.6 8.6 %collective-permute-start.7 = (bf16[2,16,1024]{2,1,0:T(8,128)(2,1)S(1)}, bf16[2,16,1024]{2,1,0:T(8,128)(2,1)S(1)}, u32[]{:S(2)}, u32[]{:S(2)}) collective-permute-start(bf16[2,16,1024]{2,1,0:T(8,128)(2,1)S(1)} %get-tuple-element.72), channel_id=1, source_target_pairs={{0,4},{4,0},{8,12},{12,8},{1,5},{5,1},{9,13},{13,9},{2,6},{6,2},{1... | collective-permute-start | bytes 196616 | tf_op jit(solution)/shard_map/ppermute | solution.py:341
  155.1 10.0 %collective-permute-start.8 = (bf16[2,16,1024]{2,1,0:T(8,128)(2,1)S(1)}, bf16[2,16,1024]{2,1,0:T(8,128)(2,1)S(1)}, u32[]{:S(2)}, u32[]{:S(2)}) collective-permute-start(bf16[2,16,1024]{2,1,0:T(8,128)(2,1)S(1)} %get-tuple-element.74), channel_id=1, source_target_pairs={{0,8},{4,12},{8,0},{12,4},{1,9},{5,13},{9,1},{13,5},{2,10},{6,14},... | collective-permute-start | bytes 196616 | tf_op jit(solution)/shard_map/ppermute | solution.py:341
  162.1 5.5 %collective-permute-start.9 = (bf16[2,16,1024]{2,1,0:T(8,128)(2,1)S(1)}, bf16[2,16,1024]{2,1,0:T(8,128)(2,1)S(1)}, u32[]{:S(2)}, u32[]{:S(2)}) collective-permute-start(bf16[2,16,1024]{2,1,0:T(8,128)(2,1)S(1)} %get-tuple-element.73), channel_id=1, source_target_pairs={{0,12},{4,8},{8,4},{12,0},{1,13},{5,9},{9,5},{13,1},{2,14},{6,10},... | collective-permute-start | bytes 196616 | tf_op jit(solution)/shard_map/ppermute | solution.py:341
  167.7 7.9 %collective-permute-start.10 = (bf16[1,16,1024]{2,1,0:T(8,128)(2,1)S(1)}, bf16[1,16,1024]{2,1,0:T(8,128)(2,1)S(1)}, u32[]{:S(2)}, u32[]{:S(2)}) collective-permute-start(bf16[1,16,1024]{2,1,0:T(8,128)(2,1)S(1)} %select_convert_fusion.1), channel_id=1, source_target_pairs={{0,16},{16,0},{1,17},{17,1},{2,18},{18,2},{3,19},{19,3},{4,20},{20... | collective-permute-start | bytes 98312 | tf_op jit(solution)/shard_map/ppermute | solution.py:327
  175.6 7.3 %collective-permute-start.11 = (bf16[4,1024]{1,0:T(4,128)(2,1)S(1)}, bf16[4,1024]{1,0:T(4,128)(2,1)S(1)}, u32[]{:S(2)}, u32[]{:S(2)}) collective-permute-start(bf16[4,1024]{1,0:T(4,128)(2,1)S(1)} %get-tuple-element.75), channel_id=1, source_target_pairs={{0,1},{1,0},{2,3},{3,2},{4,5},{5,4},{6,7},{7,6},{8,9},{9,8},{10,11... | collective-permute-start | bytes 24584 | tf_op jit(solution)/shard_map/ppermute | solution.py:341
  176.7 6.3 %collective-permute-start.12 = (bf16[4,1024]{1,0:T(4,128)(2,1)S(1)}, bf16[4,1024]{1,0:T(4,128)(2,1)S(1)}, u32[]{:S(2)}, u32[]{:S(2)}) collective-permute-start(bf16[4,1024]{1,0:T(4,128)(2,1)S(1)} %get-tuple-element.77), channel_id=1, source_target_pairs={{0,2},{1,3},{2,0},{3,1},{4,6},{5,7},{6,4},{7,5},{8,10},{9,11},{10,... | collective-permute-start | bytes 24584 | tf_op jit(solution)/shard_map/ppermute | solution.py:341
  179.0 4.9 %collective-permute-start.13 = (bf16[4,1024]{1,0:T(4,128)(2,1)S(1)}, bf16[4,1024]{1,0:T(4,128)(2,1)S(1)}, u32[]{:S(2)}, u32[]{:S(2)}) collective-permute-start(bf16[4,1024]{1,0:T(4,128)(2,1)S(1)} %get-tuple-element.76), channel_id=1, source_target_pairs={{0,3},{1,2},{2,1},{3,0},{4,7},{5,6},{6,5},{7,4},{8,11},{9,10},{10,... | collective-permute-start | bytes 24584 | tf_op jit(solution)/shard_map/ppermute | solution.py:341

commit v4 on v3

--- a/solution.py
+++ b/solution.py
@@ -215,7 +215,7 @@
     return pl.BlockSpec(shape, lambda i: (0,) * len(shape))
 
 
-def over_blocks(kernel, name, ins, outs, scratch, matmuls):
+def over_blocks(kernel, name, ins, outs, scratch, matmuls, room):
     return pl.pallas_call(
         kernel,
         grid=(SHARDS,),
@@ -223,7 +223,7 @@
         out_specs=[whole(o.shape) for o in outs],
         out_shape=outs,
         scratch_shapes=scratch,
-        compiler_params=pltpu.CompilerParams(vmem_limit_bytes=48 * 1024 * 1024),
+        compiler_params=pltpu.CompilerParams(vmem_limit_bytes=room << 20),
         cost_estimate=pl.CostEstimate(
             flops=matmuls * 2 * FRAME_ROWS * 4 * ROWS * HD,
             bytes_accessed=8 << 20,
@@ -245,7 +245,7 @@
         pltpu.VMEM((BLOCKS, HD, ROWS), BF),
         pltpu.VMEM((HD, SHARDS * PILS), BF),
     ]
-    return over_blocks(forward_kernel, "forward", ins, outs, scratch, 2)
+    return over_blocks(forward_kernel, "forward", ins, outs, scratch, 2, 60)
 
 
 def backward(ins):
@@ -260,7 +260,7 @@
         pltpu.VMEM((SHARDS * PILS, HD), F32),
         pltpu.VMEM((SHARDS * PILS, HD), F32),
     ]
-    return over_blocks(backward_kernel, "backward", ins, outs, scratch, 5)
+    return over_blocks(backward_kernel, "backward", ins, outs, scratch, 5, 60)
 
 
 def mix_kernel(att_ref, w_ref, mixed_ref):
@@ -362,7 +362,7 @@
     q, ga = pack_qg(q, g, w)
     q, kv = lax.optimization_barrier((q, kv))
     q = to_heads(q)
-    q, ga = lax.optimization_barrier((q, ga))
+    q, ga, left, right = lax.optimization_barrier((q, ga, left, right))
 
     label = jnp.pad(label, (HALF_SPAN, HALF_SPAN), constant_values=-1)
     label = lax.dynamic_slice_in_dim(label, frame * FRAME_ROWS, BLOCKS * ROWS, 0)

time: 186 us -> 176 us (0.946)
  waiting for transfers between devices: 59.2 us -> 49.4 us
  local copies, waits for them, and re-layouts: 15.2 us -> 7.9 us
  Pallas kernels: 42.3 us -> 46.5 us
  starting transfers between devices: 63.1 us -> 65.5 us
    all_to_all x6, waiting for transfers between devices: 24.1 us -> 14.4 us  [to_heads(): return lax.all_to_all(x, FRAME, 0, 0, tiled=True)]
    unnamed x39 -> x29, local copies, waits for them, and re-layouts: 13.8 us -> 4.89 us
    pallas_call x2, Pallas kernels: 20.5 us -> 24.8 us  [over_blocks(): pl.pallas_call(kernel, grid=(SHARDS,), in_specs=[whole(a.shape) for a in...]
    all_to_all x6, starting transfers between devices: 27.9 us -> 29.9 us  [to_heads(): return lax.all_to_all(x, FRAME, 0, 0, tiled=True)]
  transfers between devices with their start and end apart: 20 -> 20, of which waited for: 13 -> 12; matrix products, arithmetic and copies ran while one was open for 4% -> 6% of each run, Pallas kernels for 19% -> 23%
where the time goes in v4:
time: 176 us; the launch traced here: 175 us
  starting transfers between devices  65.5 us (37%)
  waiting for transfers between devices  49.4 us (28%)
  Pallas kernels  46.5 us (26%)
  local copies, waits for them, and re-layouts  7.9 us (4%)
  other arithmetic  4.62 us (3%)
    all_to_all x6, starting transfers between devices, to_heads(): return lax.all_to_all(x, FRAME, 0, 0, tiled=True)  29.9 us
    pallas_call x2, Pallas kernels, over_blocks(): pl.pallas_call(kernel, grid=(SHARDS,), in_specs=[whole(a.shape) for a in...  24.8 us
    all_to_all x6, waiting for transfers between devices, to_heads(): return lax.all_to_all(x, FRAME, 0, 0, tiled=True)  14.4 us
    ppermute x6, starting transfers between devices, scattered(): lax.ppermute(out, axes, [(j, j ^ apart) for j in range(count)]).astype(F32)  13.5 us
    ppermute x1, starting transfers between devices, on_device(): from_left = lax.ppermute(dright, FRAMES, ups)  13.4 us
    ppermute x2, waiting for transfers between devices, halved(): got = lax.ppermute(out, axis, [(j, j ^ 1 << bit) for j in range(count)])  12.3 us
    pallas_call x3, Pallas kernels, share_of(): pl.pallas_call(share_kernel, grid_spec=pltpu.PrefetchScalarGridSpec(num_s...  10.9 us
    ppermute x1, waiting for transfers between devices, on_device(): right = lax.ppermute(kv[0, :2 * ROWS], FRAMES, downs)  7.45 us
  transfers between devices with their start and end apart: 20, of which 12 were waited for; matrix products, arithmetic and copies ran while one was open for 6% of the time, Pallas kernels for 23%

profile of v4, /device:TPU:32, one launch (start us, length us, event | category | flops | bytes accessed | tf_op | source)
XLA Modules:
  0.0 174.8 jit_solution(17663747516723725192)
XLA Ops:
  0.6 2.2 %pack_kv.1 = bf16[8,544,128]{2,1,0:T(8,128)(2,1)} custom-call(bf16[256,1024]{1,0:T(8,128)(2,1)} %bitcast.71, bf16[256,1024]{1,0:T(8,128)(2,1)} %bitcast.72, s32[1,32]{1,0:T(1,128)} %s_ref.1), custom_call_target="tpu_custom_call" | custom-call | tf_op jit(solution)/shard_map/pack_kv/pallas_call | solution.py:48
  2.8 5.4 %all-to-all-start = ((bf16[8,544,128]{2,1,0:T(8,128)(2,1)}), bf16[8,544,128]{2,1,0:T(8,128)(2,1)S(1)}, u32[]{:S(2)}, u32[]{:S(2)}) async-start(bf16[8,544,128]{2,1,0:T(8,128)(2,1)} %pack_kv.1), calls=%async_computation | async-start | bytes 2228224 | tf_op jit(solution)/shard_map/all_to_all | solution.py:346
  8.2 4.5 %pack_qg.1 = (bf16[8,256,128]{2,1,0:T(8,128)(2,1)}, bf16[8,256,128]{2,1,0:T(8,128)(2,1)}) custom-call(bf16[256,1024]{1,0:T(8,128)(2,1)} %bitcast.73, bf16[256,1024]{1,0:T(8,128)(2,1)} %bitcast.61, bf16[1024,1024]{1,0:T(8,128)(2,1)} %w_ref.3), custom_call_target="tpu_custom_call" | custom-call | flops 536870912 | bytes 5242880 | tf_op jit(solution)/shard_map/pack_qg/pallas_call | solution.py:73
  12.7 11.0 %all-to-all-done.kv_ref = bf16[8,544,128]{2,1,0:T(8,128)(2,1)S(1)} async-done(((bf16[8,544,128]{2,1,0:T(8,128)(2,1)}), bf16[8,544,128]{2,1,0:T(8,128)(2,1)S(1)}, u32[]{:S(2)}, u32[]{:S(2)}) %all-to-all-start) | async-done | bytes 1114144 | tf_op jit(solution)/shard_map/all_to_all | solution.py:346
  23.7 3.8 %all-to-all-start.1 = ((bf16[8,256,128]{2,1,0:T(8,128)(2,1)}), bf16[8,256,128]{2,1,0:T(8,128)(2,1)S(1)}, u32[]{:S(2)}, u32[]{:S(2)}) async-start(bf16[8,256,128]{2,1,0:T(8,128)(2,1)} %get-tuple-element.37), calls=%async_computation.1 | async-start | bytes 1048576 | tf_op jit(solution)/shard_map/all_to_all | solution.py:346
  27.5 4.6 %collective-permute-start = (bf16[512,128]{1,0:T(8,128)(2,1)S(1)}, bf16[512,128]{1,0:T(8,128)(2,1)S(1)}, u32[]{:S(2)}, u32[]{:S(2)}) collective-permute-start(bf16[512,128]{1,0:T(8,128)(2,1)S(1)} %get-tuple-element.71), channel_id=1, source_target_pairs={{0,8},{8,16},{16,24},{1,9},{9,17},{17,25},{2,10},{10,18},{18,26},{... | collective-permute-start | bytes 393224 | tf_op jit(solution)/shard_map/ppermute | solution.py:360
  32.1 1.3 collective-permute-start.1
  33.4 2.8 %collective-permute-done.left_ref = bf16[512,128]{1,0:T(8,128)(2,1)S(1)} collective-permute-done((bf16[512,128]{1,0:T(8,128)(2,1)S(1)}, bf16[512,128]{1,0:T(8,128)(2,1)S(1)}, u32[]{:S(2)}, u32[]{:S(2)}) %collective-permute-start) | collective-permute-done | bytes 131104 | tf_op jit(solution)/shard_map/ppermute | solution.py:360
  36.2 7.4 %collective-permute-done.1.right_ref = bf16[512,128]{1,0:T(8,128)(2,1)S(1)} collective-permute-done((bf16[512,128]{1,0:T(8,128)(2,1)S(1)}, bf16[512,128]{1,0:T(8,128)(2,1)S(1)}, u32[]{:S(2)}, u32[]{:S(2)}) %collective-permute-start.1) | collective-permute-done | bytes 131104 | tf_op jit(solution)/shard_map/ppermute | solution.py:361
  43.7 0.0 all-to-all-done.1.q_ref
  43.7 5.5 %all-to-all-start.3 = ((bf16[8,256,128]{2,1,0:T(8,128)(2,1)}), bf16[8,256,128]{2,1,0:T(8,128)(2,1)S(1)}, u32[]{:S(2)}, u32[]{:S(2)}) async-start(bf16[8,256,128]{2,1,0:T(8,128)(2,1)} %get-tuple-element.43), calls=%async_computation.3 | async-start | bytes 1048576 | tf_op jit(solution)/shard_map/all_to_all | solution.py:346
  49.2 0.1 pad_dynamic-slice_fusion.1
  49.3 0.7 pad_dynamic-slice_fusion
  50.0 1.4 broadcast_in_dim.23.labk_ref
  51.4 10.4 %forward.1 = (bf16[8,256,128]{2,1,0:T(8,128)(2,1)}, f32[8,2,256]{2,1,0:T(2,128)}, bf16[256,128]{1,0:T(8,128)(2,1)}, bf16[256,128]{1,0:T(8,128)(2,1)}) custom-call(bf16[8,544,128]{2,1,0:T(8,128)(2,1)} %copy-done.3, bf16[8,256,128]{2,1,0:T(8,128)(2,1)} %copy-done.5, bf16[512,128]{1,0:T(8,128)(2,1)} %copy-done.9, bf16[512,128]{1,0:T(8,128)(2,1)} %copy-done.10, ...), custom_call_target="tpu_custom_call" | custom-call | flops 1073741824 | bytes 8388608 | tf_op jit(solution)/shard_map/forward/pallas_call | solution.py:219
  61.8 0.0 all-to-all-done.3.ga_ref
  61.8 0.0 copy-start.6
  61.8 5.7 %all-to-all-start.2 = ((bf16[8,256,128]{2,1,0:T(8,128)(2,1)}), bf16[8,256,128]{2,1,0:T(8,128)(2,1)S(1)}, u32[]{:S(2)}, u32[]{:S(2)}) async-start(bf16[8,256,128]{2,1,0:T(8,128)(2,1)} %get-tuple-element.42.att_ref), calls=%async_computation.2 | async-start | bytes 1048576 | tf_op jit(solution)/shard_map/all_to_all | solution.py:346
  67.5 0.5 multiply_add_fusion.heads_ref
  68.0 14.4 %backward.1 = (bf16[8,256,128]{2,1,0:T(8,128)(2,1)}, bf16[8,512,128]{2,1,0:T(8,128)(2,1)}, bf16[512,128]{1,0:T(8,128)(2,1)}, bf16[512,128]{1,0:T(8,128)(2,1)}) custom-call(bf16[8,544,128]{2,1,0:T(8,128)(2,1)} %copy-done.3, bf16[8,256,128]{2,1,0:T(8,128)(2,1)} %copy-done.5, bf16[512,128]{1,0:T(8,128)(2,1)} %copy-done.9, bf16[512,128]{1,0:T(8,128)(2,1)} %copy-done.10, ...), custom_call_target="tpu_custom_call" | custom-call | flops 2684354560 | bytes 8388608 | tf_op jit(solution)/shard_map/backward/pallas_call | solution.py:219
  82.4 0.0 copy-start
  82.4 0.8 copy-done
  83.2 4.5 %share.3 = bf16[4,128,1024]{2,1,0:T(8,128)(2,1)} custom-call(s32[4]{0:T(128)} %multiply_add_fusion.heads_ref, bf16[8,256,128]{2,1,0:T(8,128)(2,1)} %copy-done, bf16[256,1024]{1,0:T(8,128)(2,1)} %bitcast.62), custom_call_target="tpu_custom_call" | custom-call | flops 268435456 | bytes 2097152 | tf_op jit(solution)/shard_map/share/pallas_call | solution.py:304
  87.8 13.4 %collective-permute-start.3 = (bf16[512,128]{1,0:T(8,128)(2,1)S(1)}, bf16[512,128]{1,0:T(8,128)(2,1)S(1)}, u32[]{:S(2)}, u32[]{:S(2)}) collective-permute-start(bf16[512,128]{1,0:T(8,128)(2,1)S(1)} %copy-done.12), channel_id=1, source_target_pairs={{0,8},{8,16},{16,24},{1,9},{9,17},{17,25},{2,10},{10,18},{18,26},{... | collective-permute-start | bytes 393224 | tf_op jit(solution)/shard_map/ppermute | solution.py:379
  101.2 1.3 collective-permute-start.4
  102.5 0.5 fusion.13.heads_ref
  103.0 1.0 copy-done.1
  104.0 3.1 %share.5 = bf16[2,128,1024]{2,1,0:T(8,128)(2,1)} custom-call(s32[2]{0:T(128)} %fusion.13.heads_ref, bf16[8,256,128]{2,1,0:T(8,128)(2,1)} %copy-done, bf16[256,1024]{1,0:T(8,128)(2,1)} %bitcast.63, bf16[4,128,1024]{2,1,0:T(8,128)(2,1)} %copy-done.1), custom_call_target="tpu_custom_call" | custom-call | flops 134217728 | bytes 2097152 | tf_op jit(solution)/shard_map/share/pallas_call | solution.py:304
  107.1 0.0 collective-permute-done.3
  107.1 3.0 %collective-permute-done.4 = bf16[512,128]{1,0:T(8,128)(2,1)S(1)} collective-permute-done((bf16[512,128]{1,0:T(8,128)(2,1)S(1)}, bf16[512,128]{1,0:T(8,128)(2,1)S(1)}, u32[]{:S(2)}, u32[]{:S(2)}) %collective-permute-start.4) | collective-permute-done | bytes 131104 | tf_op jit(solution)/shard_map/ppermute | solution.py:378
  110.2 0.5 fusion.14.heads_ref
  110.7 0.1 slice.51
  110.8 0.0 copy-done.8
  110.8 5.1 %all-to-all-start.4 = ((bf16[8,256,128]{2,1,0:T(8,128)(2,1)}), bf16[8,256,128]{2,1,0:T(8,128)(2,1)S(1)}, u32[]{:S(2)}, u32[]{:S(2)}) async-start(bf16[8,256,128]{2,1,0:T(8,128)(2,1)} %get-tuple-element.55), calls=%async_computation.4 | async-start | bytes 1048576 | tf_op jit(solution)/shard_map/all_to_all | solution.py:346
  115.9 1.0 fusion.1
  116.9 3.2 %share.4 = f32[2,128,1024]{2,1,0:T(8,128)} custom-call(s32[2]{0:T(128)} %fusion.14.heads_ref, bf16[8,256,128]{2,1,0:T(8,128)(2,1)} %copy-done, bf16[256,1024]{1,0:T(8,128)(2,1)} %bitcast.64, bf16[4,128,1024]{2,1,0:T(8,128)(2,1)} %copy-done.1), custom_call_target="tpu_custom_call" | custom-call | flops 134217728 | bytes 2097152 | tf_op jit(solution)/shard_map/share/pallas_call | solution.py:304
  120.1 1.1 pad_maximum_fusion
  121.3 3.0 %collective-permute-done.5 = bf16[2,128,1024]{2,1,0:T(8,128)(2,1)S(1)} collective-permute-done((bf16[2,128,1024]{2,1,0:T(8,128)(2,1)}, bf16[2,128,1024]{2,1,0:T(8,128)(2,1)S(1)}, u32[]{:S(2)}, u32[]{:S(2)}) %collective-permute-start.5) | collective-permute-done | bytes 524320 | tf_op jit(solution)/shard_map/ppermute | solution.py:389
  124.3 0.1 convert_add_fusion
  124.5 0.7 all-to-all-done.4
  125.2 4.4 %all-to-all-start.5 = ((bf16[8,512,128]{2,1,0:T(8,128)(2,1)}), bf16[8,512,128]{2,1,0:T(8,128)(2,1)S(1)}, u32[]{:S(2)}, u32[]{:S(2)}) async-start(bf16[8,512,128]{2,1,0:T(8,128)(2,1)} %pad_maximum_fusion), calls=%async_computation.5 | async-start | bytes 2097152 | tf_op jit(solution)/shard_map/all_to_all | solution.py:346
  129.6 1.4 collective-permute-start.6
  131.0 4.2 %mix.1 = bf16[256,1024]{1,0:T(8,128)(2,1)} custom-call(bf16[8,256,128]{2,1,0:T(8,128)(2,1)} %copy-done, bf16[1024,1024]{1,0:T(8,128)(2,1)} %w_ref.3), custom_call_target="tpu_custom_call" | custom-call | flops 536870912 | bytes 3145728 | tf_op jit(solution)/shard_map/mix/pallas_call | solution.py:273
  135.2 5.7 %collective-permute-done.6 = bf16[1,128,1024]{2,1,0:T(8,128)(2,1)S(1)} collective-permute-done((bf16[1,128,1024]{2,1,0:T(8,128)(2,1)S(1)}, bf16[1,128,1024]{2,1,0:T(8,128)(2,1)S(1)}, u32[]{:S(2)}, u32[]{:S(2)}) %collective-permute-start.6) | collective-permute-done | bytes 262176 | tf_op jit(solution)/shard_map/ppermute | solution.py:327
  141.0 0.1 add_bitcast_fusion
  141.0 2.6 %all-to-all-done.5 = bf16[8,512,128]{2,1,0:T(8,128)(2,1)S(1)} async-done(((bf16[8,512,128]{2,1,0:T(8,128)(2,1)}), bf16[8,512,128]{2,1,0:T(8,128)(2,1)S(1)}, u32[]{:S(2)}, u32[]{:S(2)}) %all-to-all-start.5) | async-done | bytes 1048608 | tf_op jit(solution)/shard_map/all_to_all | solution.py:346
  143.7 1.6 collective-permute-start.7
  145.3 7.2 %collective-permute-start.8 = (bf16[2,16,1024]{2,1,0:T(8,128)(2,1)S(1)}, bf16[2,16,1024]{2,1,0:T(8,128)(2,1)S(1)}, u32[]{:S(2)}, u32[]{:S(2)}) collective-permute-start(bf16[2,16,1024]{2,1,0:T(8,128)(2,1)S(1)} %get-tuple-element.78), channel_id=1, source_target_pairs={{0,8},{4,12},{8,0},{12,4},{1,9},{5,13},{9,1},{13,5},{2,10},{6,14},... | collective-permute-start | bytes 196616 | tf_op jit(solution)/shard_map/ppermute | solution.py:341
  152.5 3.0 %collective-permute-done.8 = bf16[2,16,1024]{2,1,0:T(8,128)(2,1)S(1)} collective-permute-done((bf16[2,16,1024]{2,1,0:T(8,128)(2,1)S(1)}, bf16[2,16,1024]{2,1,0:T(8,128)(2,1)S(1)}, u32[]{:S(2)}, u32[]{:S(2)}) %collective-permute-start.8) | collective-permute-done | bytes 65568 | tf_op jit(solution)/shard_map/ppermute | solution.py:341
  155.5 2.4 %collective-permute-done.9 = bf16[2,16,1024]{2,1,0:T(8,128)(2,1)S(1)} collective-permute-done((bf16[2,16,1024]{2,1,0:T(8,128)(2,1)S(1)}, bf16[2,16,1024]{2,1,0:T(8,128)(2,1)S(1)}, u32[]{:S(2)}, u32[]{:S(2)}) %collective-permute-start.9) | collective-permute-done | bytes 65568 | tf_op jit(solution)/shard_map/ppermute | solution.py:341
  158.0 0.1 collective-permute-start.10
  158.1 0.2 copy.14
  158.3 1.0 copy.19
  159.3 6.6 %collective-permute-done.10 = bf16[1,16,1024]{2,1,0:T(8,128)(2,1)S(1)} collective-permute-done((bf16[1,16,1024]{2,1,0:T(8,128)(2,1)S(1)}, bf16[1,16,1024]{2,1,0:T(8,128)(2,1)S(1)}, u32[]{:S(2)}, u32[]{:S(2)}) %collective-permute-start.10) | collective-permute-done | bytes 32800 | tf_op jit(solution)/shard_map/ppermute | solution.py:327
  166.0 1.1 collective-permute-start.11
  167.0 2.3 %collective-permute-start.12 = (bf16[4,1024]{1,0:T(4,128)(2,1)S(1)}, bf16[4,1024]{1,0:T(4,128)(2,1)S(1)}, u32[]{:S(2)}, u32[]{:S(2)}) collective-permute-start(bf16[4,1024]{1,0:T(4,128)(2,1)S(1)} %get-tuple-element.81), channel_id=1, source_target_pairs={{0,2},{1,3},{2,0},{3,1},{4,6},{5,7},{6,4},{7,5},{8,10},{9,11},{10,... | collective-permute-start | bytes 24584 | tf_op jit(solution)/shard_map/ppermute | solution.py:341
  169.3 1.4 collective-permute-start.13
  170.8 0.1 slice_bitcast_fusion
  170.9 0.2 copy.15
  171.1 1.0 copy.20
  172.1 0.2 copy.16
  172.3 1.0 copy.21
  173.3 0.9 collective-permute-done.13
  174.2 0.6 fusion.9
  (38 shorter events, 0.3 us)
Async XLA Ops:
  2.8 20.9 %all-to-all-start = ((bf16[8,544,128]{2,1,0:T(8,128)(2,1)}), bf16[8,544,128]{2,1,0:T(8,128)(2,1)S(1)}, u32[]{:S(2)}, u32[]{:S(2)}) async-start(bf16[8,544,128]{2,1,0:T(8,128)(2,1)} %pack_kv.1), calls=%async_computation | async-start | bytes 2228224 | tf_op jit(solution)/shard_map/all_to_all | solution.py:346
  23.7 20.0 %copy-start.3 = (bf16[8,544,128]{2,1,0:T(8,128)(2,1)}, bf16[8,544,128]{2,1,0:T(8,128)(2,1)S(1)}, u32[]{:S(2)}) copy-start(bf16[8,544,128]{2,1,0:T(8,128)(2,1)S(1)} %all-to-all-done.kv_ref) | copy-start | bytes 3342340
  23.7 25.5 %copy-start.7 = (s32[8192]{0:T(1024)S(1)}, s32[8192]{0:T(1024)}, u32[]{:S(2)}) copy-start(s32[8192]{0:T(1024)} %param.13) | copy-start | bytes 98308
  23.7 20.0 %all-to-all-start.1 = ((bf16[8,256,128]{2,1,0:T(8,128)(2,1)}), bf16[8,256,128]{2,1,0:T(8,128)(2,1)S(1)}, u32[]{:S(2)}, u32[]{:S(2)}) async-start(bf16[8,256,128]{2,1,0:T(8,128)(2,1)} %get-tuple-element.37), calls=%async_computation.1 | async-start | bytes 1048576 | tf_op jit(solution)/shard_map/all_to_all | solution.py:346
  27.5 8.7 %collective-permute-start = (bf16[512,128]{1,0:T(8,128)(2,1)S(1)}, bf16[512,128]{1,0:T(8,128)(2,1)S(1)}, u32[]{:S(2)}, u32[]{:S(2)}) collective-permute-start(bf16[512,128]{1,0:T(8,128)(2,1)S(1)} %get-tuple-element.71), channel_id=1, source_target_pairs={{0,8},{8,16},{16,24},{1,9},{9,17},{17,25},{2,10},{10,18},{18,26},{... | collective-permute-start | bytes 393224 | tf_op jit(solution)/shard_map/ppermute | solution.py:360
  32.1 11.5 %collective-permute-start.1 = (bf16[512,128]{1,0:T(8,128)(2,1)S(1)}, bf16[512,128]{1,0:T(8,128)(2,1)S(1)}, u32[]{:S(2)}, u32[]{:S(2)}) collective-permute-start(bf16[512,128]{1,0:T(8,128)(2,1)S(1)} %get-tuple-element.70), channel_id=1, source_target_pairs={{8,0},{16,8},{24,16},{9,1},{17,9},{25,17},{10,2},{18,10},{26,18},{... | collective-permute-start | bytes 393224 | tf_op jit(solution)/shard_map/ppermute | solution.py:361
  36.2 15.2 %copy-start.9 = (bf16[512,128]{1,0:T(8,128)(2,1)}, bf16[512,128]{1,0:T(8,128)(2,1)S(1)}, u32[]{:S(2)}) copy-start(bf16[512,128]{1,0:T(8,128)(2,1)S(1)} %collective-permute-done.left_ref) | copy-start | bytes 393220
  43.7 7.7 %copy-start.10 = (bf16[512,128]{1,0:T(8,128)(2,1)}, bf16[512,128]{1,0:T(8,128)(2,1)S(1)}, u32[]{:S(2)}) copy-start(bf16[512,128]{1,0:T(8,128)(2,1)S(1)} %collective-permute-done.1.right_ref) | copy-start | bytes 393220
  43.7 7.7 %copy-start.5 = (bf16[8,256,128]{2,1,0:T(8,128)(2,1)}, bf16[8,256,128]{2,1,0:T(8,128)(2,1)S(1)}, u32[]{:S(2)}) copy-start(bf16[8,256,128]{2,1,0:T(8,128)(2,1)S(1)} %all-to-all-done.1.q_ref) | copy-start | bytes 1572868
  43.7 18.1 %all-to-all-start.3 = ((bf16[8,256,128]{2,1,0:T(8,128)(2,1)}), bf16[8,256,128]{2,1,0:T(8,128)(2,1)S(1)}, u32[]{:S(2)}, u32[]{:S(2)}) async-start(bf16[8,256,128]{2,1,0:T(8,128)(2,1)} %get-tuple-element.43), calls=%async_computation.3 | async-start | bytes 1048576 | tf_op jit(solution)/shard_map/all_to_all | solution.py:346
  61.8 6.2 %copy-start.6 = (bf16[8,256,128]{2,1,0:T(8,128)(2,1)}, bf16[8,256,128]{2,1,0:T(8,128)(2,1)S(1)}, u32[]{:S(2)}) copy-start(bf16[8,256,128]{2,1,0:T(8,128)(2,1)S(1)} %all-to-all-done.3.ga_ref) | copy-start | bytes 1572868
  61.8 20.6 %all-to-all-start.2 = ((bf16[8,256,128]{2,1,0:T(8,128)(2,1)}), bf16[8,256,128]{2,1,0:T(8,128)(2,1)S(1)}, u32[]{:S(2)}, u32[]{:S(2)}) async-start(bf16[8,256,128]{2,1,0:T(8,128)(2,1)} %get-tuple-element.42.att_ref), calls=%async_computation.2 | async-start | bytes 1048576 | tf_op jit(solution)/shard_map/all_to_all | solution.py:346
  82.4 5.4 %copy-start.12 = (bf16[512,128]{1,0:T(8,128)(2,1)S(1)}, bf16[512,128]{1,0:T(8,128)(2,1)}, u32[]{:S(2)}) copy-start(bf16[512,128]{1,0:T(8,128)(2,1)} %get-tuple-element.52) | copy-start | bytes 393220
  82.4 18.7 %copy-start.11 = (bf16[512,128]{1,0:T(8,128)(2,1)S(1)}, bf16[512,128]{1,0:T(8,128)(2,1)}, u32[]{:S(2)}) copy-start(bf16[512,128]{1,0:T(8,128)(2,1)} %get-tuple-element.53) | copy-start | bytes 393220
  82.4 0.8 copy-start
  87.8 15.2 %collective-permute-start.2 = (bf16[4,128,1024]{2,1,0:T(8,128)(2,1)}, bf16[4,128,1024]{2,1,0:T(8,128)(2,1)S(1)}, u32[]{:S(2)}, u32[]{:S(2)}) collective-permute-start(bf16[4,128,1024]{2,1,0:T(8,128)(2,1)} %share.3), channel_id=1, source_target_pairs={{0,32},{32,0},{1,33},{33,1},{2,34},{34,2},{3,35},{35,3},{4,36},{36... | collective-permute-start | bytes 3145736 | tf_op jit(solution)/shard_map/ppermute | solution.py:384
  87.8 19.4 %collective-permute-start.3 = (bf16[512,128]{1,0:T(8,128)(2,1)S(1)}, bf16[512,128]{1,0:T(8,128)(2,1)S(1)}, u32[]{:S(2)}, u32[]{:S(2)}) collective-permute-start(bf16[512,128]{1,0:T(8,128)(2,1)S(1)} %copy-done.12), channel_id=1, source_target_pairs={{0,8},{8,16},{16,24},{1,9},{9,17},{17,25},{2,10},{10,18},{18,26},{... | collective-permute-start | bytes 393224 | tf_op jit(solution)/shard_map/ppermute | solution.py:379
  101.2 9.0 %collective-permute-start.4 = (bf16[512,128]{1,0:T(8,128)(2,1)S(1)}, bf16[512,128]{1,0:T(8,128)(2,1)S(1)}, u32[]{:S(2)}, u32[]{:S(2)}) collective-permute-start(bf16[512,128]{1,0:T(8,128)(2,1)S(1)} %copy-done.11), channel_id=1, source_target_pairs={{8,0},{16,8},{24,16},{9,1},{17,9},{25,17},{10,2},{18,10},{26,18},{... | collective-permute-start | bytes 393224 | tf_op jit(solution)/shard_map/ppermute | solution.py:378
  103.0 7.8 %copy-start.4 = (bf16[8,512,128]{2,1,0:T(8,128)(2,1)S(1)}, bf16[8,512,128]{2,1,0:T(8,128)(2,1)}, u32[]{:S(2)}) copy-start(bf16[8,512,128]{2,1,0:T(8,128)(2,1)} %get-tuple-element.56) | copy-start | bytes 3145732
  103.0 1.0 copy-start.1
  110.2 0.7 copy-start.8
  110.2 14.1 %collective-permute-start.5 = (bf16[2,128,1024]{2,1,0:T(8,128)(2,1)}, bf16[2,128,1024]{2,1,0:T(8,128)(2,1)S(1)}, u32[]{:S(2)}, u32[]{:S(2)}) collective-permute-start(bf16[2,128,1024]{2,1,0:T(8,128)(2,1)} %share.5), channel_id=1, source_target_pairs={{0,64},{64,0},{128,192},{192,128},{1,65},{65,1},{129,193},{193,129... | collective-permute-start | bytes 1572872 | tf_op jit(solution)/shard_map/ppermute | solution.py:389
  110.8 14.3 %all-to-all-start.4 = ((bf16[8,256,128]{2,1,0:T(8,128)(2,1)}), bf16[8,256,128]{2,1,0:T(8,128)(2,1)S(1)}, u32[]{:S(2)}, u32[]{:S(2)}) async-start(bf16[8,256,128]{2,1,0:T(8,128)(2,1)} %get-tuple-element.55), calls=%async_computation.4 | async-start | bytes 1048576 | tf_op jit(solution)/shard_map/all_to_all | solution.py:346
  120.1 4.2 %copy-start.2 = (f32[2,128,1024]{2,1,0:T(8,128)S(1)}, f32[2,128,1024]{2,1,0:T(8,128)}, u32[]{:S(2)}) copy-start(f32[2,128,1024]{2,1,0:T(8,128)} %share.4) | copy-start | bytes 3145732
  125.2 18.5 %all-to-all-start.5 = ((bf16[8,512,128]{2,1,0:T(8,128)(2,1)}), bf16[8,512,128]{2,1,0:T(8,128)(2,1)S(1)}, u32[]{:S(2)}, u32[]{:S(2)}) async-start(bf16[8,512,128]{2,1,0:T(8,128)(2,1)} %pad_maximum_fusion), calls=%async_computation.5 | async-start | bytes 2097152 | tf_op jit(solution)/shard_map/all_to_all | solution.py:346
  129.6 11.3 %collective-permute-start.6 = (bf16[1,128,1024]{2,1,0:T(8,128)(2,1)S(1)}, bf16[1,128,1024]{2,1,0:T(8,128)(2,1)S(1)}, u32[]{:S(2)}, u32[]{:S(2)}) collective-permute-start(bf16[1,128,1024]{2,1,0:T(8,128)(2,1)S(1)} %select_convert_fusion), channel_id=1, source_target_pairs={{0,128},{64,192},{128,0},{192,64},{1,129},{65,193},{129,1},{193,65... | collective-permute-start | bytes 786440 | tf_op jit(solution)/shard_map/ppermute | solution.py:327
  143.7 8.8 %collective-permute-start.7 = (bf16[2,16,1024]{2,1,0:T(8,128)(2,1)S(1)}, bf16[2,16,1024]{2,1,0:T(8,128)(2,1)S(1)}, u32[]{:S(2)}, u32[]{:S(2)}) collective-permute-start(bf16[2,16,1024]{2,1,0:T(8,128)(2,1)S(1)} %get-tuple-element.76), channel_id=1, source_target_pairs={{0,4},{4,0},{8,12},{12,8},{1,5},{5,1},{9,13},{13,9},{2,6},{6,2},{1... | collective-permute-start | bytes 196616 | tf_op jit(solution)/shard_map/ppermute | solution.py:341
  145.3 10.2 %collective-permute-start.8 = (bf16[2,16,1024]{2,1,0:T(8,128)(2,1)S(1)}, bf16[2,16,1024]{2,1,0:T(8,128)(2,1)S(1)}, u32[]{:S(2)}, u32[]{:S(2)}) collective-permute-start(bf16[2,16,1024]{2,1,0:T(8,128)(2,1)S(1)} %get-tuple-element.78), channel_id=1, source_target_pairs={{0,8},{4,12},{8,0},{12,4},{1,9},{5,13},{9,1},{13,5},{2,10},{6,14},... | collective-permute-start | bytes 196616 | tf_op jit(solution)/shard_map/ppermute | solution.py:341
  152.5 5.5 %collective-permute-start.9 = (bf16[2,16,1024]{2,1,0:T(8,128)(2,1)S(1)}, bf16[2,16,1024]{2,1,0:T(8,128)(2,1)S(1)}, u32[]{:S(2)}, u32[]{:S(2)}) collective-permute-start(bf16[2,16,1024]{2,1,0:T(8,128)(2,1)S(1)} %get-tuple-element.77), channel_id=1, source_target_pairs={{0,12},{4,8},{8,4},{12,0},{1,13},{5,9},{9,5},{13,1},{2,14},{6,10},... | collective-permute-start | bytes 196616 | tf_op jit(solution)/shard_map/ppermute | solution.py:341
  158.0 7.9 %collective-permute-start.10 = (bf16[1,16,1024]{2,1,0:T(8,128)(2,1)S(1)}, bf16[1,16,1024]{2,1,0:T(8,128)(2,1)S(1)}, u32[]{:S(2)}, u32[]{:S(2)}) collective-permute-start(bf16[1,16,1024]{2,1,0:T(8,128)(2,1)S(1)} %select_convert_fusion.1), channel_id=1, source_target_pairs={{0,16},{16,0},{1,17},{17,1},{2,18},{18,2},{3,19},{19,3},{4,20},{20... | collective-permute-start | bytes 98312 | tf_op jit(solution)/shard_map/ppermute | solution.py:327
  166.0 7.3 %collective-permute-start.11 = (bf16[4,1024]{1,0:T(4,128)(2,1)S(1)}, bf16[4,1024]{1,0:T(4,128)(2,1)S(1)}, u32[]{:S(2)}, u32[]{:S(2)}) collective-permute-start(bf16[4,1024]{1,0:T(4,128)(2,1)S(1)} %get-tuple-element.79), channel_id=1, source_target_pairs={{0,1},{1,0},{2,3},{3,2},{4,5},{5,4},{6,7},{7,6},{8,9},{9,8},{10,11... | collective-permute-start | bytes 24584 | tf_op jit(solution)/shard_map/ppermute | solution.py:341
  167.0 6.3 %collective-permute-start.12 = (bf16[4,1024]{1,0:T(4,128)(2,1)S(1)}, bf16[4,1024]{1,0:T(4,128)(2,1)S(1)}, u32[]{:S(2)}, u32[]{:S(2)}) collective-permute-start(bf16[4,1024]{1,0:T(4,128)(2,1)S(1)} %get-tuple-element.81), channel_id=1, source_target_pairs={{0,2},{1,3},{2,0},{3,1},{4,6},{5,7},{6,4},{7,5},{8,10},{9,11},{10,... | collective-permute-start | bytes 24584 | tf_op jit(solution)/shard_map/ppermute | solution.py:341
  169.3 4.9 %collective-permute-start.13 = (bf16[4,1024]{1,0:T(4,128)(2,1)S(1)}, bf16[4,1024]{1,0:T(4,128)(2,1)S(1)}, u32[]{:S(2)}, u32[]{:S(2)}) collective-permute-start(bf16[4,1024]{1,0:T(4,128)(2,1)S(1)} %get-tuple-element.80), channel_id=1, source_target_pairs={{0,3},{1,2},{2,1},{3,0},{4,7},{5,6},{6,5},{7,4},{8,11},{9,10},{10,... | collective-permute-start | bytes 24584 | tf_op jit(solution)/shard_map/ppermute | solution.py:341

commit v5 on v4

--- a/solution.py
+++ b/solution.py
@@ -59,12 +59,12 @@
     )(k, v, comb_shift)
 
 
-def pack_qg_kernel(q_ref, g_ref, w_ref, qo_ref, go_ref):
+def pack_qg_kernel(q_ref, g_ref, w_ref, o_ref):
     grad = mm(g_ref[...], w_ref[...], 1, 1).astype(BF)
-    for n in range(qo_ref.shape[0]):
+    for n in range(o_ref.shape[0]):
         columns = slice(n * HD, (n + 1) * HD)
-        qo_ref[n] = q_ref[:, columns]
-        go_ref[n] = grad[:, columns]
+        o_ref[n, :ROWS] = q_ref[:, columns]
+        o_ref[n, ROWS:] = grad[:, columns]
 
 
 def pack_qg(q, g, w):
@@ -78,8 +78,8 @@
             pl.BlockSpec((ROWS, width), lambda h: (0, 0)),
             pl.BlockSpec((some * HD, width), lambda h: (h, 0)),
         ],
-        out_specs=[pl.BlockSpec((some, ROWS, HD), lambda h: (h, 0, 0))] * 2,
-        out_shape=[jax.ShapeDtypeStruct((HEADS, ROWS, HD), BF)] * 2,
+        out_specs=pl.BlockSpec((some, 2 * ROWS, HD), lambda h: (h, 0, 0)),
+        out_shape=jax.ShapeDtypeStruct((HEADS, 2 * ROWS, HD), BF),
         cost_estimate=pl.CostEstimate(
             flops=2 * ROWS * width * width, bytes_accessed=5 << 20, transcendentals=0
         ),
@@ -94,13 +94,13 @@
     return jnp.concatenate(picks, axis=1).astype(BF)
 
 
-def window_scores(i, q, k_all, k_pil, labk_ref, labq_ref):
-    label_q = labq_ref[i]
+def window_scores(i, q, k_all, k_pil, label_ref, label_col):
+    label_q = label_ref[i + 1]
     key_at = lax.broadcasted_iota(jnp.int32, (ROWS, ROWS), 0)
     query_at = lax.broadcasted_iota(jnp.int32, (ROWS, ROWS), 1)
     scores = []
     for part in range(3):
-        admit = labk_ref[i + part][:, :1] == label_q
+        admit = label_col[i + part][:, :1] == label_q
         if part == 0:
             admit = admit & (key_at >= query_at)
         elif part == 2:
@@ -118,9 +118,9 @@
 
 
 def forward_kernel(
-    kv_ref, q_ref, left_ref, right_ref, labk_ref, labq_ref,
+    kv_ref, q_ref, left_ref, right_ref, label_ref,
     att_ref, stat_ref, k_pil, v_pil,
-    k_all, vt_all, vt_pil,
+    k_all, vt_all, vt_pil, label_col,
 ):
     i = pl.program_id(0)
 
@@ -129,6 +129,7 @@
         for b in range(BLOCKS):
             kb, vb = block_of(b, kv_ref, left_ref, right_ref)
             k_all[b] = kb
+            label_col[b] = jnp.broadcast_to(label_ref[b], (HD, ROWS)).T
             vt_all[b] = vb.T
             if 0 < b < BLOCKS - 1:
                 pick = pilot_pick(kv_ref[b - 1, 2 * ROWS :])
@@ -137,7 +138,7 @@
                 v_pil[at] = mm(pick, vb, 1, 0).astype(BF)
         vt_pil[...] = v_pil[...].T
 
-    scores = window_scores(i, q_ref[i], k_all, k_pil, labk_ref, labq_ref)
+    scores = window_scores(i, q_ref[i], k_all, k_pil, label_ref, label_col)
     factor = SCALE * LOG2E
     top = functools.reduce(jnp.maximum, [jnp.max(s, axis=0, keepdims=True) for s in scores])
     top = top * factor
@@ -152,9 +153,9 @@
 
 
 def backward_kernel(
-    kv_ref, q_ref, left_ref, right_ref, labk_ref, labq_ref, ga_ref, att_ref, stat_ref, k_pil, v_pil,
+    kv_ref, q_ref, left_ref, right_ref, label_ref, ga_ref, att_ref, stat_ref, k_pil, v_pil,
     dq_ref, dkv_ref, dleft_ref, dright_ref,
-    k_all, v_all, kt_all, kt_pil, dk_all, dv_all, dk_pil, dv_pil,
+    k_all, v_all, kt_all, kt_pil, dk_all, dv_all, dk_pil, dv_pil, label_col,
 ):
     i = pl.program_id(0)
 
@@ -163,6 +164,7 @@
         for b in range(BLOCKS):
             kb, vb = block_of(b, kv_ref, left_ref, right_ref)
             k_all[b] = kb
+            label_col[b] = jnp.broadcast_to(label_ref[b], (HD, ROWS)).T
             v_all[b] = vb
             kt_all[b] = kb.T
         kt_pil[...] = k_pil[...].T
@@ -173,7 +175,7 @@
 
     q = q_ref[i]
     ga = ga_ref[i]
-    scores = window_scores(i, q, k_all, k_pil, labk_ref, labq_ref)
+    scores = window_scores(i, q, k_all, k_pil, label_ref, label_col)
     top, inverse = stat_ref[i][:1], stat_ref[i][1:]
     product = ga.astype(F32) * att_ref[i].astype(F32)
     delta = jnp.sum(product.T, axis=0, keepdims=True)
@@ -216,10 +218,13 @@
 
 
 def over_blocks(kernel, name, ins, outs, scratch, matmuls, room):
+    in_specs = [whole(a.shape) for a in ins]
+    for at, half in ((1, 0), (5, 1))[: len(ins) // 5]:
+        in_specs[at] = pl.BlockSpec((SHARDS, ROWS, HD), lambda i, half=half: (0, half, 0))
     return pl.pallas_call(
         kernel,
         grid=(SHARDS,),
-        in_specs=[whole(a.shape) for a in ins],
+        in_specs=in_specs,
         out_specs=[whole(o.shape) for o in outs],
         out_shape=outs,
         scratch_shapes=scratch,
@@ -244,6 +249,7 @@
         pltpu.VMEM((BLOCKS, ROWS, HD), BF),
         pltpu.VMEM((BLOCKS, HD, ROWS), BF),
         pltpu.VMEM((HD, SHARDS * PILS), BF),
+        pltpu.VMEM((BLOCKS, ROWS, HD), F32),
     ]
     return over_blocks(forward_kernel, "forward", ins, outs, scratch, 2, 60)
 
@@ -259,6 +265,7 @@
         pltpu.VMEM((BLOCKS, ROWS, HD), F32),
         pltpu.VMEM((SHARDS * PILS, HD), F32),
         pltpu.VMEM((SHARDS * PILS, HD), F32),
+        pltpu.VMEM((BLOCKS, ROWS, HD), F32),
     ]
     return over_blocks(backward_kernel, "backward", ins, outs, scratch, 5, 60)
 
@@ -359,21 +366,18 @@
     kv = to_heads(pack_kv(k, v, comb_shift))
     left = lax.ppermute(kv[SHARDS - 1, : 2 * ROWS], FRAMES, ups)
     right = lax.ppermute(kv[0, : 2 * ROWS], FRAMES, downs)
-    q, ga = pack_qg(q, g, w)
-    q, kv = lax.optimization_barrier((q, kv))
-    q = to_heads(q)
-    q, ga, left, right = lax.optimization_barrier((q, ga, left, right))
+    qg = pack_qg(q, g, w)
+    qg, kv = lax.optimization_barrier((qg, kv))
+    qg = to_heads(qg)
 
     label = jnp.pad(label, (HALF_SPAN, HALF_SPAN), constant_values=-1)
     label = lax.dynamic_slice_in_dim(label, frame * FRAME_ROWS, BLOCKS * ROWS, 0)
-    labk = jnp.broadcast_to(label.reshape(BLOCKS, ROWS, 1), (BLOCKS, ROWS, HD))
-    labq = label[HALF_SPAN : HALF_SPAN + FRAME_ROWS].reshape(SHARDS, 1, ROWS)
-
-    frame_ins = (kv, q, left, right, labk, labq)
+    label = label.astype(F32).reshape(BLOCKS, 1, ROWS)
+
+    frame_ins = (kv, qg, left, right, label)
     att, stats, k_pil, v_pil = forward(frame_ins)
-    ga = to_heads(ga)
     att_rows = to_heads(att)
-    dq, dkv, dleft, dright = backward(frame_ins + (ga, att, stats, k_pil, v_pil))
+    dq, dkv, dleft, dright = backward(frame_ins + (qg, att, stats, k_pil, v_pil))
     att_rows, dq, dkv, dleft, dright = lax.optimization_barrier((att_rows, dq, dkv, dleft, dright))
     from_right = lax.ppermute(dleft, FRAMES, downs)
     from_left = lax.ppermute(dright, FRAMES, ups)
@@ -384,7 +388,6 @@
     got = lax.ppermute(share, "c", [(0, 1), (1, 0)])
     mine = jnp.arange(2, dtype=jnp.int32) * 4 + core
     send = share_of(att_rows, g, mine + 2 * (1 - z_bit), got, BF)
-    send, from_left, from_right = lax.optimization_barrier((send, from_left, from_right))
     keep = share_of(att_rows, g, mine + 2 * z_bit, got, F32)
     got = lax.ppermute(send, "zl", [(j, j ^ 1) for j in range(4)])
     share = keep + got.astype(F32)

time: 176 us -> 171 us (0.972)
  waiting for transfers between devices: 49.4 us -> 45.5 us
    all_to_all x6 -> x5, starting transfers between devices: 29.9 us -> 22.6 us  [to_heads(): return lax.all_to_all(x, FRAME, 0, 0, tiled=True)]
    ppermute x1, waiting for transfers between devices: 2.79 us -> 7.74 us  [on_device(): left = lax.ppermute(kv[SHARDS - 1, :2 * ROWS], FRAMES, ups)]
    ppermute x2, waiting for transfers between devices: 12.3 us -> 7.59 us  [halved(): got = lax.ppermute(out, axis, [(j, j ^ 1 << bit) for j in range(count)])]
    ppermute x1, waiting for transfers between devices: 7.45 us -> 3.18 us  [on_device(): right = lax.ppermute(kv[0, :2 * ROWS], FRAMES, downs)]
    ppermute x2, starting transfers between devices: 1.48 us -> 5.58 us  [halved(): got = lax.ppermute(out, axis, [(j, j ^ 1 << bit) for j in range(count)])]
    ppermute x1, waiting for transfers between devices: 3.02 us -> 0.01 us  [on_device(): got = lax.ppermute(send, 'zl', [(j, j ^ 1) for j in range(4)])]
    all_to_all x6 -> x5, waiting for transfers between devices: 14.4 us -> 17 us  [to_heads(): return lax.all_to_all(x, FRAME, 0, 0, tiled=True)]
    ppermute x6, starting transfers between devices: 13.5 us -> 16.1 us  [scattered(): lax.ppermute(out, axes, [(j, j ^ apart) for j in range(count)]).astype(F32)]
  transfers between devices with their start and end apart: 20 -> 19, of which waited for: 12 -> 12; matrix products, arithmetic and copies ran while one was open for 6% -> 5% of each run, Pallas kernels for 23% -> 16%
where the time goes in v5:
time: 171 us; the launch traced here: 170 us
  starting transfers between devices  64 us (37%)
  Pallas kernels  46.6 us (27%)
  waiting for transfers between devices  45.5 us (27%)
  local copies, waits for them, and re-layouts  7.9 us (5%)
  other arithmetic  5.04 us (3%)
    pallas_call x2, Pallas kernels, over_blocks(): pl.pallas_call(kernel, grid=(SHARDS,), in_specs=in_specs, out_specs=[whol...  24.8 us
    all_to_all x5, starting transfers between devices, to_heads(): return lax.all_to_all(x, FRAME, 0, 0, tiled=True)  22.6 us
    all_to_all x5, waiting for transfers between devices, to_heads(): return lax.all_to_all(x, FRAME, 0, 0, tiled=True)  17 us
    ppermute x6, starting transfers between devices, scattered(): lax.ppermute(out, axes, [(j, j ^ apart) for j in range(count)]).astype(F32)  16.1 us
    ppermute x1, starting transfers between devices, on_device(): from_left = lax.ppermute(dright, FRAMES, ups)  12.2 us
    pallas_call x3, Pallas kernels, share_of(): pl.pallas_call(share_kernel, grid_spec=pltpu.PrefetchScalarGridSpec(num_s...  10.8 us
    ppermute x1, waiting for transfers between devices, on_device(): left = lax.ppermute(kv[SHARDS - 1, :2 * ROWS], FRAMES, ups)  7.74 us
    ppermute x2, waiting for transfers between devices, halved(): got = lax.ppermute(out, axis, [(j, j ^ 1 << bit) for j in range(count)])  7.59 us
  transfers between devices with their start and end apart: 19, of which 12 were waited for; matrix products, arithmetic and copies ran while one was open for 5% of the time, Pallas kernels for 16%

profile of v5, /device:TPU:32, one launch (start us, length us, event | category | flops | bytes accessed | tf_op | source)
XLA Modules:
  0.0 169.8 jit_solution(14337347306972914668)
XLA Ops:
  0.6 2.2 %pack_kv.1 = bf16[8,544,128]{2,1,0:T(8,128)(2,1)} custom-call(bf16[256,1024]{1,0:T(8,128)(2,1)} %bitcast.70, bf16[256,1024]{1,0:T(8,128)(2,1)} %bitcast.71, s32[1,32]{1,0:T(1,128)} %s_ref.1), custom_call_target="tpu_custom_call" | custom-call | tf_op jit(solution)/shard_map/pack_kv/pallas_call | solution.py:48
  2.8 5.4 %all-to-all-start = ((bf16[8,544,128]{2,1,0:T(8,128)(2,1)}), bf16[8,544,128]{2,1,0:T(8,128)(2,1)S(1)}, u32[]{:S(2)}, u32[]{:S(2)}) async-start(bf16[8,544,128]{2,1,0:T(8,128)(2,1)} %pack_kv.1), calls=%async_computation | async-start | bytes 2228224 | tf_op jit(solution)/shard_map/all_to_all | solution.py:353
  8.2 4.5 %pack_qg.1 = bf16[8,512,128]{2,1,0:T(8,128)(2,1)} custom-call(bf16[256,1024]{1,0:T(8,128)(2,1)} %bitcast.73, bf16[256,1024]{1,0:T(8,128)(2,1)} %bitcast.60, bf16[1024,1024]{1,0:T(8,128)(2,1)} %w_ref.3), custom_call_target="tpu_custom_call" | custom-call | flops 536870912 | bytes 5242880 | tf_op jit(solution)/shard_map/pack_qg/pallas_call | solution.py:73
  12.7 11.0 %all-to-all-done.kv_ref = bf16[8,544,128]{2,1,0:T(8,128)(2,1)S(1)} async-done(((bf16[8,544,128]{2,1,0:T(8,128)(2,1)}), bf16[8,544,128]{2,1,0:T(8,128)(2,1)S(1)}, u32[]{:S(2)}, u32[]{:S(2)}) %all-to-all-start) | async-done | bytes 1114144 | tf_op jit(solution)/shard_map/all_to_all | solution.py:353
  23.7 3.6 %all-to-all-start.1 = ((bf16[8,512,128]{2,1,0:T(8,128)(2,1)}), bf16[8,512,128]{2,1,0:T(8,128)(2,1)S(1)}, u32[]{:S(2)}, u32[]{:S(2)}) async-start(bf16[8,512,128]{2,1,0:T(8,128)(2,1)} %pack_qg.1), calls=%async_computation.1 | async-start | bytes 2097152 | tf_op jit(solution)/shard_map/all_to_all | solution.py:353
  27.4 4.6 %collective-permute-start = (bf16[512,128]{1,0:T(8,128)(2,1)S(1)}, bf16[512,128]{1,0:T(8,128)(2,1)S(1)}, u32[]{:S(2)}, u32[]{:S(2)}) collective-permute-start(bf16[512,128]{1,0:T(8,128)(2,1)S(1)} %get-tuple-element.53), channel_id=1, source_target_pairs={{0,8},{8,16},{16,24},{1,9},{9,17},{17,25},{2,10},{10,18},{18,26},{... | collective-permute-start | bytes 393224 | tf_op jit(solution)/shard_map/ppermute | solution.py:367
  32.0 1.3 collective-permute-start.1
  33.3 0.1 fusion.10
  33.4 0.6 reshape.25.label_ref
  34.0 7.7 %collective-permute-done.left_ref = bf16[512,128]{1,0:T(8,128)(2,1)S(1)} collective-permute-done((bf16[512,128]{1,0:T(8,128)(2,1)S(1)}, bf16[512,128]{1,0:T(8,128)(2,1)S(1)}, u32[]{:S(2)}, u32[]{:S(2)}) %collective-permute-start) | collective-permute-done | bytes 131104 | tf_op jit(solution)/shard_map/ppermute | solution.py:367
  41.8 3.2 %collective-permute-done.1.right_ref = bf16[512,128]{1,0:T(8,128)(2,1)S(1)} collective-permute-done((bf16[512,128]{1,0:T(8,128)(2,1)S(1)}, bf16[512,128]{1,0:T(8,128)(2,1)S(1)}, u32[]{:S(2)}, u32[]{:S(2)}) %collective-permute-start.1) | collective-permute-done | bytes 131104 | tf_op jit(solution)/shard_map/ppermute | solution.py:368
  45.0 0.6 copy-done.7
  45.6 1.0 copy-done.4
  46.6 10.3 %forward.1 = (bf16[8,256,128]{2,1,0:T(8,128)(2,1)}, f32[8,2,256]{2,1,0:T(2,128)}, bf16[256,128]{1,0:T(8,128)(2,1)}, bf16[256,128]{1,0:T(8,128)(2,1)}) custom-call(bf16[8,544,128]{2,1,0:T(8,128)(2,1)} %copy-done.2, bf16[8,512,128]{2,1,0:T(8,128)(2,1)} %copy-done.4, bf16[512,128]{1,0:T(8,128)(2,1)} %copy-done.6, bf16[512,128]{1,0:T(8,128)(2,1)} %copy-done.7, ...), custom_call_target="tpu_custom_call" | custom-call | flops 1073741824 | bytes 8388608 | tf_op jit(solution)/shard_map/forward/pallas_call | solution.py:224
  56.9 4.9 %all-to-all-start.2 = ((bf16[8,256,128]{2,1,0:T(8,128)(2,1)}), bf16[8,256,128]{2,1,0:T(8,128)(2,1)S(1)}, u32[]{:S(2)}, u32[]{:S(2)}) async-start(bf16[8,256,128]{2,1,0:T(8,128)(2,1)} %get-tuple-element.28.att_ref), calls=%async_computation.2 | async-start | bytes 1048576 | tf_op jit(solution)/shard_map/all_to_all | solution.py:353
  61.8 0.6 multiply_add_fusion.heads_ref
  62.4 14.5 %backward.1 = (bf16[8,256,128]{2,1,0:T(8,128)(2,1)}, bf16[8,512,128]{2,1,0:T(8,128)(2,1)}, bf16[512,128]{1,0:T(8,128)(2,1)}, bf16[512,128]{1,0:T(8,128)(2,1)}) custom-call(bf16[8,544,128]{2,1,0:T(8,128)(2,1)} %copy-done.2, bf16[8,512,128]{2,1,0:T(8,128)(2,1)} %copy-done.4, bf16[512,128]{1,0:T(8,128)(2,1)} %copy-done.6, bf16[512,128]{1,0:T(8,128)(2,1)} %copy-done.7, ...), custom_call_target="tpu_custom_call" | custom-call | flops 2684354560 | bytes 8388608 | tf_op jit(solution)/shard_map/backward/pallas_call | solution.py:224
  76.9 0.0 all-to-all-done.2.att_ref
  76.9 0.8 copy-done
  77.7 4.5 %share.3 = bf16[4,128,1024]{2,1,0:T(8,128)(2,1)} custom-call(s32[4]{0:T(128)} %multiply_add_fusion.heads_ref, bf16[8,256,128]{2,1,0:T(8,128)(2,1)} %copy-done, bf16[256,1024]{1,0:T(8,128)(2,1)} %bitcast.61), custom_call_target="tpu_custom_call" | custom-call | flops 268435456 | bytes 2097152 | tf_op jit(solution)/shard_map/share/pallas_call | solution.py:311
  82.2 0.0 collective-permute-start.2
  82.2 0.5 fusion.14.heads_ref
  82.7 2.3 %collective-permute-done.2.refs_0_ = bf16[4,128,1024]{2,1,0:T(8,128)(2,1)S(1)} collective-permute-done((bf16[4,128,1024]{2,1,0:T(8,128)(2,1)}, bf16[4,128,1024]{2,1,0:T(8,128)(2,1)S(1)}, u32[]{:S(2)}, u32[]{:S(2)}) %collective-permute-start.2) | collective-permute-done | bytes 1048608 | tf_op jit(solution)/shard_map/ppermute | solution.py:388
  85.0 1.0 copy-done.1
  86.0 3.1 %share.5 = bf16[2,128,1024]{2,1,0:T(8,128)(2,1)} custom-call(s32[2]{0:T(128)} %fusion.14.heads_ref, bf16[8,256,128]{2,1,0:T(8,128)(2,1)} %copy-done, bf16[256,1024]{1,0:T(8,128)(2,1)} %bitcast.62, bf16[4,128,1024]{2,1,0:T(8,128)(2,1)} %copy-done.1), custom_call_target="tpu_custom_call" | custom-call | flops 134217728 | bytes 2097152 | tf_op jit(solution)/shard_map/share/pallas_call | solution.py:311
  89.2 0.3 collective-permute-start.3
  89.4 12.2 %collective-permute-start.4 = (bf16[512,128]{1,0:T(8,128)(2,1)}, bf16[512,128]{1,0:T(8,128)(2,1)S(1)}, u32[]{:S(2)}, u32[]{:S(2)}) collective-permute-start(bf16[512,128]{1,0:T(8,128)(2,1)} %get-tuple-element.39), channel_id=1, source_target_pairs={{0,8},{8,16},{16,24},{1,9},{9,17},{17,25},{2,10},{10,18},{18,26},{... | collective-permute-start | bytes 393224 | tf_op jit(solution)/shard_map/ppermute | solution.py:383
  101.7 1.3 collective-permute-start.5
  103.0 0.5 fusion.15.heads_ref
  103.5 0.1 slice.36
  103.6 5.1 %all-to-all-start.3 = ((bf16[8,256,128]{2,1,0:T(8,128)(2,1)}), bf16[8,256,128]{2,1,0:T(8,128)(2,1)S(1)}, u32[]{:S(2)}, u32[]{:S(2)}) async-start(bf16[8,256,128]{2,1,0:T(8,128)(2,1)} %get-tuple-element.37), calls=%async_computation.3 | async-start | bytes 1048576 | tf_op jit(solution)/shard_map/all_to_all | solution.py:353
  108.7 1.7 collective-permute-done.5
  110.4 0.1 fusion.1
  110.4 1.1 pad_maximum_fusion
  111.5 3.2 %share.4 = f32[2,128,1024]{2,1,0:T(8,128)} custom-call(s32[2]{0:T(128)} %fusion.15.heads_ref, bf16[8,256,128]{2,1,0:T(8,128)(2,1)} %copy-done, bf16[256,1024]{1,0:T(8,128)(2,1)} %bitcast.63, bf16[4,128,1024]{2,1,0:T(8,128)(2,1)} %copy-done.1), custom_call_target="tpu_custom_call" | custom-call | flops 134217728 | bytes 2097152 | tf_op jit(solution)/shard_map/share/pallas_call | solution.py:311
  114.7 0.0 collective-permute-done.3
  114.7 1.4 convert_add_fusion
  116.1 4.8 %all-to-all-done.3 = bf16[8,256,128]{2,1,0:T(8,128)(2,1)S(1)} async-done(((bf16[8,256,128]{2,1,0:T(8,128)(2,1)}), bf16[8,256,128]{2,1,0:T(8,128)(2,1)S(1)}, u32[]{:S(2)}, u32[]{:S(2)}) %all-to-all-start.3) | async-done | bytes 524320 | tf_op jit(solution)/shard_map/all_to_all | solution.py:353
  121.0 3.6 %all-to-all-start.4 = ((bf16[8,512,128]{2,1,0:T(8,128)(2,1)}), bf16[8,512,128]{2,1,0:T(8,128)(2,1)S(1)}, u32[]{:S(2)}, u32[]{:S(2)}) async-start(bf16[8,512,128]{2,1,0:T(8,128)(2,1)} %pad_maximum_fusion), calls=%async_computation.4 | async-start | bytes 2097152 | tf_op jit(solution)/shard_map/all_to_all | solution.py:353
  124.6 2.3 %collective-permute-start.6 = (bf16[1,128,1024]{2,1,0:T(8,128)(2,1)S(1)}, bf16[1,128,1024]{2,1,0:T(8,128)(2,1)S(1)}, u32[]{:S(2)}, u32[]{:S(2)}) collective-permute-start(bf16[1,128,1024]{2,1,0:T(8,128)(2,1)S(1)} %select_convert_fusion), channel_id=1, source_target_pairs={{0,128},{64,192},{128,0},{192,64},{1,129},{65,193},{129,1},{193,65... | collective-permute-start | bytes 786440 | tf_op jit(solution)/shard_map/ppermute | solution.py:334
  126.9 4.2 %mix.1 = bf16[256,1024]{1,0:T(8,128)(2,1)} custom-call(bf16[8,256,128]{2,1,0:T(8,128)(2,1)} %copy-done, bf16[1024,1024]{1,0:T(8,128)(2,1)} %w_ref.3), custom_call_target="tpu_custom_call" | custom-call | flops 536870912 | bytes 3145728 | tf_op jit(solution)/shard_map/mix/pallas_call | solution.py:280
  131.1 4.1 %collective-permute-done.6 = bf16[1,128,1024]{2,1,0:T(8,128)(2,1)S(1)} collective-permute-done((bf16[1,128,1024]{2,1,0:T(8,128)(2,1)S(1)}, bf16[1,128,1024]{2,1,0:T(8,128)(2,1)S(1)}, u32[]{:S(2)}, u32[]{:S(2)}) %collective-permute-start.6) | collective-permute-done | bytes 262176 | tf_op jit(solution)/shard_map/ppermute | solution.py:334
  135.3 0.1 add_bitcast_fusion
  135.4 1.2 all-to-all-done.4
  136.5 1.6 collective-permute-start.7
  138.1 9.7 %collective-permute-start.8 = (bf16[2,16,1024]{2,1,0:T(8,128)(2,1)S(1)}, bf16[2,16,1024]{2,1,0:T(8,128)(2,1)S(1)}, u32[]{:S(2)}, u32[]{:S(2)}) collective-permute-start(bf16[2,16,1024]{2,1,0:T(8,128)(2,1)S(1)} %get-tuple-element.60), channel_id=1, source_target_pairs={{0,8},{4,12},{8,0},{12,4},{1,9},{5,13},{9,1},{13,5},{2,10},{6,14},... | collective-permute-start | bytes 196616 | tf_op jit(solution)/shard_map/ppermute | solution.py:348
  147.8 0.0 collective-permute-start.9
  147.8 0.0 collective-permute-done.7
  147.8 3.0 %collective-permute-done.8 = bf16[2,16,1024]{2,1,0:T(8,128)(2,1)S(1)} collective-permute-done((bf16[2,16,1024]{2,1,0:T(8,128)(2,1)S(1)}, bf16[2,16,1024]{2,1,0:T(8,128)(2,1)S(1)}, u32[]{:S(2)}, u32[]{:S(2)}) %collective-permute-start.8) | collective-permute-done | bytes 65568 | tf_op jit(solution)/shard_map/ppermute | solution.py:348
  150.8 2.5 %collective-permute-done.9 = bf16[2,16,1024]{2,1,0:T(8,128)(2,1)S(1)} collective-permute-done((bf16[2,16,1024]{2,1,0:T(8,128)(2,1)S(1)}, bf16[2,16,1024]{2,1,0:T(8,128)(2,1)S(1)}, u32[]{:S(2)}, u32[]{:S(2)}) %collective-permute-start.9) | collective-permute-done | bytes 65568 | tf_op jit(solution)/shard_map/ppermute | solution.py:348
  153.3 3.2 %collective-permute-start.10 = (bf16[1,16,1024]{2,1,0:T(8,128)(2,1)S(1)}, bf16[1,16,1024]{2,1,0:T(8,128)(2,1)S(1)}, u32[]{:S(2)}, u32[]{:S(2)}) collective-permute-start(bf16[1,16,1024]{2,1,0:T(8,128)(2,1)S(1)} %select_convert_fusion.1), channel_id=1, source_target_pairs={{0,16},{16,0},{1,17},{17,1},{2,18},{18,2},{3,19},{19,3},{4,20},{20... | collective-permute-start | bytes 98312 | tf_op jit(solution)/shard_map/ppermute | solution.py:334
  156.6 0.2 copy.14
  156.8 1.0 copy.19
  157.8 3.5 %collective-permute-done.10 = bf16[1,16,1024]{2,1,0:T(8,128)(2,1)S(1)} collective-permute-done((bf16[1,16,1024]{2,1,0:T(8,128)(2,1)S(1)}, bf16[1,16,1024]{2,1,0:T(8,128)(2,1)S(1)}, u32[]{:S(2)}, u32[]{:S(2)}) %collective-permute-start.10) | collective-permute-done | bytes 32800 | tf_op jit(solution)/shard_map/ppermute | solution.py:334
  161.3 0.9 collective-permute-start.11
  162.3 2.1 %collective-permute-start.12 = (bf16[4,1024]{1,0:T(4,128)(2,1)S(1)}, bf16[4,1024]{1,0:T(4,128)(2,1)S(1)}, u32[]{:S(2)}, u32[]{:S(2)}) collective-permute-start(bf16[4,1024]{1,0:T(4,128)(2,1)S(1)} %get-tuple-element.63), channel_id=1, source_target_pairs={{0,2},{1,3},{2,0},{3,1},{4,6},{5,7},{6,4},{7,5},{8,10},{9,11},{10,... | collective-permute-start | bytes 24584 | tf_op jit(solution)/shard_map/ppermute | solution.py:348
  164.3 1.8 %collective-permute-start.13 = (bf16[4,1024]{1,0:T(4,128)(2,1)S(1)}, bf16[4,1024]{1,0:T(4,128)(2,1)S(1)}, u32[]{:S(2)}, u32[]{:S(2)}) collective-permute-start(bf16[4,1024]{1,0:T(4,128)(2,1)S(1)} %get-tuple-element.62), channel_id=1, source_target_pairs={{0,3},{1,2},{2,1},{3,0},{4,7},{5,6},{6,5},{7,4},{8,11},{9,10},{10,... | collective-permute-start | bytes 24584 | tf_op jit(solution)/shard_map/ppermute | solution.py:348
  166.1 0.1 slice_bitcast_fusion
  166.2 0.2 copy.15
  166.4 1.0 copy.20
  167.4 0.2 copy.16
  167.7 1.0 copy.21
  168.7 0.5 collective-permute-done.13
  169.2 0.6 fusion.9
  (26 shorter events, 0.2 us)
Async XLA Ops:
  2.8 20.9 %all-to-all-start = ((bf16[8,544,128]{2,1,0:T(8,128)(2,1)}), bf16[8,544,128]{2,1,0:T(8,128)(2,1)S(1)}, u32[]{:S(2)}, u32[]{:S(2)}) async-start(bf16[8,544,128]{2,1,0:T(8,128)(2,1)} %pack_kv.1), calls=%async_computation | async-start | bytes 2228224 | tf_op jit(solution)/shard_map/all_to_all | solution.py:353
  12.7 20.6 %copy-start.5 = (s32[8192]{0:T(1024)S(1)}, s32[8192]{0:T(1024)}, u32[]{:S(2)}) copy-start(s32[8192]{0:T(1024)} %param.13) | copy-start | bytes 98308
  23.7 3.7 %copy-start.2 = (bf16[8,544,128]{2,1,0:T(8,128)(2,1)}, bf16[8,544,128]{2,1,0:T(8,128)(2,1)S(1)}, u32[]{:S(2)}) copy-start(bf16[8,544,128]{2,1,0:T(8,128)(2,1)S(1)} %all-to-all-done.kv_ref) | copy-start | bytes 3342340
  23.7 21.3 %all-to-all-start.1 = ((bf16[8,512,128]{2,1,0:T(8,128)(2,1)}), bf16[8,512,128]{2,1,0:T(8,128)(2,1)S(1)}, u32[]{:S(2)}, u32[]{:S(2)}) async-start(bf16[8,512,128]{2,1,0:T(8,128)(2,1)} %pack_qg.1), calls=%async_computation.1 | async-start | bytes 2097152 | tf_op jit(solution)/shard_map/all_to_all | solution.py:353
  27.4 14.4 %collective-permute-start = (bf16[512,128]{1,0:T(8,128)(2,1)S(1)}, bf16[512,128]{1,0:T(8,128)(2,1)S(1)}, u32[]{:S(2)}, u32[]{:S(2)}) collective-permute-start(bf16[512,128]{1,0:T(8,128)(2,1)S(1)} %get-tuple-element.53), channel_id=1, source_target_pairs={{0,8},{8,16},{16,24},{1,9},{9,17},{17,25},{2,10},{10,18},{18,26},{... | collective-permute-start | bytes 393224 | tf_op jit(solution)/shard_map/ppermute | solution.py:367
  32.0 12.9 %collective-permute-start.1 = (bf16[512,128]{1,0:T(8,128)(2,1)S(1)}, bf16[512,128]{1,0:T(8,128)(2,1)S(1)}, u32[]{:S(2)}, u32[]{:S(2)}) collective-permute-start(bf16[512,128]{1,0:T(8,128)(2,1)S(1)} %get-tuple-element.52), channel_id=1, source_target_pairs={{8,0},{16,8},{24,16},{9,1},{17,9},{25,17},{10,2},{18,10},{26,18},{... | collective-permute-start | bytes 393224 | tf_op jit(solution)/shard_map/ppermute | solution.py:368
  41.8 3.2 %copy-start.6 = (bf16[512,128]{1,0:T(8,128)(2,1)}, bf16[512,128]{1,0:T(8,128)(2,1)S(1)}, u32[]{:S(2)}) copy-start(bf16[512,128]{1,0:T(8,128)(2,1)S(1)} %collective-permute-done.left_ref) | copy-start | bytes 393220
  45.0 0.7 copy-start.7
  45.6 1.0 copy-start.4
  56.9 19.9 %all-to-all-start.2 = ((bf16[8,256,128]{2,1,0:T(8,128)(2,1)}), bf16[8,256,128]{2,1,0:T(8,128)(2,1)S(1)}, u32[]{:S(2)}, u32[]{:S(2)}) async-start(bf16[8,256,128]{2,1,0:T(8,128)(2,1)} %get-tuple-element.28.att_ref), calls=%async_computation.2 | async-start | bytes 1048576 | tf_op jit(solution)/shard_map/all_to_all | solution.py:353
  76.9 0.8 copy-start
  82.2 2.9 %collective-permute-start.2 = (bf16[4,128,1024]{2,1,0:T(8,128)(2,1)}, bf16[4,128,1024]{2,1,0:T(8,128)(2,1)S(1)}, u32[]{:S(2)}, u32[]{:S(2)}) collective-permute-start(bf16[4,128,1024]{2,1,0:T(8,128)(2,1)} %share.3), channel_id=1, source_target_pairs={{0,32},{32,0},{1,33},{33,1},{2,34},{34,2},{3,35},{35,3},{4,36},{36... | collective-permute-start | bytes 3145736 | tf_op jit(solution)/shard_map/ppermute | solution.py:388
  82.7 19.0 %copy-start.8 = (bf16[512,128]{1,0:T(8,128)(2,1)S(1)}, bf16[512,128]{1,0:T(8,128)(2,1)}, u32[]{:S(2)}) copy-start(bf16[512,128]{1,0:T(8,128)(2,1)} %get-tuple-element.40) | copy-start | bytes 393220
  82.7 20.8 %copy-start.3 = (bf16[8,512,128]{2,1,0:T(8,128)(2,1)S(1)}, bf16[8,512,128]{2,1,0:T(8,128)(2,1)}, u32[]{:S(2)}) copy-start(bf16[8,512,128]{2,1,0:T(8,128)(2,1)} %get-tuple-element.38) | copy-start | bytes 3145732
  85.0 1.0 copy-start.1
  89.2 25.6 %collective-permute-start.3 = (bf16[2,128,1024]{2,1,0:T(8,128)(2,1)}, bf16[2,128,1024]{2,1,0:T(8,128)(2,1)S(1)}, u32[]{:S(2)}, u32[]{:S(2)}) collective-permute-start(bf16[2,128,1024]{2,1,0:T(8,128)(2,1)} %share.5), channel_id=1, source_target_pairs={{0,64},{64,0},{128,192},{192,128},{1,65},{65,1},{129,193},{193,129... | collective-permute-start | bytes 1572872 | tf_op jit(solution)/shard_map/ppermute | solution.py:392
  89.4 19.3 %collective-permute-start.4 = (bf16[512,128]{1,0:T(8,128)(2,1)}, bf16[512,128]{1,0:T(8,128)(2,1)S(1)}, u32[]{:S(2)}, u32[]{:S(2)}) collective-permute-start(bf16[512,128]{1,0:T(8,128)(2,1)} %get-tuple-element.39), channel_id=1, source_target_pairs={{0,8},{8,16},{16,24},{1,9},{9,17},{17,25},{2,10},{10,18},{18,26},{... | collective-permute-start | bytes 393224 | tf_op jit(solution)/shard_map/ppermute | solution.py:383
  101.7 8.7 %collective-permute-start.5 = (bf16[512,128]{1,0:T(8,128)(2,1)S(1)}, bf16[512,128]{1,0:T(8,128)(2,1)S(1)}, u32[]{:S(2)}, u32[]{:S(2)}) collective-permute-start(bf16[512,128]{1,0:T(8,128)(2,1)S(1)} %copy-done.8), channel_id=1, source_target_pairs={{8,0},{16,8},{24,16},{9,1},{17,9},{25,17},{10,2},{18,10},{26,18},{... | collective-permute-start | bytes 393224 | tf_op jit(solution)/shard_map/ppermute | solution.py:382
  103.6 17.4 %all-to-all-start.3 = ((bf16[8,256,128]{2,1,0:T(8,128)(2,1)}), bf16[8,256,128]{2,1,0:T(8,128)(2,1)S(1)}, u32[]{:S(2)}, u32[]{:S(2)}) async-start(bf16[8,256,128]{2,1,0:T(8,128)(2,1)} %get-tuple-element.37), calls=%async_computation.3 | async-start | bytes 1048576 | tf_op jit(solution)/shard_map/all_to_all | solution.py:353
  121.0 15.6 %all-to-all-start.4 = ((bf16[8,512,128]{2,1,0:T(8,128)(2,1)}), bf16[8,512,128]{2,1,0:T(8,128)(2,1)S(1)}, u32[]{:S(2)}, u32[]{:S(2)}) async-start(bf16[8,512,128]{2,1,0:T(8,128)(2,1)} %pad_maximum_fusion), calls=%async_computation.4 | async-start | bytes 2097152 | tf_op jit(solution)/shard_map/all_to_all | solution.py:353
  124.6 10.7 %collective-permute-start.6 = (bf16[1,128,1024]{2,1,0:T(8,128)(2,1)S(1)}, bf16[1,128,1024]{2,1,0:T(8,128)(2,1)S(1)}, u32[]{:S(2)}, u32[]{:S(2)}) collective-permute-start(bf16[1,128,1024]{2,1,0:T(8,128)(2,1)S(1)} %select_convert_fusion), channel_id=1, source_target_pairs={{0,128},{64,192},{128,0},{192,64},{1,129},{65,193},{129,1},{193,65... | collective-permute-start | bytes 786440 | tf_op jit(solution)/shard_map/ppermute | solution.py:334
  136.5 11.3 %collective-permute-start.7 = (bf16[2,16,1024]{2,1,0:T(8,128)(2,1)S(1)}, bf16[2,16,1024]{2,1,0:T(8,128)(2,1)S(1)}, u32[]{:S(2)}, u32[]{:S(2)}) collective-permute-start(bf16[2,16,1024]{2,1,0:T(8,128)(2,1)S(1)} %get-tuple-element.58), channel_id=1, source_target_pairs={{0,4},{4,0},{8,12},{12,8},{1,5},{5,1},{9,13},{13,9},{2,6},{6,2},{1... | collective-permute-start | bytes 196616 | tf_op jit(solution)/shard_map/ppermute | solution.py:348
  138.1 12.7 %collective-permute-start.8 = (bf16[2,16,1024]{2,1,0:T(8,128)(2,1)S(1)}, bf16[2,16,1024]{2,1,0:T(8,128)(2,1)S(1)}, u32[]{:S(2)}, u32[]{:S(2)}) collective-permute-start(bf16[2,16,1024]{2,1,0:T(8,128)(2,1)S(1)} %get-tuple-element.60), channel_id=1, source_target_pairs={{0,8},{4,12},{8,0},{12,4},{1,9},{5,13},{9,1},{13,5},{2,10},{6,14},... | collective-permute-start | bytes 196616 | tf_op jit(solution)/shard_map/ppermute | solution.py:348
  147.8 5.5 %collective-permute-start.9 = (bf16[2,16,1024]{2,1,0:T(8,128)(2,1)S(1)}, bf16[2,16,1024]{2,1,0:T(8,128)(2,1)S(1)}, u32[]{:S(2)}, u32[]{:S(2)}) collective-permute-start(bf16[2,16,1024]{2,1,0:T(8,128)(2,1)S(1)} %get-tuple-element.59), channel_id=1, source_target_pairs={{0,12},{4,8},{8,4},{12,0},{1,13},{5,9},{9,5},{13,1},{2,14},{6,10},... | collective-permute-start | bytes 196616 | tf_op jit(solution)/shard_map/ppermute | solution.py:348
  153.3 7.9 %collective-permute-start.10 = (bf16[1,16,1024]{2,1,0:T(8,128)(2,1)S(1)}, bf16[1,16,1024]{2,1,0:T(8,128)(2,1)S(1)}, u32[]{:S(2)}, u32[]{:S(2)}) collective-permute-start(bf16[1,16,1024]{2,1,0:T(8,128)(2,1)S(1)} %select_convert_fusion.1), channel_id=1, source_target_pairs={{0,16},{16,0},{1,17},{17,1},{2,18},{18,2},{3,19},{19,3},{4,20},{20... | collective-permute-start | bytes 98312 | tf_op jit(solution)/shard_map/ppermute | solution.py:334
  161.3 7.3 %collective-permute-start.11 = (bf16[4,1024]{1,0:T(4,128)(2,1)S(1)}, bf16[4,1024]{1,0:T(4,128)(2,1)S(1)}, u32[]{:S(2)}, u32[]{:S(2)}) collective-permute-start(bf16[4,1024]{1,0:T(4,128)(2,1)S(1)} %get-tuple-element.61), channel_id=1, source_target_pairs={{0,1},{1,0},{2,3},{3,2},{4,5},{5,4},{6,7},{7,6},{8,9},{9,8},{10,11... | collective-permute-start | bytes 24584 | tf_op jit(solution)/shard_map/ppermute | solution.py:348
  162.3 6.4 %collective-permute-start.12 = (bf16[4,1024]{1,0:T(4,128)(2,1)S(1)}, bf16[4,1024]{1,0:T(4,128)(2,1)S(1)}, u32[]{:S(2)}, u32[]{:S(2)}) collective-permute-start(bf16[4,1024]{1,0:T(4,128)(2,1)S(1)} %get-tuple-element.63), channel_id=1, source_target_pairs={{0,2},{1,3},{2,0},{3,1},{4,6},{5,7},{6,4},{7,5},{8,10},{9,11},{10,... | collective-permute-start | bytes 24584 | tf_op jit(solution)/shard_map/ppermute | solution.py:348
  164.3 4.9 %collective-permute-start.13 = (bf16[4,1024]{1,0:T(4,128)(2,1)S(1)}, bf16[4,1024]{1,0:T(4,128)(2,1)S(1)}, u32[]{:S(2)}, u32[]{:S(2)}) collective-permute-start(bf16[4,1024]{1,0:T(4,128)(2,1)S(1)} %get-tuple-element.62), channel_id=1, source_target_pairs={{0,3},{1,2},{2,1},{3,0},{4,7},{5,6},{6,5},{7,4},{8,11},{9,10},{10,... | collective-permute-start | bytes 24584 | tf_op jit(solution)/shard_map/ppermute | solution.py:348

commit v6 on v5

--- a/solution.py
+++ b/solution.py
@@ -396,14 +396,14 @@
     first = dkv[:1].astype(F32) + from_left.astype(F32)[None]
     last = dkv[SHARDS - 1 :].astype(F32) + from_right.astype(F32)[None]
     dkv = jnp.concatenate([first.astype(BF), dkv[1 : SHARDS - 1], last.astype(BF)], axis=0)
-    share, dq, dkv = lax.optimization_barrier((share, dq, dkv))
     dkv = to_heads(dkv)
     mixed = mix(att_rows, w)
     share = halved(share, 0, "zl", 1)[0]
-    share, dkv, mixed = lax.optimization_barrier((share, dkv, mixed))
+    share, dq = lax.optimization_barrier((share, dq))
 
     width = share.shape[-1]
     share = scattered(share.reshape(2, 4, 16, width), 1, ("xh", "xl"))
+    share, dkv, mixed = lax.optimization_barrier((share, dkv, mixed))
     share = halved(share, 0, "zh", 0)
     share = scattered(share.reshape(4, 4, width), 0, ("y",))
     weight_grad = share * (1.0 / math.sqrt(8 * 32 * ROWS))

time: 171 us -> 168 us (0.982)
  waiting for transfers between devices: 45.5 us -> 38.2 us
  other arithmetic: 5.04 us -> 7.48 us
    all_to_all x5, waiting for transfers between devices: 17 us -> 12 us  [to_heads(): return lax.all_to_all(x, FRAME, 0, 0, tiled=True)]
    unnamed x21 -> x23, local copies, waits for them, and re-layouts: 6.44 us -> 6.42 us
  transfers between devices with their start and end apart: 19 -> 19, of which waited for: 12 -> 10; matrix products, arithmetic and copies ran while one was open for 5% -> 7% of each run, Pallas kernels for 16% -> 16%
where the time goes in v6:
time: 168 us; the launch traced here: 166 us
  starting transfers between devices  64.6 us (38%)
  Pallas kernels  46.6 us (28%)
  waiting for transfers between devices  38.2 us (23%)
  local copies, waits for them, and re-layouts  7.9 us (5%)
  other arithmetic  7.48 us (4%)
    pallas_call x2, Pallas kernels, over_blocks(): pl.pallas_call(kernel, grid=(SHARDS,), in_specs=in_specs, out_specs=[whol...  24.8 us
    all_to_all x5, starting transfers between devices, to_heads(): return lax.all_to_all(x, FRAME, 0, 0, tiled=True)  23.1 us
    ppermute x6, starting transfers between devices, scattered(): lax.ppermute(out, axes, [(j, j ^ apart) for j in range(count)]).astype(F32)  16 us
    ppermute x1, starting transfers between devices, on_device(): from_left = lax.ppermute(dright, FRAMES, ups)  12.3 us
    all_to_all x5, waiting for transfers between devices, to_heads(): return lax.all_to_all(x, FRAME, 0, 0, tiled=True)  12 us
    pallas_call x3, Pallas kernels, share_of(): pl.pallas_call(share_kernel, grid_spec=pltpu.PrefetchScalarGridSpec(num_s...  10.9 us
    ppermute x1, waiting for transfers between devices, on_device(): left = lax.ppermute(kv[SHARDS - 1, :2 * ROWS], FRAMES, ups)  7.74 us
    ppermute x2, waiting for transfers between devices, halved(): got = lax.ppermute(out, axis, [(j, j ^ 1 << bit) for j in range(count)])  6.93 us
  transfers between devices with their start and end apart: 19, of which 10 were waited for; matrix products, arithmetic and copies ran while one was open for 7% of the time, Pallas kernels for 16%

profile of v6, /device:TPU:32, one launch (start us, length us, event | category | flops | bytes accessed | tf_op | source)
XLA Modules:
  0.0 165.7 jit_solution(7996392549897508190)
XLA Ops:
  0.6 2.2 %pack_kv.1 = bf16[8,544,128]{2,1,0:T(8,128)(2,1)} custom-call(bf16[256,1024]{1,0:T(8,128)(2,1)} %bitcast.70, bf16[256,1024]{1,0:T(8,128)(2,1)} %bitcast.71, s32[1,32]{1,0:T(1,128)} %s_ref.1), custom_call_target="tpu_custom_call" | custom-call | tf_op jit(solution)/shard_map/pack_kv/pallas_call | solution.py:48
  2.8 5.4 %all-to-all-start = ((bf16[8,544,128]{2,1,0:T(8,128)(2,1)}), bf16[8,544,128]{2,1,0:T(8,128)(2,1)S(1)}, u32[]{:S(2)}, u32[]{:S(2)}) async-start(bf16[8,544,128]{2,1,0:T(8,128)(2,1)} %pack_kv.1), calls=%async_computation | async-start | bytes 2228224 | tf_op jit(solution)/shard_map/all_to_all | solution.py:353
  8.2 4.6 %pack_qg.1 = bf16[8,512,128]{2,1,0:T(8,128)(2,1)} custom-call(bf16[256,1024]{1,0:T(8,128)(2,1)} %bitcast.73, bf16[256,1024]{1,0:T(8,128)(2,1)} %bitcast.60, bf16[1024,1024]{1,0:T(8,128)(2,1)} %w_ref.3), custom_call_target="tpu_custom_call" | custom-call | flops 536870912 | bytes 5242880 | tf_op jit(solution)/shard_map/pack_qg/pallas_call | solution.py:73
  12.8 10.9 %all-to-all-done.kv_ref = bf16[8,544,128]{2,1,0:T(8,128)(2,1)S(1)} async-done(((bf16[8,544,128]{2,1,0:T(8,128)(2,1)}), bf16[8,544,128]{2,1,0:T(8,128)(2,1)S(1)}, u32[]{:S(2)}, u32[]{:S(2)}) %all-to-all-start) | async-done | bytes 1114144 | tf_op jit(solution)/shard_map/all_to_all | solution.py:353
  23.7 3.6 %all-to-all-start.1 = ((bf16[8,512,128]{2,1,0:T(8,128)(2,1)}), bf16[8,512,128]{2,1,0:T(8,128)(2,1)S(1)}, u32[]{:S(2)}, u32[]{:S(2)}) async-start(bf16[8,512,128]{2,1,0:T(8,128)(2,1)} %pack_qg.1), calls=%async_computation.1 | async-start | bytes 2097152 | tf_op jit(solution)/shard_map/all_to_all | solution.py:353
  27.4 4.6 %collective-permute-start = (bf16[512,128]{1,0:T(8,128)(2,1)S(1)}, bf16[512,128]{1,0:T(8,128)(2,1)S(1)}, u32[]{:S(2)}, u32[]{:S(2)}) collective-permute-start(bf16[512,128]{1,0:T(8,128)(2,1)S(1)} %get-tuple-element.51), channel_id=1, source_target_pairs={{0,8},{8,16},{16,24},{1,9},{9,17},{17,25},{2,10},{10,18},{18,26},{... | collective-permute-start | bytes 393224 | tf_op jit(solution)/shard_map/ppermute | solution.py:367
  32.0 1.3 collective-permute-start.1
  33.3 0.1 fusion.10
  33.4 0.6 reshape.25.label_ref
  34.0 7.7 %collective-permute-done.left_ref = bf16[512,128]{1,0:T(8,128)(2,1)S(1)} collective-permute-done((bf16[512,128]{1,0:T(8,128)(2,1)S(1)}, bf16[512,128]{1,0:T(8,128)(2,1)S(1)}, u32[]{:S(2)}, u32[]{:S(2)}) %collective-permute-start) | collective-permute-done | bytes 131104 | tf_op jit(solution)/shard_map/ppermute | solution.py:367
  41.8 3.2 %collective-permute-done.1.right_ref = bf16[512,128]{1,0:T(8,128)(2,1)S(1)} collective-permute-done((bf16[512,128]{1,0:T(8,128)(2,1)S(1)}, bf16[512,128]{1,0:T(8,128)(2,1)S(1)}, u32[]{:S(2)}, u32[]{:S(2)}) %collective-permute-start.1) | collective-permute-done | bytes 131104 | tf_op jit(solution)/shard_map/ppermute | solution.py:368
  45.0 0.0 all-to-all-done.1.q_ref.ga_ref
  45.0 0.6 copy-done.9
  45.6 1.0 copy-done.4
  46.6 10.3 %forward.1 = (bf16[8,256,128]{2,1,0:T(8,128)(2,1)}, f32[8,2,256]{2,1,0:T(2,128)}, bf16[256,128]{1,0:T(8,128)(2,1)}, bf16[256,128]{1,0:T(8,128)(2,1)}) custom-call(bf16[8,544,128]{2,1,0:T(8,128)(2,1)} %copy-done.2, bf16[8,512,128]{2,1,0:T(8,128)(2,1)} %copy-done.4, bf16[512,128]{1,0:T(8,128)(2,1)} %copy-done.7, bf16[512,128]{1,0:T(8,128)(2,1)} %copy-done.9, ...), custom_call_target="tpu_custom_call" | custom-call | flops 1073741824 | bytes 8388608 | tf_op jit(solution)/shard_map/forward/pallas_call | solution.py:224
  56.9 4.9 %all-to-all-start.2 = ((bf16[8,256,128]{2,1,0:T(8,128)(2,1)}), bf16[8,256,128]{2,1,0:T(8,128)(2,1)S(1)}, u32[]{:S(2)}, u32[]{:S(2)}) async-start(bf16[8,256,128]{2,1,0:T(8,128)(2,1)} %get-tuple-element.27.att_ref), calls=%async_computation.2 | async-start | bytes 1048576 | tf_op jit(solution)/shard_map/all_to_all | solution.py:353
  61.8 0.5 multiply_add_fusion.heads_ref
  62.3 14.5 %backward.1 = (bf16[8,256,128]{2,1,0:T(8,128)(2,1)}, bf16[8,512,128]{2,1,0:T(8,128)(2,1)}, bf16[512,128]{1,0:T(8,128)(2,1)}, bf16[512,128]{1,0:T(8,128)(2,1)}) custom-call(bf16[8,544,128]{2,1,0:T(8,128)(2,1)} %copy-done.2, bf16[8,512,128]{2,1,0:T(8,128)(2,1)} %copy-done.4, bf16[512,128]{1,0:T(8,128)(2,1)} %copy-done.7, bf16[512,128]{1,0:T(8,128)(2,1)} %copy-done.9, ...), custom_call_target="tpu_custom_call" | custom-call | flops 2684354560 | bytes 8388608 | tf_op jit(solution)/shard_map/backward/pallas_call | solution.py:224
  76.8 0.8 copy-done
  77.6 4.5 %share.3 = bf16[4,128,1024]{2,1,0:T(8,128)(2,1)} custom-call(s32[4]{0:T(128)} %multiply_add_fusion.heads_ref, bf16[8,256,128]{2,1,0:T(8,128)(2,1)} %copy-done, bf16[256,1024]{1,0:T(8,128)(2,1)} %bitcast.61), custom_call_target="tpu_custom_call" | custom-call | flops 268435456 | bytes 2097152 | tf_op jit(solution)/shard_map/share/pallas_call | solution.py:311
  82.2 0.0 collective-permute-start.2
  82.2 0.5 fusion.14.heads_ref
  82.7 2.3 %collective-permute-done.2.refs_0_ = bf16[4,128,1024]{2,1,0:T(8,128)(2,1)S(1)} collective-permute-done((bf16[4,128,1024]{2,1,0:T(8,128)(2,1)}, bf16[4,128,1024]{2,1,0:T(8,128)(2,1)S(1)}, u32[]{:S(2)}, u32[]{:S(2)}) %collective-permute-start.2) | collective-permute-done | bytes 1048608 | tf_op jit(solution)/shard_map/ppermute | solution.py:388
  85.0 1.0 copy-done.1
  86.0 3.1 %share.5 = bf16[2,128,1024]{2,1,0:T(8,128)(2,1)} custom-call(s32[2]{0:T(128)} %fusion.14.heads_ref, bf16[8,256,128]{2,1,0:T(8,128)(2,1)} %copy-done, bf16[256,1024]{1,0:T(8,128)(2,1)} %bitcast.62, bf16[4,128,1024]{2,1,0:T(8,128)(2,1)} %copy-done.1), custom_call_target="tpu_custom_call" | custom-call | flops 134217728 | bytes 2097152 | tf_op jit(solution)/shard_map/share/pallas_call | solution.py:311
  89.1 0.3 collective-permute-start.3
  89.4 12.3 %collective-permute-start.8 = (bf16[512,128]{1,0:T(8,128)(2,1)}, bf16[512,128]{1,0:T(8,128)(2,1)S(1)}, u32[]{:S(2)}, u32[]{:S(2)}) collective-permute-start(bf16[512,128]{1,0:T(8,128)(2,1)} %get-tuple-element.39), channel_id=1, source_target_pairs={{0,8},{8,16},{16,24},{1,9},{9,17},{17,25},{2,10},{10,18},{18,26},{... | collective-permute-start | bytes 393224 | tf_op jit(solution)/shard_map/ppermute | solution.py:383
  101.7 1.3 collective-permute-start.9
  103.0 0.5 fusion.15.heads_ref
  103.5 0.1 slice.38
  103.6 5.1 %all-to-all-start.3 = ((bf16[8,256,128]{2,1,0:T(8,128)(2,1)}), bf16[8,256,128]{2,1,0:T(8,128)(2,1)S(1)}, u32[]{:S(2)}, u32[]{:S(2)}) async-start(bf16[8,256,128]{2,1,0:T(8,128)(2,1)} %get-tuple-element.36), calls=%async_computation.3 | async-start | bytes 1048576 | tf_op jit(solution)/shard_map/all_to_all | solution.py:353
  108.7 1.7 %collective-permute-done.9 = bf16[512,128]{1,0:T(8,128)(2,1)S(1)} collective-permute-done((bf16[512,128]{1,0:T(8,128)(2,1)S(1)}, bf16[512,128]{1,0:T(8,128)(2,1)S(1)}, u32[]{:S(2)}, u32[]{:S(2)}) %collective-permute-start.9) | collective-permute-done | bytes 131104 | tf_op jit(solution)/shard_map/ppermute | solution.py:382
  110.3 0.7 fusion.1
  111.1 3.2 %share.4 = f32[2,128,1024]{2,1,0:T(8,128)} custom-call(s32[2]{0:T(128)} %fusion.15.heads_ref, bf16[8,256,128]{2,1,0:T(8,128)(2,1)} %copy-done, bf16[256,1024]{1,0:T(8,128)(2,1)} %bitcast.63, bf16[4,128,1024]{2,1,0:T(8,128)(2,1)} %copy-done.1), custom_call_target="tpu_custom_call" | custom-call | flops 134217728 | bytes 2097152 | tf_op jit(solution)/shard_map/share/pallas_call | solution.py:311
  114.3 1.5 convert_add_fusion
  115.8 0.8 select_convert_fusion
  116.6 2.2 %collective-permute-start.4 = (bf16[1,128,1024]{2,1,0:T(8,128)(2,1)}, bf16[1,128,1024]{2,1,0:T(8,128)(2,1)}, u32[]{:S(2)}, u32[]{:S(2)}) collective-permute-start(bf16[1,128,1024]{2,1,0:T(8,128)(2,1)} %select_convert_fusion), channel_id=1, source_target_pairs={{0,128},{64,192},{128,0},{192,64},{1,129},{65,193},{129,1},{193,65... | collective-permute-start | bytes 786440 | tf_op jit(solution)/shard_map/ppermute | solution.py:334
  118.8 1.1 pad_maximum_fusion
  119.9 1.0 all-to-all-done.3
  120.9 4.1 %all-to-all-start.4 = ((bf16[8,512,128]{2,1,0:T(8,128)(2,1)}), bf16[8,512,128]{2,1,0:T(8,128)(2,1)S(1)}, u32[]{:S(2)}, u32[]{:S(2)}) async-start(bf16[8,512,128]{2,1,0:T(8,128)(2,1)} %pad_maximum_fusion), calls=%async_computation.4 | async-start | bytes 2097152 | tf_op jit(solution)/shard_map/all_to_all | solution.py:353
  125.0 3.9 %collective-permute-done.4 = bf16[1,128,1024]{2,1,0:T(8,128)(2,1)} collective-permute-done((bf16[1,128,1024]{2,1,0:T(8,128)(2,1)}, bf16[1,128,1024]{2,1,0:T(8,128)(2,1)}, u32[]{:S(2)}, u32[]{:S(2)}) %collective-permute-start.4) | collective-permute-done | bytes 262176 | tf_op jit(solution)/shard_map/ppermute | solution.py:334
  128.9 1.0 add_bitcast_fusion
  129.9 1.5 collective-permute-start.5
  131.5 9.7 %collective-permute-start.6 = (bf16[2,16,1024]{2,1,0:T(8,128)(2,1)S(1)}, bf16[2,16,1024]{2,1,0:T(8,128)(2,1)S(1)}, u32[]{:S(2)}, u32[]{:S(2)}) collective-permute-start(bf16[2,16,1024]{2,1,0:T(8,128)(2,1)S(1)} %get-tuple-element.58), channel_id=1, source_target_pairs={{0,8},{4,12},{8,0},{12,4},{1,9},{5,13},{9,1},{13,5},{2,10},{6,14},... | collective-permute-start | bytes 196616 | tf_op jit(solution)/shard_map/ppermute | solution.py:348
  141.1 0.0 collective-permute-start.7
  141.1 4.2 %mix.1 = bf16[256,1024]{1,0:T(8,128)(2,1)} custom-call(bf16[8,256,128]{2,1,0:T(8,128)(2,1)} %copy-done, bf16[1024,1024]{1,0:T(8,128)(2,1)} %w_ref.3), custom_call_target="tpu_custom_call" | custom-call | flops 536870912 | bytes 3145728 | tf_op jit(solution)/shard_map/mix/pallas_call | solution.py:280
  145.4 0.0 collective-permute-done.5
  145.4 2.3 %collective-permute-done.6 = bf16[2,16,1024]{2,1,0:T(8,128)(2,1)S(1)} collective-permute-done((bf16[2,16,1024]{2,1,0:T(8,128)(2,1)S(1)}, bf16[2,16,1024]{2,1,0:T(8,128)(2,1)S(1)}, u32[]{:S(2)}, u32[]{:S(2)}) %collective-permute-start.6) | collective-permute-done | bytes 65568 | tf_op jit(solution)/shard_map/ppermute | solution.py:348
  147.7 0.0 collective-permute-done.7
  147.7 3.6 %collective-permute-start.10 = (bf16[1,16,1024]{2,1,0:T(8,128)(2,1)S(1)}, bf16[1,16,1024]{2,1,0:T(8,128)(2,1)S(1)}, u32[]{:S(2)}, u32[]{:S(2)}) collective-permute-start(bf16[1,16,1024]{2,1,0:T(8,128)(2,1)S(1)} %select_convert_fusion.1), channel_id=1, source_target_pairs={{0,16},{16,0},{1,17},{17,1},{2,18},{18,2},{3,19},{19,3},{4,20},{20... | collective-permute-start | bytes 98312 | tf_op jit(solution)/shard_map/ppermute | solution.py:334
  151.3 0.2 copy.16
  151.6 1.0 copy.19
  152.6 3.1 %collective-permute-done.10 = bf16[1,16,1024]{2,1,0:T(8,128)(2,1)S(1)} collective-permute-done((bf16[1,16,1024]{2,1,0:T(8,128)(2,1)S(1)}, bf16[1,16,1024]{2,1,0:T(8,128)(2,1)S(1)}, u32[]{:S(2)}, u32[]{:S(2)}) %collective-permute-start.10) | collective-permute-done | bytes 32800 | tf_op jit(solution)/shard_map/ppermute | solution.py:334
  155.7 1.9 %collective-permute-start.11 = (bf16[4,1024]{1,0:T(4,128)(2,1)S(1)}, bf16[4,1024]{1,0:T(4,128)(2,1)S(1)}, u32[]{:S(2)}, u32[]{:S(2)}) collective-permute-start(bf16[4,1024]{1,0:T(4,128)(2,1)S(1)} %get-tuple-element.59), channel_id=1, source_target_pairs={{0,1},{1,0},{2,3},{3,2},{4,5},{5,4},{6,7},{7,6},{8,9},{9,8},{10,11... | collective-permute-start | bytes 24584 | tf_op jit(solution)/shard_map/ppermute | solution.py:348
  157.6 2.7 %collective-permute-start.12 = (bf16[4,1024]{1,0:T(4,128)(2,1)S(1)}, bf16[4,1024]{1,0:T(4,128)(2,1)S(1)}, u32[]{:S(2)}, u32[]{:S(2)}) collective-permute-start(bf16[4,1024]{1,0:T(4,128)(2,1)S(1)} %get-tuple-element.61), channel_id=1, source_target_pairs={{0,2},{1,3},{2,0},{3,1},{4,6},{5,7},{6,4},{7,5},{8,10},{9,11},{10,... | collective-permute-start | bytes 24584 | tf_op jit(solution)/shard_map/ppermute | solution.py:348
  160.3 0.2 collective-permute-start.13
  160.5 0.1 slice_bitcast_fusion
  160.6 0.2 copy.17
  160.8 1.0 copy.20
  161.8 0.2 copy.18
  162.0 1.0 copy.21
  163.0 0.0 collective-permute-done.11
  163.0 2.1 %collective-permute-done.13 = bf16[4,1024]{1,0:T(4,128)(2,1)S(1)} collective-permute-done((bf16[4,1024]{1,0:T(4,128)(2,1)S(1)}, bf16[4,1024]{1,0:T(4,128)(2,1)S(1)}, u32[]{:S(2)}, u32[]{:S(2)}) %collective-permute-start.13) | collective-permute-done | bytes 8224 | tf_op jit(solution)/shard_map/ppermute | solution.py:348
  165.1 0.6 fusion.9
  (28 shorter events, 0.2 us)
Async XLA Ops:
  2.8 20.9 %all-to-all-start = ((bf16[8,544,128]{2,1,0:T(8,128)(2,1)}), bf16[8,544,128]{2,1,0:T(8,128)(2,1)S(1)}, u32[]{:S(2)}, u32[]{:S(2)}) async-start(bf16[8,544,128]{2,1,0:T(8,128)(2,1)} %pack_kv.1), calls=%async_computation | async-start | bytes 2228224 | tf_op jit(solution)/shard_map/all_to_all | solution.py:353
  12.8 20.6 %copy-start.6 = (s32[8192]{0:T(1024)S(1)}, s32[8192]{0:T(1024)}, u32[]{:S(2)}) copy-start(s32[8192]{0:T(1024)} %param.13) | copy-start | bytes 98308
  23.7 3.7 %copy-start.2 = (bf16[8,544,128]{2,1,0:T(8,128)(2,1)}, bf16[8,544,128]{2,1,0:T(8,128)(2,1)S(1)}, u32[]{:S(2)}) copy-start(bf16[8,544,128]{2,1,0:T(8,128)(2,1)S(1)} %all-to-all-done.kv_ref) | copy-start | bytes 3342340
  23.7 21.3 %all-to-all-start.1 = ((bf16[8,512,128]{2,1,0:T(8,128)(2,1)}), bf16[8,512,128]{2,1,0:T(8,128)(2,1)S(1)}, u32[]{:S(2)}, u32[]{:S(2)}) async-start(bf16[8,512,128]{2,1,0:T(8,128)(2,1)} %pack_qg.1), calls=%async_computation.1 | async-start | bytes 2097152 | tf_op jit(solution)/shard_map/all_to_all | solution.py:353
  27.4 14.4 %collective-permute-start = (bf16[512,128]{1,0:T(8,128)(2,1)S(1)}, bf16[512,128]{1,0:T(8,128)(2,1)S(1)}, u32[]{:S(2)}, u32[]{:S(2)}) collective-permute-start(bf16[512,128]{1,0:T(8,128)(2,1)S(1)} %get-tuple-element.51), channel_id=1, source_target_pairs={{0,8},{8,16},{16,24},{1,9},{9,17},{17,25},{2,10},{10,18},{18,26},{... | collective-permute-start | bytes 393224 | tf_op jit(solution)/shard_map/ppermute | solution.py:367
  32.0 12.9 %collective-permute-start.1 = (bf16[512,128]{1,0:T(8,128)(2,1)S(1)}, bf16[512,128]{1,0:T(8,128)(2,1)S(1)}, u32[]{:S(2)}, u32[]{:S(2)}) collective-permute-start(bf16[512,128]{1,0:T(8,128)(2,1)S(1)} %get-tuple-element.50), channel_id=1, source_target_pairs={{8,0},{16,8},{24,16},{9,1},{17,9},{25,17},{10,2},{18,10},{26,18},{... | collective-permute-start | bytes 393224 | tf_op jit(solution)/shard_map/ppermute | solution.py:368
  41.8 3.2 %copy-start.7 = (bf16[512,128]{1,0:T(8,128)(2,1)}, bf16[512,128]{1,0:T(8,128)(2,1)S(1)}, u32[]{:S(2)}) copy-start(bf16[512,128]{1,0:T(8,128)(2,1)S(1)} %collective-permute-done.left_ref) | copy-start | bytes 393220
  45.0 0.7 copy-start.9
  45.6 1.0 copy-start.4
  56.9 19.9 %all-to-all-start.2 = ((bf16[8,256,128]{2,1,0:T(8,128)(2,1)}), bf16[8,256,128]{2,1,0:T(8,128)(2,1)S(1)}, u32[]{:S(2)}, u32[]{:S(2)}) async-start(bf16[8,256,128]{2,1,0:T(8,128)(2,1)} %get-tuple-element.27.att_ref), calls=%async_computation.2 | async-start | bytes 1048576 | tf_op jit(solution)/shard_map/all_to_all | solution.py:353
  76.8 0.8 copy-start
  82.2 2.9 %collective-permute-start.2 = (bf16[4,128,1024]{2,1,0:T(8,128)(2,1)}, bf16[4,128,1024]{2,1,0:T(8,128)(2,1)S(1)}, u32[]{:S(2)}, u32[]{:S(2)}) collective-permute-start(bf16[4,128,1024]{2,1,0:T(8,128)(2,1)} %share.3), channel_id=1, source_target_pairs={{0,32},{32,0},{1,33},{33,1},{2,34},{34,2},{3,35},{35,3},{4,36},{36... | collective-permute-start | bytes 3145736 | tf_op jit(solution)/shard_map/ppermute | solution.py:388
  82.7 19.0 %copy-start.8 = (bf16[512,128]{1,0:T(8,128)(2,1)S(1)}, bf16[512,128]{1,0:T(8,128)(2,1)}, u32[]{:S(2)}) copy-start(bf16[512,128]{1,0:T(8,128)(2,1)} %get-tuple-element.40) | copy-start | bytes 393220
  82.7 20.8 %copy-start.3 = (bf16[8,512,128]{2,1,0:T(8,128)(2,1)S(1)}, bf16[8,512,128]{2,1,0:T(8,128)(2,1)}, u32[]{:S(2)}) copy-start(bf16[8,512,128]{2,1,0:T(8,128)(2,1)} %get-tuple-element.38) | copy-start | bytes 3145732
  85.0 1.0 copy-start.1
  89.1 25.2 %collective-permute-start.3 = (bf16[2,128,1024]{2,1,0:T(8,128)(2,1)}, bf16[2,128,1024]{2,1,0:T(8,128)(2,1)}, u32[]{:S(2)}, u32[]{:S(2)}) collective-permute-start(bf16[2,128,1024]{2,1,0:T(8,128)(2,1)} %share.5), channel_id=1, source_target_pairs={{0,64},{64,0},{128,192},{192,128},{1,65},{65,1},{129,193},{193,129... | collective-permute-start | bytes 1572872 | tf_op jit(solution)/shard_map/ppermute | solution.py:392
  89.4 19.3 %collective-permute-start.8 = (bf16[512,128]{1,0:T(8,128)(2,1)}, bf16[512,128]{1,0:T(8,128)(2,1)S(1)}, u32[]{:S(2)}, u32[]{:S(2)}) collective-permute-start(bf16[512,128]{1,0:T(8,128)(2,1)} %get-tuple-element.39), channel_id=1, source_target_pairs={{0,8},{8,16},{16,24},{1,9},{9,17},{17,25},{2,10},{10,18},{18,26},{... | collective-permute-start | bytes 393224 | tf_op jit(solution)/shard_map/ppermute | solution.py:383
  101.7 8.7 %collective-permute-start.9 = (bf16[512,128]{1,0:T(8,128)(2,1)S(1)}, bf16[512,128]{1,0:T(8,128)(2,1)S(1)}, u32[]{:S(2)}, u32[]{:S(2)}) collective-permute-start(bf16[512,128]{1,0:T(8,128)(2,1)S(1)} %copy-done.8), channel_id=1, source_target_pairs={{8,0},{16,8},{24,16},{9,1},{17,9},{25,17},{10,2},{18,10},{26,18},{... | collective-permute-start | bytes 393224 | tf_op jit(solution)/shard_map/ppermute | solution.py:382
  103.6 17.4 %all-to-all-start.3 = ((bf16[8,256,128]{2,1,0:T(8,128)(2,1)}), bf16[8,256,128]{2,1,0:T(8,128)(2,1)S(1)}, u32[]{:S(2)}, u32[]{:S(2)}) async-start(bf16[8,256,128]{2,1,0:T(8,128)(2,1)} %get-tuple-element.36), calls=%async_computation.3 | async-start | bytes 1048576 | tf_op jit(solution)/shard_map/all_to_all | solution.py:353
  114.3 4.5 %copy-start.5 = (bf16[1,512,128]{2,1,0:T(8,128)(2,1)S(1)}, bf16[1,512,128]{2,1,0:T(8,128)(2,1)}, u32[]{:S(2)}) copy-start(bf16[1,512,128]{2,1,0:T(8,128)(2,1)} %get-tuple-element.55) | copy-start | bytes 393220
  116.6 12.3 %collective-permute-start.4 = (bf16[1,128,1024]{2,1,0:T(8,128)(2,1)}, bf16[1,128,1024]{2,1,0:T(8,128)(2,1)}, u32[]{:S(2)}, u32[]{:S(2)}) collective-permute-start(bf16[1,128,1024]{2,1,0:T(8,128)(2,1)} %select_convert_fusion), channel_id=1, source_target_pairs={{0,128},{64,192},{128,0},{192,64},{1,129},{65,193},{129,1},{193,65... | collective-permute-start | bytes 786440 | tf_op jit(solution)/shard_map/ppermute | solution.py:334
  120.9 26.8 %all-to-all-start.4 = ((bf16[8,512,128]{2,1,0:T(8,128)(2,1)}), bf16[8,512,128]{2,1,0:T(8,128)(2,1)S(1)}, u32[]{:S(2)}, u32[]{:S(2)}) async-start(bf16[8,512,128]{2,1,0:T(8,128)(2,1)} %pad_maximum_fusion), calls=%async_computation.4 | async-start | bytes 2097152 | tf_op jit(solution)/shard_map/all_to_all | solution.py:353
  129.9 15.4 %collective-permute-start.5 = (bf16[2,16,1024]{2,1,0:T(8,128)(2,1)S(1)}, bf16[2,16,1024]{2,1,0:T(8,128)(2,1)S(1)}, u32[]{:S(2)}, u32[]{:S(2)}) collective-permute-start(bf16[2,16,1024]{2,1,0:T(8,128)(2,1)S(1)} %get-tuple-element.56), channel_id=1, source_target_pairs={{0,4},{4,0},{8,12},{12,8},{1,5},{5,1},{9,13},{13,9},{2,6},{6,2},{1... | collective-permute-start | bytes 196616 | tf_op jit(solution)/shard_map/ppermute | solution.py:348
  131.5 16.2 %collective-permute-start.6 = (bf16[2,16,1024]{2,1,0:T(8,128)(2,1)S(1)}, bf16[2,16,1024]{2,1,0:T(8,128)(2,1)S(1)}, u32[]{:S(2)}, u32[]{:S(2)}) collective-permute-start(bf16[2,16,1024]{2,1,0:T(8,128)(2,1)S(1)} %get-tuple-element.58), channel_id=1, source_target_pairs={{0,8},{4,12},{8,0},{12,4},{1,9},{5,13},{9,1},{13,5},{2,10},{6,14},... | collective-permute-start | bytes 196616 | tf_op jit(solution)/shard_map/ppermute | solution.py:348
  141.1 6.5 %collective-permute-start.7 = (bf16[2,16,1024]{2,1,0:T(8,128)(2,1)S(1)}, bf16[2,16,1024]{2,1,0:T(8,128)(2,1)S(1)}, u32[]{:S(2)}, u32[]{:S(2)}) collective-permute-start(bf16[2,16,1024]{2,1,0:T(8,128)(2,1)S(1)} %get-tuple-element.57), channel_id=1, source_target_pairs={{0,12},{4,8},{8,4},{12,0},{1,13},{5,9},{9,5},{13,1},{2,14},{6,10},... | collective-permute-start | bytes 196616 | tf_op jit(solution)/shard_map/ppermute | solution.py:348
  147.7 7.9 %collective-permute-start.10 = (bf16[1,16,1024]{2,1,0:T(8,128)(2,1)S(1)}, bf16[1,16,1024]{2,1,0:T(8,128)(2,1)S(1)}, u32[]{:S(2)}, u32[]{:S(2)}) collective-permute-start(bf16[1,16,1024]{2,1,0:T(8,128)(2,1)S(1)} %select_convert_fusion.1), channel_id=1, source_target_pairs={{0,16},{16,0},{1,17},{17,1},{2,18},{18,2},{3,19},{19,3},{4,20},{20... | collective-permute-start | bytes 98312 | tf_op jit(solution)/shard_map/ppermute | solution.py:334
  155.7 7.3 %collective-permute-start.11 = (bf16[4,1024]{1,0:T(4,128)(2,1)S(1)}, bf16[4,1024]{1,0:T(4,128)(2,1)S(1)}, u32[]{:S(2)}, u32[]{:S(2)}) collective-permute-start(bf16[4,1024]{1,0:T(4,128)(2,1)S(1)} %get-tuple-element.59), channel_id=1, source_target_pairs={{0,1},{1,0},{2,3},{3,2},{4,5},{5,4},{6,7},{7,6},{8,9},{9,8},{10,11... | collective-permute-start | bytes 24584 | tf_op jit(solution)/shard_map/ppermute | solution.py:348
  157.6 5.5 %collective-permute-start.12 = (bf16[4,1024]{1,0:T(4,128)(2,1)S(1)}, bf16[4,1024]{1,0:T(4,128)(2,1)S(1)}, u32[]{:S(2)}, u32[]{:S(2)}) collective-permute-start(bf16[4,1024]{1,0:T(4,128)(2,1)S(1)} %get-tuple-element.61), channel_id=1, source_target_pairs={{0,2},{1,3},{2,0},{3,1},{4,6},{5,7},{6,4},{7,5},{8,10},{9,11},{10,... | collective-permute-start | bytes 24584 | tf_op jit(solution)/shard_map/ppermute | solution.py:348
  160.3 4.9 %collective-permute-start.13 = (bf16[4,1024]{1,0:T(4,128)(2,1)S(1)}, bf16[4,1024]{1,0:T(4,128)(2,1)S(1)}, u32[]{:S(2)}, u32[]{:S(2)}) collective-permute-start(bf16[4,1024]{1,0:T(4,128)(2,1)S(1)} %get-tuple-element.60), channel_id=1, source_target_pairs={{0,3},{1,2},{2,1},{3,0},{4,7},{5,6},{6,5},{7,4},{8,11},{9,10},{10,... | collective-permute-start | bytes 24584 | tf_op jit(solution)/shard_map/ppermute | solution.py:348

commit v7 on v6

--- a/solution.py
+++ b/solution.py
@@ -379,8 +379,6 @@
     att_rows = to_heads(att)
     dq, dkv, dleft, dright = backward(frame_ins + (qg, att, stats, k_pil, v_pil))
     att_rows, dq, dkv, dleft, dright = lax.optimization_barrier((att_rows, dq, dkv, dleft, dright))
-    from_right = lax.ppermute(dleft, FRAMES, downs)
-    from_left = lax.ppermute(dright, FRAMES, ups)
 
     core, z_bit = lax.axis_index("c"), lax.axis_index("zl") & 1
     head = jnp.arange(4, dtype=jnp.int32) * 2
@@ -392,19 +390,25 @@
     got = lax.ppermute(send, "zl", [(j, j ^ 1) for j in range(4)])
     share = keep + got.astype(F32)
 
+    upper = (lax.axis_index("zl") >> 1) & 1 == 1
+    out = jnp.where(upper, share[0], share[1]).astype(BF)
+    from_right = lax.ppermute(dleft, FRAMES, downs)
+    from_left = lax.ppermute(dright, FRAMES, ups)
+    out, from_left, from_right, dq = lax.optimization_barrier((out, from_left, from_right, dq))
+    got = lax.ppermute(out, "zl", [(j, j ^ 2) for j in range(4)])
     dq = to_heads(dq)
     first = dkv[:1].astype(F32) + from_left.astype(F32)[None]
     last = dkv[SHARDS - 1 :].astype(F32) + from_right.astype(F32)[None]
     dkv = jnp.concatenate([first.astype(BF), dkv[1 : SHARDS - 1], last.astype(BF)], axis=0)
     dkv = to_heads(dkv)
     mixed = mix(att_rows, w)
-    share = halved(share, 0, "zl", 1)[0]
-    share, dq = lax.optimization_barrier((share, dq))
+    share = jnp.where(upper, share[1], share[0]) + got.astype(F32)
 
     width = share.shape[-1]
     share = scattered(share.reshape(2, 4, 16, width), 1, ("xh", "xl"))
-    share, dkv, mixed = lax.optimization_barrier((share, dkv, mixed))
+    share, dq, mixed = lax.optimization_barrier((share, dq, mixed))
     share = halved(share, 0, "zh", 0)
+    share, dkv = lax.optimization_barrier((share, dkv))
     share = scattered(share.reshape(4, 4, width), 0, ("y",))
     weight_grad = share * (1.0 / math.sqrt(8 * 32 * ROWS))
     return (

time: 168 us -> 172 us (1.024)
  waiting for transfers between devices: 38.2 us -> 46.2 us
  other arithmetic: 7.48 us -> 5 us
    all_to_all x5, waiting for transfers between devices: 12 us -> 17.6 us  [to_heads(): return lax.all_to_all(x, FRAME, 0, 0, tiled=True)]
    ppermute x6, waiting for transfers between devices: 4.38 us -> 9.38 us  [scattered(): lax.ppermute(out, axes, [(j, j ^ apart) for j in range(count)]).astype(F32)]
    ppermute x2 -> x1, waiting for transfers between devices: 6.93 us -> 3.26 us  [halved(): got = lax.ppermute(out, axis, [(j, j ^ 1 << bit) for j in range(count)])]
    ppermute x2 -> x1, starting transfers between devices: 5.8 us -> 3.43 us  [halved(): got = lax.ppermute(out, axis, [(j, j ^ 1 << bit) for j in range(count)])]
    ppermute x0 -> x1, starting transfers between devices: none -> 2.29 us  [on_device(): got = lax.ppermute(out, 'zl', [(j, j ^ 2) for j in range(4)])]
  transfers between devices with their start and end apart: 19 -> 19, of which waited for: 10 -> 9; matrix products, arithmetic and copies ran while one was open for 7% -> 5% of each run, Pallas kernels for 16% -> 15%
where the time goes in v7:
time: 172 us; the launch traced here: 171 us
  starting transfers between devices  64.5 us (38%)
  Pallas kernels  46.6 us (27%)
  waiting for transfers between devices  46.2 us (27%)
  local copies, waits for them, and re-layouts  7.91 us (5%)
  other arithmetic  5 us (3%)
    pallas_call x2, Pallas kernels, over_blocks(): pl.pallas_call(kernel, grid=(SHARDS,), in_specs=in_specs, out_specs=[whol...  24.8 us
    all_to_all x5, starting transfers between devices, to_heads(): return lax.all_to_all(x, FRAME, 0, 0, tiled=True)  22.5 us
    all_to_all x5, waiting for transfers between devices, to_heads(): return lax.all_to_all(x, FRAME, 0, 0, tiled=True)  17.6 us
    ppermute x6, starting transfers between devices, scattered(): lax.ppermute(out, axes, [(j, j ^ apart) for j in range(count)]).astype(F32)  16.5 us
    ppermute x1, starting transfers between devices, on_device(): from_left = lax.ppermute(dright, FRAMES, ups)  12.3 us
    pallas_call x3, Pallas kernels, share_of(): pl.pallas_call(share_kernel, grid_spec=pltpu.PrefetchScalarGridSpec(num_s...  10.9 us
    ppermute x6, waiting for transfers between devices, scattered(): lax.ppermute(out, axes, [(j, j ^ apart) for j in range(count)]).astype(F32)  9.38 us
    ppermute x1, waiting for transfers between devices, on_device(): left = lax.ppermute(kv[SHARDS - 1, :2 * ROWS], FRAMES, ups)  7.74 us
  transfers between devices with their start and end apart: 19, of which 9 were waited for; matrix products, arithmetic and copies ran while one was open for 5% of the time, Pallas kernels for 15%

profile of v7, /device:TPU:32, one launch (start us, length us, event | category | flops | bytes accessed | tf_op | source)
XLA Modules:
  0.0 171.1 jit_solution(6011640918120839407)
XLA Ops:
  0.6 2.2 %pack_kv.1 = bf16[8,544,128]{2,1,0:T(8,128)(2,1)} custom-call(bf16[256,1024]{1,0:T(8,128)(2,1)} %bitcast.72, bf16[256,1024]{1,0:T(8,128)(2,1)} %bitcast.73, s32[1,32]{1,0:T(1,128)} %s_ref.1), custom_call_target="tpu_custom_call" | custom-call | tf_op jit(solution)/shard_map/pack_kv/pallas_call | solution.py:48
  2.8 5.4 %all-to-all-start = ((bf16[8,544,128]{2,1,0:T(8,128)(2,1)}), bf16[8,544,128]{2,1,0:T(8,128)(2,1)S(1)}, u32[]{:S(2)}, u32[]{:S(2)}) async-start(bf16[8,544,128]{2,1,0:T(8,128)(2,1)} %pack_kv.1), calls=%async_computation | async-start | bytes 2228224 | tf_op jit(solution)/shard_map/all_to_all | solution.py:353
  8.2 4.6 %pack_qg.1 = bf16[8,512,128]{2,1,0:T(8,128)(2,1)} custom-call(bf16[256,1024]{1,0:T(8,128)(2,1)} %bitcast.75, bf16[256,1024]{1,0:T(8,128)(2,1)} %bitcast.62, bf16[1024,1024]{1,0:T(8,128)(2,1)} %w_ref.3), custom_call_target="tpu_custom_call" | custom-call | flops 536870912 | bytes 5242880 | tf_op jit(solution)/shard_map/pack_qg/pallas_call | solution.py:73
  12.8 10.9 %all-to-all-done.kv_ref = bf16[8,544,128]{2,1,0:T(8,128)(2,1)S(1)} async-done(((bf16[8,544,128]{2,1,0:T(8,128)(2,1)}), bf16[8,544,128]{2,1,0:T(8,128)(2,1)S(1)}, u32[]{:S(2)}, u32[]{:S(2)}) %all-to-all-start) | async-done | bytes 1114144 | tf_op jit(solution)/shard_map/all_to_all | solution.py:353
  23.7 3.6 %all-to-all-start.1 = ((bf16[8,512,128]{2,1,0:T(8,128)(2,1)}), bf16[8,512,128]{2,1,0:T(8,128)(2,1)S(1)}, u32[]{:S(2)}, u32[]{:S(2)}) async-start(bf16[8,512,128]{2,1,0:T(8,128)(2,1)} %pack_qg.1), calls=%async_computation.1 | async-start | bytes 2097152 | tf_op jit(solution)/shard_map/all_to_all | solution.py:353
  27.4 4.6 %collective-permute-start = (bf16[512,128]{1,0:T(8,128)(2,1)S(1)}, bf16[512,128]{1,0:T(8,128)(2,1)S(1)}, u32[]{:S(2)}, u32[]{:S(2)}) collective-permute-start(bf16[512,128]{1,0:T(8,128)(2,1)S(1)} %get-tuple-element.59), channel_id=1, source_target_pairs={{0,8},{8,16},{16,24},{1,9},{9,17},{17,25},{2,10},{10,18},{18,26},{... | collective-permute-start | bytes 393224 | tf_op jit(solution)/shard_map/ppermute | solution.py:367
  32.0 1.3 collective-permute-start.1
  33.3 0.1 fusion.11
  33.4 0.6 reshape.30.label_ref
  34.0 7.7 %collective-permute-done.left_ref = bf16[512,128]{1,0:T(8,128)(2,1)S(1)} collective-permute-done((bf16[512,128]{1,0:T(8,128)(2,1)S(1)}, bf16[512,128]{1,0:T(8,128)(2,1)S(1)}, u32[]{:S(2)}, u32[]{:S(2)}) %collective-permute-start) | collective-permute-done | bytes 131104 | tf_op jit(solution)/shard_map/ppermute | solution.py:367
  41.8 3.2 %collective-permute-done.1.right_ref = bf16[512,128]{1,0:T(8,128)(2,1)S(1)} collective-permute-done((bf16[512,128]{1,0:T(8,128)(2,1)S(1)}, bf16[512,128]{1,0:T(8,128)(2,1)S(1)}, u32[]{:S(2)}, u32[]{:S(2)}) %collective-permute-start.1) | collective-permute-done | bytes 131104 | tf_op jit(solution)/shard_map/ppermute | solution.py:368
  45.0 0.0 all-to-all-done.1.q_ref.ga_ref
  45.0 0.6 copy-done.9
  45.6 1.0 copy-done.4
  46.6 10.3 %forward.1 = (bf16[8,256,128]{2,1,0:T(8,128)(2,1)}, f32[8,2,256]{2,1,0:T(2,128)}, bf16[256,128]{1,0:T(8,128)(2,1)}, bf16[256,128]{1,0:T(8,128)(2,1)}) custom-call(bf16[8,544,128]{2,1,0:T(8,128)(2,1)} %copy-done.2, bf16[8,512,128]{2,1,0:T(8,128)(2,1)} %copy-done.4, bf16[512,128]{1,0:T(8,128)(2,1)} %copy-done.8, bf16[512,128]{1,0:T(8,128)(2,1)} %copy-done.9, ...), custom_call_target="tpu_custom_call" | custom-call | flops 1073741824 | bytes 8388608 | tf_op jit(solution)/shard_map/forward/pallas_call | solution.py:224
  56.9 4.9 %all-to-all-start.2 = ((bf16[8,256,128]{2,1,0:T(8,128)(2,1)}), bf16[8,256,128]{2,1,0:T(8,128)(2,1)S(1)}, u32[]{:S(2)}, u32[]{:S(2)}) async-start(bf16[8,256,128]{2,1,0:T(8,128)(2,1)} %get-tuple-element.31.att_ref), calls=%async_computation.2 | async-start | bytes 1048576 | tf_op jit(solution)/shard_map/all_to_all | solution.py:353
  61.8 0.5 multiply_add_fusion.heads_ref
  62.3 14.5 %backward.1 = (bf16[8,256,128]{2,1,0:T(8,128)(2,1)}, bf16[8,512,128]{2,1,0:T(8,128)(2,1)}, bf16[512,128]{1,0:T(8,128)(2,1)}, bf16[512,128]{1,0:T(8,128)(2,1)}) custom-call(bf16[8,544,128]{2,1,0:T(8,128)(2,1)} %copy-done.2, bf16[8,512,128]{2,1,0:T(8,128)(2,1)} %copy-done.4, bf16[512,128]{1,0:T(8,128)(2,1)} %copy-done.8, bf16[512,128]{1,0:T(8,128)(2,1)} %copy-done.9, ...), custom_call_target="tpu_custom_call" | custom-call | flops 2684354560 | bytes 8388608 | tf_op jit(solution)/shard_map/backward/pallas_call | solution.py:224
  76.8 0.8 copy-done
  77.6 4.5 %share.3 = bf16[4,128,1024]{2,1,0:T(8,128)(2,1)} custom-call(s32[4]{0:T(128)} %multiply_add_fusion.heads_ref, bf16[8,256,128]{2,1,0:T(8,128)(2,1)} %copy-done, bf16[256,1024]{1,0:T(8,128)(2,1)} %bitcast.63), custom_call_target="tpu_custom_call" | custom-call | flops 268435456 | bytes 2097152 | tf_op jit(solution)/shard_map/share/pallas_call | solution.py:311
  82.2 0.5 fusion.15.heads_ref
  82.7 2.3 %collective-permute-done.2.refs_0_ = bf16[4,128,1024]{2,1,0:T(8,128)(2,1)S(1)} collective-permute-done((bf16[4,128,1024]{2,1,0:T(8,128)(2,1)}, bf16[4,128,1024]{2,1,0:T(8,128)(2,1)S(1)}, u32[]{:S(2)}, u32[]{:S(2)}) %collective-permute-start.2) | collective-permute-done | bytes 1048608 | tf_op jit(solution)/shard_map/ppermute | solution.py:386
  85.0 1.0 copy-done.1
  86.0 3.1 %share.5 = bf16[2,128,1024]{2,1,0:T(8,128)(2,1)} custom-call(s32[2]{0:T(128)} %fusion.15.heads_ref, bf16[8,256,128]{2,1,0:T(8,128)(2,1)} %copy-done, bf16[256,1024]{1,0:T(8,128)(2,1)} %bitcast.64, bf16[4,128,1024]{2,1,0:T(8,128)(2,1)} %copy-done.1), custom_call_target="tpu_custom_call" | custom-call | flops 134217728 | bytes 2097152 | tf_op jit(solution)/shard_map/share/pallas_call | solution.py:311
  89.1 0.3 collective-permute-start.3
  89.4 0.5 fusion.16.heads_ref
  89.9 12.3 %collective-permute-start.4 = (bf16[512,128]{1,0:T(8,128)(2,1)S(1)}, bf16[512,128]{1,0:T(8,128)(2,1)S(1)}, u32[]{:S(2)}, u32[]{:S(2)}) collective-permute-start(bf16[512,128]{1,0:T(8,128)(2,1)S(1)} %copy-done.7), channel_id=1, source_target_pairs={{0,8},{8,16},{16,24},{1,9},{9,17},{17,25},{2,10},{10,18},{18,26},{... | collective-permute-start | bytes 393224 | tf_op jit(solution)/shard_map/ppermute | solution.py:396
  102.2 1.3 collective-permute-start.5
  103.5 3.2 %share.4 = f32[2,128,1024]{2,1,0:T(8,128)} custom-call(s32[2]{0:T(128)} %fusion.16.heads_ref, bf16[8,256,128]{2,1,0:T(8,128)(2,1)} %copy-done, bf16[256,1024]{1,0:T(8,128)(2,1)} %bitcast.65, bf16[4,128,1024]{2,1,0:T(8,128)(2,1)} %copy-done.1), custom_call_target="tpu_custom_call" | custom-call | flops 134217728 | bytes 2097152 | tf_op jit(solution)/shard_map/share/pallas_call | solution.py:311
  106.7 0.0 collective-permute-done.3
  106.8 1.4 convert_add_fusion
  108.1 0.1 fusion
  108.2 0.0 collective-permute-done.4
  108.2 2.7 %collective-permute-done.5 = bf16[512,128]{1,0:T(8,128)(2,1)S(1)} collective-permute-done((bf16[512,128]{1,0:T(8,128)(2,1)S(1)}, bf16[512,128]{1,0:T(8,128)(2,1)S(1)}, u32[]{:S(2)}, u32[]{:S(2)}) %collective-permute-start.5) | collective-permute-done | bytes 131104 | tf_op jit(solution)/shard_map/ppermute | solution.py:395
  110.9 5.1 %all-to-all-start.3 = ((bf16[8,256,128]{2,1,0:T(8,128)(2,1)}), bf16[8,256,128]{2,1,0:T(8,128)(2,1)S(1)}, u32[]{:S(2)}, u32[]{:S(2)}) async-start(bf16[8,256,128]{2,1,0:T(8,128)(2,1)} %get-tuple-element.44), calls=%async_computation.3 | async-start | bytes 1048576 | tf_op jit(solution)/shard_map/all_to_all | solution.py:353
  116.0 0.1 slice.42
  116.0 2.3 %collective-permute-start.6 = (bf16[128,1024]{1,0:T(8,128)(2,1)S(1)}, bf16[128,1024]{1,0:T(8,128)(2,1)S(1)}, u32[]{:S(2)}, u32[]{:S(2)}) collective-permute-start(bf16[128,1024]{1,0:T(8,128)(2,1)S(1)} %fusion), channel_id=1, source_target_pairs={{0,128},{64,192},{128,0},{192,64},{1,129},{65,193},{129,1},{193,65... | collective-permute-start | bytes 786440 | tf_op jit(solution)/shard_map/ppermute | solution.py:398
  118.3 0.1 fusion.2
  118.4 1.1 pad_maximum_fusion
  119.5 6.7 %all-to-all-done.3 = bf16[8,256,128]{2,1,0:T(8,128)(2,1)S(1)} async-done(((bf16[8,256,128]{2,1,0:T(8,128)(2,1)}), bf16[8,256,128]{2,1,0:T(8,128)(2,1)S(1)}, u32[]{:S(2)}, u32[]{:S(2)}) %all-to-all-start.3) | async-done | bytes 524320 | tf_op jit(solution)/shard_map/all_to_all | solution.py:353
  126.2 3.6 %all-to-all-start.4 = ((bf16[8,512,128]{2,1,0:T(8,128)(2,1)}), bf16[8,512,128]{2,1,0:T(8,128)(2,1)S(1)}, u32[]{:S(2)}, u32[]{:S(2)}) async-start(bf16[8,512,128]{2,1,0:T(8,128)(2,1)} %pad_maximum_fusion), calls=%async_computation.4 | async-start | bytes 2097152 | tf_op jit(solution)/shard_map/all_to_all | solution.py:353
  129.7 0.1 bitcast_add_fusion
  129.9 2.0 %collective-permute-start.7 = (bf16[2,16,1024]{2,1,0:T(8,128)(2,1)S(1)}, bf16[2,16,1024]{2,1,0:T(8,128)(2,1)S(1)}, u32[]{:S(2)}, u32[]{:S(2)}) collective-permute-start(bf16[2,16,1024]{2,1,0:T(8,128)(2,1)S(1)} %get-tuple-element.64), channel_id=1, source_target_pairs={{0,4},{4,0},{8,12},{12,8},{1,5},{5,1},{9,13},{13,9},{2,6},{6,2},{1... | collective-permute-start | bytes 196616 | tf_op jit(solution)/shard_map/ppermute | solution.py:348
  131.9 9.7 %collective-permute-start.8 = (bf16[2,16,1024]{2,1,0:T(8,128)(2,1)S(1)}, bf16[2,16,1024]{2,1,0:T(8,128)(2,1)S(1)}, u32[]{:S(2)}, u32[]{:S(2)}) collective-permute-start(bf16[2,16,1024]{2,1,0:T(8,128)(2,1)S(1)} %get-tuple-element.66), channel_id=1, source_target_pairs={{0,8},{4,12},{8,0},{12,4},{1,9},{5,13},{9,1},{13,5},{2,10},{6,14},... | collective-permute-start | bytes 196616 | tf_op jit(solution)/shard_map/ppermute | solution.py:348
  141.6 0.0 collective-permute-start.9
  141.6 4.2 %mix.1 = bf16[256,1024]{1,0:T(8,128)(2,1)} custom-call(bf16[8,256,128]{2,1,0:T(8,128)(2,1)} %copy-done, bf16[1024,1024]{1,0:T(8,128)(2,1)} %w_ref.3), custom_call_target="tpu_custom_call" | custom-call | flops 536870912 | bytes 3145728 | tf_op jit(solution)/shard_map/mix/pallas_call | solution.py:280
  145.8 0.0 collective-permute-done.7
  145.8 7.3 %collective-permute-done.8 = bf16[2,16,1024]{2,1,0:T(8,128)(2,1)S(1)} collective-permute-done((bf16[2,16,1024]{2,1,0:T(8,128)(2,1)S(1)}, bf16[2,16,1024]{2,1,0:T(8,128)(2,1)S(1)}, u32[]{:S(2)}, u32[]{:S(2)}) %collective-permute-start.8) | collective-permute-done | bytes 65568 | tf_op jit(solution)/shard_map/ppermute | solution.py:348
  153.1 0.0 collective-permute-done.9
  153.1 3.4 %collective-permute-start.10 = (bf16[1,16,1024]{2,1,0:T(8,128)(2,1)S(1)}, bf16[1,16,1024]{2,1,0:T(8,128)(2,1)S(1)}, u32[]{:S(2)}, u32[]{:S(2)}) collective-permute-start(bf16[1,16,1024]{2,1,0:T(8,128)(2,1)S(1)} %select_convert_fusion.1), channel_id=1, source_target_pairs={{0,16},{16,0},{1,17},{17,1},{2,18},{18,2},{3,19},{19,3},{4,20},{20... | collective-permute-start | bytes 98312 | tf_op jit(solution)/shard_map/ppermute | solution.py:334
  156.6 0.2 copy.16
  156.8 1.0 copy.19
  157.8 3.3 %collective-permute-done.10 = bf16[1,16,1024]{2,1,0:T(8,128)(2,1)S(1)} collective-permute-done((bf16[1,16,1024]{2,1,0:T(8,128)(2,1)S(1)}, bf16[1,16,1024]{2,1,0:T(8,128)(2,1)S(1)}, u32[]{:S(2)}, u32[]{:S(2)}) %collective-permute-start.10) | collective-permute-done | bytes 32800 | tf_op jit(solution)/shard_map/ppermute | solution.py:334
  161.1 1.9 %collective-permute-start.11 = (bf16[4,1024]{1,0:T(4,128)(2,1)S(1)}, bf16[4,1024]{1,0:T(4,128)(2,1)S(1)}, u32[]{:S(2)}, u32[]{:S(2)}) collective-permute-start(bf16[4,1024]{1,0:T(4,128)(2,1)S(1)} %get-tuple-element.67), channel_id=1, source_target_pairs={{0,1},{1,0},{2,3},{3,2},{4,5},{5,4},{6,7},{7,6},{8,9},{9,8},{10,11... | collective-permute-start | bytes 24584 | tf_op jit(solution)/shard_map/ppermute | solution.py:348
  163.0 2.7 %collective-permute-start.12 = (bf16[4,1024]{1,0:T(4,128)(2,1)S(1)}, bf16[4,1024]{1,0:T(4,128)(2,1)S(1)}, u32[]{:S(2)}, u32[]{:S(2)}) collective-permute-start(bf16[4,1024]{1,0:T(4,128)(2,1)S(1)} %get-tuple-element.69), channel_id=1, source_target_pairs={{0,2},{1,3},{2,0},{3,1},{4,6},{5,7},{6,4},{7,5},{8,10},{9,11},{10,... | collective-permute-start | bytes 24584 | tf_op jit(solution)/shard_map/ppermute | solution.py:348
  165.7 0.2 collective-permute-start.13
  165.9 0.1 slice_bitcast_fusion
  166.0 0.2 copy.17
  166.2 1.0 copy.20
  167.2 0.2 copy.18
  167.4 1.0 copy.21
  168.4 0.0 collective-permute-done.11
  168.5 2.1 %collective-permute-done.13 = bf16[4,1024]{1,0:T(4,128)(2,1)S(1)} collective-permute-done((bf16[4,1024]{1,0:T(4,128)(2,1)S(1)}, bf16[4,1024]{1,0:T(4,128)(2,1)S(1)}, u32[]{:S(2)}, u32[]{:S(2)}) %collective-permute-start.13) | collective-permute-done | bytes 8224 | tf_op jit(solution)/shard_map/ppermute | solution.py:348
  170.5 0.6 fusion.10
  (28 shorter events, 0.2 us)
Async XLA Ops:
  2.8 20.9 %all-to-all-start = ((bf16[8,544,128]{2,1,0:T(8,128)(2,1)}), bf16[8,544,128]{2,1,0:T(8,128)(2,1)S(1)}, u32[]{:S(2)}, u32[]{:S(2)}) async-start(bf16[8,544,128]{2,1,0:T(8,128)(2,1)} %pack_kv.1), calls=%async_computation | async-start | bytes 2228224 | tf_op jit(solution)/shard_map/all_to_all | solution.py:353
  12.8 20.6 %copy-start.5 = (s32[8192]{0:T(1024)S(1)}, s32[8192]{0:T(1024)}, u32[]{:S(2)}) copy-start(s32[8192]{0:T(1024)} %param.13) | copy-start | bytes 98308
  23.7 3.7 %copy-start.2 = (bf16[8,544,128]{2,1,0:T(8,128)(2,1)}, bf16[8,544,128]{2,1,0:T(8,128)(2,1)S(1)}, u32[]{:S(2)}) copy-start(bf16[8,544,128]{2,1,0:T(8,128)(2,1)S(1)} %all-to-all-done.kv_ref) | copy-start | bytes 3342340
  23.7 21.3 %all-to-all-start.1 = ((bf16[8,512,128]{2,1,0:T(8,128)(2,1)}), bf16[8,512,128]{2,1,0:T(8,128)(2,1)S(1)}, u32[]{:S(2)}, u32[]{:S(2)}) async-start(bf16[8,512,128]{2,1,0:T(8,128)(2,1)} %pack_qg.1), calls=%async_computation.1 | async-start | bytes 2097152 | tf_op jit(solution)/shard_map/all_to_all | solution.py:353
  27.4 14.4 %collective-permute-start = (bf16[512,128]{1,0:T(8,128)(2,1)S(1)}, bf16[512,128]{1,0:T(8,128)(2,1)S(1)}, u32[]{:S(2)}, u32[]{:S(2)}) collective-permute-start(bf16[512,128]{1,0:T(8,128)(2,1)S(1)} %get-tuple-element.59), channel_id=1, source_target_pairs={{0,8},{8,16},{16,24},{1,9},{9,17},{17,25},{2,10},{10,18},{18,26},{... | collective-permute-start | bytes 393224 | tf_op jit(solution)/shard_map/ppermute | solution.py:367
  32.0 12.9 %collective-permute-start.1 = (bf16[512,128]{1,0:T(8,128)(2,1)S(1)}, bf16[512,128]{1,0:T(8,128)(2,1)S(1)}, u32[]{:S(2)}, u32[]{:S(2)}) collective-permute-start(bf16[512,128]{1,0:T(8,128)(2,1)S(1)} %get-tuple-element.58), channel_id=1, source_target_pairs={{8,0},{16,8},{24,16},{9,1},{17,9},{25,17},{10,2},{18,10},{26,18},{... | collective-permute-start | bytes 393224 | tf_op jit(solution)/shard_map/ppermute | solution.py:368
  41.8 3.2 %copy-start.8 = (bf16[512,128]{1,0:T(8,128)(2,1)}, bf16[512,128]{1,0:T(8,128)(2,1)S(1)}, u32[]{:S(2)}) copy-start(bf16[512,128]{1,0:T(8,128)(2,1)S(1)} %collective-permute-done.left_ref) | copy-start | bytes 393220
  45.0 0.7 copy-start.9
  45.6 1.0 copy-start.4
  56.9 19.9 %all-to-all-start.2 = ((bf16[8,256,128]{2,1,0:T(8,128)(2,1)}), bf16[8,256,128]{2,1,0:T(8,128)(2,1)S(1)}, u32[]{:S(2)}, u32[]{:S(2)}) async-start(bf16[8,256,128]{2,1,0:T(8,128)(2,1)} %get-tuple-element.31.att_ref), calls=%async_computation.2 | async-start | bytes 1048576 | tf_op jit(solution)/shard_map/all_to_all | solution.py:353
  76.8 0.8 copy-start
  82.2 2.9 %collective-permute-start.2 = (bf16[4,128,1024]{2,1,0:T(8,128)(2,1)}, bf16[4,128,1024]{2,1,0:T(8,128)(2,1)S(1)}, u32[]{:S(2)}, u32[]{:S(2)}) collective-permute-start(bf16[4,128,1024]{2,1,0:T(8,128)(2,1)} %share.3), channel_id=1, source_target_pairs={{0,32},{32,0},{1,33},{33,1},{2,34},{34,2},{3,35},{35,3},{4,36},{36... | collective-permute-start | bytes 3145736 | tf_op jit(solution)/shard_map/ppermute | solution.py:386
  82.7 7.3 %copy-start.7 = (bf16[512,128]{1,0:T(8,128)(2,1)S(1)}, bf16[512,128]{1,0:T(8,128)(2,1)}, u32[]{:S(2)}) copy-start(bf16[512,128]{1,0:T(8,128)(2,1)} %get-tuple-element.40) | copy-start | bytes 393220
  82.7 19.5 %copy-start.6 = (bf16[512,128]{1,0:T(8,128)(2,1)S(1)}, bf16[512,128]{1,0:T(8,128)(2,1)}, u32[]{:S(2)}) copy-start(bf16[512,128]{1,0:T(8,128)(2,1)} %get-tuple-element.41) | copy-start | bytes 393220
  85.0 1.0 copy-start.1
  89.1 17.6 %collective-permute-start.3 = (bf16[2,128,1024]{2,1,0:T(8,128)(2,1)}, bf16[2,128,1024]{2,1,0:T(8,128)(2,1)S(1)}, u32[]{:S(2)}, u32[]{:S(2)}) collective-permute-start(bf16[2,128,1024]{2,1,0:T(8,128)(2,1)} %share.5), channel_id=1, source_target_pairs={{0,64},{64,0},{128,192},{192,128},{1,65},{65,1},{129,193},{193,129... | collective-permute-start | bytes 1572872 | tf_op jit(solution)/shard_map/ppermute | solution.py:390
  89.9 18.3 %collective-permute-start.4 = (bf16[512,128]{1,0:T(8,128)(2,1)S(1)}, bf16[512,128]{1,0:T(8,128)(2,1)S(1)}, u32[]{:S(2)}, u32[]{:S(2)}) collective-permute-start(bf16[512,128]{1,0:T(8,128)(2,1)S(1)} %copy-done.7), channel_id=1, source_target_pairs={{0,8},{8,16},{16,24},{1,9},{9,17},{17,25},{2,10},{10,18},{18,26},{... | collective-permute-start | bytes 393224 | tf_op jit(solution)/shard_map/ppermute | solution.py:396
  102.2 8.7 %collective-permute-start.5 = (bf16[512,128]{1,0:T(8,128)(2,1)S(1)}, bf16[512,128]{1,0:T(8,128)(2,1)S(1)}, u32[]{:S(2)}, u32[]{:S(2)}) collective-permute-start(bf16[512,128]{1,0:T(8,128)(2,1)S(1)} %copy-done.6), channel_id=1, source_target_pairs={{8,0},{16,8},{24,16},{9,1},{17,9},{25,17},{10,2},{18,10},{26,18},{... | collective-permute-start | bytes 393224 | tf_op jit(solution)/shard_map/ppermute | solution.py:395
  108.1 7.8 %copy-start.3 = (bf16[8,512,128]{2,1,0:T(8,128)(2,1)S(1)}, bf16[8,512,128]{2,1,0:T(8,128)(2,1)}, u32[]{:S(2)}) copy-start(bf16[8,512,128]{2,1,0:T(8,128)(2,1)} %get-tuple-element.48) | copy-start | bytes 3145732
  110.9 15.3 %all-to-all-start.3 = ((bf16[8,256,128]{2,1,0:T(8,128)(2,1)}), bf16[8,256,128]{2,1,0:T(8,128)(2,1)S(1)}, u32[]{:S(2)}, u32[]{:S(2)}) async-start(bf16[8,256,128]{2,1,0:T(8,128)(2,1)} %get-tuple-element.44), calls=%async_computation.3 | async-start | bytes 1048576 | tf_op jit(solution)/shard_map/all_to_all | solution.py:353
  116.0 13.7 %collective-permute-start.6 = (bf16[128,1024]{1,0:T(8,128)(2,1)S(1)}, bf16[128,1024]{1,0:T(8,128)(2,1)S(1)}, u32[]{:S(2)}, u32[]{:S(2)}) collective-permute-start(bf16[128,1024]{1,0:T(8,128)(2,1)S(1)} %fusion), channel_id=1, source_target_pairs={{0,128},{64,192},{128,0},{192,64},{1,129},{65,193},{129,1},{193,65... | collective-permute-start | bytes 786440 | tf_op jit(solution)/shard_map/ppermute | solution.py:398
  126.2 34.9 %all-to-all-start.4 = ((bf16[8,512,128]{2,1,0:T(8,128)(2,1)}), bf16[8,512,128]{2,1,0:T(8,128)(2,1)S(1)}, u32[]{:S(2)}, u32[]{:S(2)}) async-start(bf16[8,512,128]{2,1,0:T(8,128)(2,1)} %pad_maximum_fusion), calls=%async_computation.4 | async-start | bytes 2097152 | tf_op jit(solution)/shard_map/all_to_all | solution.py:353
  129.9 15.9 %collective-permute-start.7 = (bf16[2,16,1024]{2,1,0:T(8,128)(2,1)S(1)}, bf16[2,16,1024]{2,1,0:T(8,128)(2,1)S(1)}, u32[]{:S(2)}, u32[]{:S(2)}) collective-permute-start(bf16[2,16,1024]{2,1,0:T(8,128)(2,1)S(1)} %get-tuple-element.64), channel_id=1, source_target_pairs={{0,4},{4,0},{8,12},{12,8},{1,5},{5,1},{9,13},{13,9},{2,6},{6,2},{1... | collective-permute-start | bytes 196616 | tf_op jit(solution)/shard_map/ppermute | solution.py:348
  131.9 21.2 %collective-permute-start.8 = (bf16[2,16,1024]{2,1,0:T(8,128)(2,1)S(1)}, bf16[2,16,1024]{2,1,0:T(8,128)(2,1)S(1)}, u32[]{:S(2)}, u32[]{:S(2)}) collective-permute-start(bf16[2,16,1024]{2,1,0:T(8,128)(2,1)S(1)} %get-tuple-element.66), channel_id=1, source_target_pairs={{0,8},{4,12},{8,0},{12,4},{1,9},{5,13},{9,1},{13,5},{2,10},{6,14},... | collective-permute-start | bytes 196616 | tf_op jit(solution)/shard_map/ppermute | solution.py:348
  141.6 11.5 %collective-permute-start.9 = (bf16[2,16,1024]{2,1,0:T(8,128)(2,1)S(1)}, bf16[2,16,1024]{2,1,0:T(8,128)(2,1)S(1)}, u32[]{:S(2)}, u32[]{:S(2)}) collective-permute-start(bf16[2,16,1024]{2,1,0:T(8,128)(2,1)S(1)} %get-tuple-element.65), channel_id=1, source_target_pairs={{0,12},{4,8},{8,4},{12,0},{1,13},{5,9},{9,5},{13,1},{2,14},{6,10},... | collective-permute-start | bytes 196616 | tf_op jit(solution)/shard_map/ppermute | solution.py:348
  153.1 7.9 %collective-permute-start.10 = (bf16[1,16,1024]{2,1,0:T(8,128)(2,1)S(1)}, bf16[1,16,1024]{2,1,0:T(8,128)(2,1)S(1)}, u32[]{:S(2)}, u32[]{:S(2)}) collective-permute-start(bf16[1,16,1024]{2,1,0:T(8,128)(2,1)S(1)} %select_convert_fusion.1), channel_id=1, source_target_pairs={{0,16},{16,0},{1,17},{17,1},{2,18},{18,2},{3,19},{19,3},{4,20},{20... | collective-permute-start | bytes 98312 | tf_op jit(solution)/shard_map/ppermute | solution.py:334
  161.1 7.3 %collective-permute-start.11 = (bf16[4,1024]{1,0:T(4,128)(2,1)S(1)}, bf16[4,1024]{1,0:T(4,128)(2,1)S(1)}, u32[]{:S(2)}, u32[]{:S(2)}) collective-permute-start(bf16[4,1024]{1,0:T(4,128)(2,1)S(1)} %get-tuple-element.67), channel_id=1, source_target_pairs={{0,1},{1,0},{2,3},{3,2},{4,5},{5,4},{6,7},{7,6},{8,9},{9,8},{10,11... | collective-permute-start | bytes 24584 | tf_op jit(solution)/shard_map/ppermute | solution.py:348
  163.0 5.5 %collective-permute-start.12 = (bf16[4,1024]{1,0:T(4,128)(2,1)S(1)}, bf16[4,1024]{1,0:T(4,128)(2,1)S(1)}, u32[]{:S(2)}, u32[]{:S(2)}) collective-permute-start(bf16[4,1024]{1,0:T(4,128)(2,1)S(1)} %get-tuple-element.69), channel_id=1, source_target_pairs={{0,2},{1,3},{2,0},{3,1},{4,6},{5,7},{6,4},{7,5},{8,10},{9,11},{10,... | collective-permute-start | bytes 24584 | tf_op jit(solution)/shard_map/ppermute | solution.py:348
  165.7 4.9 %collective-permute-start.13 = (bf16[4,1024]{1,0:T(4,128)(2,1)S(1)}, bf16[4,1024]{1,0:T(4,128)(2,1)S(1)}, u32[]{:S(2)}, u32[]{:S(2)}) collective-permute-start(bf16[4,1024]{1,0:T(4,128)(2,1)S(1)} %get-tuple-element.68), channel_id=1, source_target_pairs={{0,3},{1,2},{2,1},{3,0},{4,7},{5,6},{6,5},{7,4},{8,11},{9,10},{10,... | collective-permute-start | bytes 24584 | tf_op jit(solution)/shard_map/ppermute | solution.py:348
